TPU v7x, 32 devices: a whole 2x2x4 slice. The times are simulated.
32 devices in a mesh: fsdp: 4 (over y, core), ctx: 8 (over z, x).
Axes of the slice: x: 2, y: 2, z: 4, core: 2. Of those that a mesh axis runs over, the one named last changes fastest.
Arguments:
- inputs: bfloat16 [4, 4096, 1536], P('fsdp', 'ctx'), may hold values from -8 to 8
- segment_ids: int32 [4, 4096], P('fsdp', 'ctx'), may hold values from 0 to 3, never falling along the last dimension, each value on 1 to 2048 neighbouring positions
- out_grad: bfloat16 [4, 4096, 1536], P('fsdp', 'ctx'), may hold values from -6 to 6
- in_matrix: bfloat16 [1536, 6448], P('fsdp'), may hold values from -0.15625 to 0.15625
- out_matrix: bfloat16 [3072, 1536], P('fsdp'), may hold values from -0.109375 to 0.109375
- conv_taps: bfloat16 [3328, 4], P('fsdp'), may hold values from -3 to 3
- conv_bias: bfloat16 [3328], P('fsdp'), may hold values from -2.5 to 2.5
- dt_bias: bfloat16 [48], P('fsdp'), may hold values from -6 to -2
- decay_log: bfloat16 [48], P('fsdp'), may hold values from -7 to 2.5
- skip_scale: bfloat16 [48], P('fsdp'), may hold values from 0.5 to 2
- mixer_gain: bfloat16 [3072], P('fsdp'), may hold values from 0.5 to 1.5
- input_gain: bfloat16 [1536], P('fsdp'), may hold values from 0.5 to 1.5
Outputs:
- block_out: bfloat16 [4, 4096, 1536], P('fsdp', 'ctx')
- input_grad: bfloat16 [4, 4096, 1536], P('fsdp', 'ctx')
- in_matrix_grad: float32 [1536, 6448], P('fsdp')
- out_matrix_grad: float32 [3072, 1536], P('fsdp')
- conv_taps_grad: float32 [3328, 4], P('fsdp')
- conv_bias_grad: float32 [3328], P('fsdp')
- dt_bias_grad: float32 [48], P('fsdp')
- decay_log_grad: float32 [48], P('fsdp')
- skip_scale_grad: float32 [48], P('fsdp')
- mixer_gain_grad: float32 [3072], P('fsdp')
- input_gain_grad: float32 [1536], P('fsdp')
- rms_stats: float32 [2], replicated
Inputs may be any that keep to these rules, and one draw needn't show every extreme that they name: `segment_ids`: along each sequence the numbers never fall; a run of equal numbers is one document; every number of 0 to 3 is used, and the longest document has exactly 2048 tokens.
All inputs are finite; a program needn't handle non-finite values.
Results may differ from a plain program's by a relative error of at most 0.015.
Values may be sent and summed in bfloat16 or wider, within the bound.
A program may use at most 320 MiB of HBM per device.

v0:
```python
import jax
import jax.numpy as jnp
from jax import lax
from jax.sharding import PartitionSpec as P

D = 1536
HEADS = 48
HDIM = 64
STATE = 128
CONV = 4
GROUP = 256
INNER = 3072
XBC = 3328


epsilon = 1e-05
precise = lax.Precision.HIGHEST


def passed_along(block, axis, distance):
    devices = range(lax.axis_size(axis))
    route = [(i - distance, i) for i in devices if i - distance in devices]
    return lax.ppermute(block, axis, route)


def prefix(x, axis, join, neutral):
    place = lax.axis_index(axis)
    gathered = jax.tree.map(
        lambda a, kind: lax.all_gather(a.astype(kind), axis), x, (jnp.bfloat16, jnp.bfloat16)
    )
    state = jax.tree.map(lambda a, e: jnp.zeros_like(a) + jnp.asarray(e, a.dtype), x, neutral)

    def one(lap, state):
        return join(
            state,
            jax.tree.map(
                lambda a, own: lax.dynamic_index_in_dim(a, lap, 0, False).astype(own.dtype),
                gathered,
                x,
            ),
        )

    return lax.fori_loop(0, place, one, state)


def prefix_2(x, axis, combine, identity):
    count, mine = (lax.axis_size(axis), lax.axis_index(axis))
    everything = jax.tree.map(
        lambda part, kind: lax.all_gather(part.astype(kind), axis),
        x,
        jax.tree.map(lambda a: jnp.bfloat16 if a.dtype == jnp.float32 else a.dtype, x),
    )
    start = jax.tree.map(
        lambda part, zero: jnp.broadcast_to(jnp.asarray(zero, part.dtype), part.shape), x, identity
    )

    def lap(k, before):
        at = count - 1 - k
        reached = at > mine
        new = combine(
            before, jax.tree.map(lambda part, own: part[at].astype(own.dtype), everything, x)
        )
        return jax.tree.map(lambda a, b: jnp.where(reached, a, b), new, before)

    return lax.fori_loop(0, count, lap, start)


def combine(earlier, later_pair):
    return (earlier[0] * later_pair[0], later_pair[0][:, None, None] * earlier[1] + later_pair[1])


def block_step(carry_pair, sliced):
    carried, seg_before, offset = carry_pair
    xblock, bblock, cblock, dblock, lblock, sblock = sliced
    block_len = sblock.shape[0]
    running = jnp.cumsum(lblock, axis=0)
    rowpos = lax.broadcasted_iota(jnp.int32, (block_len, block_len), 0)
    colpos = lax.broadcasted_iota(jnp.int32, (block_len, block_len), 1)
    allowed = (sblock[:, None] == sblock[None, :]) & (colpos <= rowpos)
    log_gap = running.T[:, :, None] - running.T[:, None, :]
    decays = jnp.exp(jnp.where(allowed[None], log_gap, -1e30))
    scores = jnp.dot(cblock, bblock.T, precision=precise)
    mixing = decays * scores[None] * dblock.T[:, None, :]
    y_diag = jnp.einsum("hts,shp->thp", mixing, xblock, precision=precise)
    carry_in = (sblock == seg_before).astype(jnp.float32)
    y_off = (jnp.exp(running) * carry_in[:, None])[:, :, None] * jnp.einsum(
        "tn,hpn->thp", cblock, carried, precision=precise
    )
    final_log = running[block_len - 1]
    tail_weight = (
        jnp.exp(final_log[None, :] - running)
        * (sblock == sblock[block_len - 1]).astype(jnp.float32)[:, None]
        * dblock
    )
    retain = jnp.exp(final_log) * (sblock[block_len - 1] == seg_before).astype(jnp.float32)
    carried = retain[:, None, None] * carried + jnp.einsum(
        "sh,shp,sn->hpn", tail_weight, xblock, bblock, precision=precise
    )
    return (
        (carried, sblock[block_len - 1], offset + final_log),
        (y_diag + y_off, running + offset[None, :]),
    )


def scan_ssd(values, b_rows, c_rows, dt_rows, log_decay, seg_ids, seg_start):
    length = seg_ids.shape[0]
    blocks = length // GROUP
    sliced = (
        values.reshape(blocks, GROUP, HEADS, HDIM),
        b_rows.reshape(blocks, GROUP, STATE),
        c_rows.reshape(blocks, GROUP, STATE),
        dt_rows.reshape(blocks, GROUP, HEADS),
        log_decay.reshape(blocks, GROUP, HEADS),
        seg_ids.reshape(blocks, GROUP),
    )
    initial = (
        jnp.zeros((HEADS, HDIM, STATE), jnp.float32),
        seg_start,
        jnp.zeros((HEADS,), jnp.float32),
    )
    finish, (outputs, running) = lax.scan(jax.checkpoint(block_step), initial, sliced)
    return (outputs.reshape(length, HEADS, HDIM), running.reshape(length, HEADS), finish[0])


def mixer_front(
    ext_rows, dt_raw, conv_taps, conv_bias, dt_bias, decay_log, seg_ext, seg_ids, seg_start
):
    length = seg_ids.shape[0]
    summed = jnp.broadcast_to(conv_bias, (length, conv_bias.shape[0]))
    for tap_index in range(CONV):
        same_doc = (seg_ext[tap_index : tap_index + length] == seg_ids).astype(jnp.float32)
        summed = (
            summed
            + conv_taps[:, tap_index] * ext_rows[tap_index : tap_index + length] * same_doc[:, None]
        )
    active = jax.nn.silu(summed)
    values = active[:, :INNER].reshape(length, HEADS, HDIM)
    b_rows = active[:, INNER : INNER + STATE]
    c_rows = active[:, INNER + STATE :]
    dt_rows = jax.nn.softplus(dt_raw + dt_bias)
    log_decay = -dt_rows * jnp.exp(decay_log)
    y_local, running, carried = scan_ssd(
        values, b_rows, c_rows, dt_rows, log_decay, seg_ids, seg_start
    )
    retain = jnp.exp(running[length - 1]) * (seg_ids[length - 1] == seg_start).astype(jnp.float32)
    return (values, c_rows, running, y_local, carried, retain)


def mixer_tail(
    values, c_rows, running, y_local, carried_in, gate_part, skip_scale, mixer_gain, carry_flag
):
    length = gate_part.shape[0]
    incoming = jnp.einsum("tn,hpn->thp", c_rows, carried_in, precision=precise)
    weights = jnp.exp(running) * carry_flag[:, None]
    mixed_ssd = y_local + weights[:, :, None] * incoming + skip_scale[None, :, None] * values
    gated = mixed_ssd.reshape(length, INNER) * jax.nn.silu(gate_part)
    return gated * lax.rsqrt(jnp.mean(gated * gated, axis=-1, keepdims=True) + epsilon) * mixer_gain


def on_device(
    inputs,
    segment_ids,
    out_grad,
    in_matrix,
    out_matrix,
    conv_taps,
    conv_bias,
    dt_bias,
    decay_log,
    skip_scale,
    mixer_gain,
    input_gain,
):
    units = inputs[0].astype(jnp.float32)
    seg_ids = segment_ids[0]
    length = units.shape[0]
    inv_rms = lax.rsqrt(jnp.mean(units * units, axis=-1, keepdims=True) + epsilon)
    base_rows = units * inv_rms
    w_piece = lax.all_gather(in_matrix, "fsdp", axis=0, tiled=True)
    g_piece = lax.all_gather(input_gain, "fsdp", axis=0, tiled=True)
    g_float = g_piece.astype(jnp.float32)
    part_rows = (base_rows * g_float).astype(jnp.bfloat16)
    product = jnp.dot(part_rows, w_piece, preferred_element_type=jnp.float32)
    projected = product
    projected = projected.astype(jnp.bfloat16)
    gate_part = projected[:, :INNER].astype(jnp.float32)
    conv_input = projected[:, INNER : INNER + XBC]
    dt_raw = projected[:, INNER + XBC :].astype(jnp.float32)
    out_whole, taps_whole, bias_whole, dtb_whole, decay_whole, skip_whole, norm_whole = (
        lax.all_gather(out_matrix, "fsdp", axis=0, tiled=True),
        lax.all_gather(conv_taps, "fsdp", axis=0, tiled=True),
        lax.all_gather(conv_bias, "fsdp", axis=0, tiled=True),
        lax.all_gather(dt_bias, "fsdp", axis=0, tiled=True),
        lax.all_gather(decay_log, "fsdp", axis=0, tiled=True),
        lax.all_gather(skip_scale, "fsdp", axis=0, tiled=True),
        lax.all_gather(mixer_gain, "fsdp", axis=0, tiled=True),
    )
    rim_rows, rim_seg = passed_along(
        (conv_input[length - CONV + 1 :], seg_ids[length - CONV + 1 :]), "ctx", 1
    )
    ext_rows = jnp.concatenate([rim_rows, conv_input], axis=0).astype(jnp.float32)
    seg_ext = jnp.concatenate([rim_seg, seg_ids], axis=0)
    seg_start = rim_seg[CONV - 2]

    def front_fn(ext_arg, dt_arg, taps_arg, bias_arg, dtb_arg, decay_arg):
        return mixer_front(
            ext_arg, dt_arg, taps_arg, bias_arg, dtb_arg, decay_arg, seg_ext, seg_ids, seg_start
        )

    front_out, front_back = jax.vjp(
        front_fn,
        ext_rows,
        dt_raw,
        taps_whole.astype(jnp.float32),
        bias_whole.astype(jnp.float32),
        dtb_whole.astype(jnp.float32),
        decay_whole.astype(jnp.float32),
    )
    values, c_rows, running, y_local, carried, retain = front_out
    identity = (jnp.ones((HEADS,), jnp.float32), jnp.zeros((HEADS, HDIM, STATE), jnp.float32))
    passed = prefix((retain, carried), "ctx", combine, identity)
    carried_in = passed[1]
    carry_flag = (seg_ids == seg_start).astype(jnp.float32)

    def tail_fn(
        values_arg, c_arg, running_arg, local_arg, carried_arg, gate_arg, skip_arg, gain_arg
    ):
        return mixer_tail(
            values_arg,
            c_arg,
            running_arg,
            local_arg,
            carried_arg,
            gate_arg,
            skip_arg,
            gain_arg,
            carry_flag,
        )

    mixer_out, tail_back = jax.vjp(
        tail_fn,
        values,
        c_rows,
        running,
        y_local,
        carried_in,
        gate_part,
        skip_whole.astype(jnp.float32),
        norm_whole.astype(jnp.float32),
    )
    mixer_low = mixer_out.astype(jnp.bfloat16)
    mixed = jnp.dot(mixer_low, out_whole, preferred_element_type=jnp.float32)
    summed_out = units + mixed
    block_out = summed_out.astype(jnp.bfloat16)
    cot_rows = out_grad[0]
    d_out_matrix = lax.dot_general(
        mixer_low, cot_rows, (((0,), (0,)), ((), ())), preferred_element_type=jnp.float32
    )
    d_mixer = lax.dot_general(
        cot_rows, out_whole, (((1,), (1,)), ((), ())), preferred_element_type=jnp.float32
    )
    d_values, d_c_rows, d_running, d_local, d_carried, d_gate, d_skip, d_norm_gain = tail_back(
        d_mixer
    )
    reversed_pair = prefix_2((retain, d_carried), "ctx", combine, identity)
    d_state = reversed_pair[1]
    d_retain = jnp.sum(d_state * carried_in, axis=(1, 2))
    d_ext, d_dt_raw, d_taps, d_bias, d_dtb, d_decay = front_back(
        (d_values, d_c_rows, d_running, d_local, d_state, d_retain)
    )
    returned = passed_along(d_ext[: CONV - 1].astype(jnp.bfloat16), "ctx", -1).astype(jnp.float32)
    d_conv_in = jnp.concatenate([d_ext[CONV - 1 : length], d_ext[length:] + returned], axis=0)
    d_projected = jnp.concatenate([d_gate, d_conv_in, d_dt_raw], axis=1).astype(jnp.bfloat16)
    d_in_matrix = lax.dot_general(
        part_rows, d_projected, (((0,), (0,)), ((), ())), preferred_element_type=jnp.float32
    )
    d_normed = lax.dot_general(
        d_projected,
        lax.all_gather(in_matrix, "fsdp", axis=0, tiled=True),
        (((1,), (1,)), ((), ())),
        preferred_element_type=jnp.float32,
    )
    d_input_gain = jnp.sum(d_normed * base_rows, axis=0)
    d_base = d_normed * g_float
    d_units = inv_rms * (d_base - base_rows * jnp.mean(d_base * base_rows, axis=-1, keepdims=True))
    input_grad = (cot_rows.astype(jnp.float32) + d_units).astype(jnp.bfloat16)
    split_sums = (
        lax.psum_scatter(
            d_in_matrix.astype(jnp.bfloat16), "fsdp", scatter_dimension=0, tiled=True
        ).astype(jnp.float32),
        lax.psum_scatter(
            d_out_matrix.astype(jnp.bfloat16), "fsdp", scatter_dimension=0, tiled=True
        ).astype(jnp.float32),
        lax.psum_scatter(
            d_taps.astype(jnp.bfloat16), "fsdp", scatter_dimension=0, tiled=True
        ).astype(jnp.float32),
        lax.psum_scatter(
            d_bias.astype(jnp.bfloat16), "fsdp", scatter_dimension=0, tiled=True
        ).astype(jnp.float32),
        lax.psum_scatter(
            d_norm_gain.astype(jnp.bfloat16), "fsdp", scatter_dimension=0, tiled=True
        ).astype(jnp.float32),
        lax.psum_scatter(
            d_input_gain.astype(jnp.bfloat16), "fsdp", scatter_dimension=0, tiled=True
        ).astype(jnp.float32),
    )
    reduced = (
        lax.psum(split_sums[0].astype(jnp.bfloat16), "ctx").astype(jnp.float32),
        lax.psum(split_sums[1].astype(jnp.bfloat16), "ctx").astype(jnp.float32),
        lax.psum(split_sums[2].astype(jnp.bfloat16), "ctx").astype(jnp.float32),
        lax.psum(split_sums[3].astype(jnp.bfloat16), "ctx").astype(jnp.float32),
        lax.psum(split_sums[4].astype(jnp.bfloat16), "ctx").astype(jnp.float32),
        lax.psum(split_sums[5].astype(jnp.bfloat16), "ctx").astype(jnp.float32),
    )
    square_sums = jnp.stack([jnp.sum(summed_out * summed_out), jnp.sum(mixed * mixed)])
    head_dt, head_decay, head_skip, stat_sums = lax.psum(
        (d_dtb, d_decay, d_skip, square_sums), ("fsdp", "ctx")
    )
    per_shard = HEADS // lax.axis_size("fsdp")
    offset_rows = lax.axis_index("fsdp") * per_shard
    dt_grad = lax.dynamic_slice_in_dim(head_dt, offset_rows, per_shard, 0)
    decay_grad = lax.dynamic_slice_in_dim(head_decay, offset_rows, per_shard, 0)
    skip_grad = lax.dynamic_slice_in_dim(head_skip, offset_rows, per_shard, 0)
    entries = length * lax.axis_size("fsdp") * lax.axis_size("ctx") * D
    rms_stats = jnp.sqrt(stat_sums / entries)
    return (
        block_out[None],
        input_grad[None],
        reduced[0],
        reduced[1],
        reduced[2],
        reduced[3],
        dt_grad,
        decay_grad,
        skip_grad,
        reduced[4],
        reduced[5],
        rms_stats,
    )


def solution(mesh):
    return jax.shard_map(
        on_device,
        mesh=mesh,
        in_specs=(
            P("fsdp", "ctx", None),
            P("fsdp", "ctx"),
            P("fsdp", "ctx", None),
            P("fsdp", None),
            P("fsdp", None),
            P("fsdp", None),
            P("fsdp"),
            P("fsdp"),
            P("fsdp"),
            P("fsdp"),
            P("fsdp"),
            P("fsdp"),
        ),
        out_specs=(
            P("fsdp", "ctx", None),
            P("fsdp", "ctx", None),
            P("fsdp", None),
            P("fsdp", None),
            P("fsdp", None),
            P("fsdp"),
            P("fsdp"),
            P("fsdp"),
            P("fsdp"),
            P("fsdp"),
            P("fsdp"),
            P(),
        ),
        check_vma=False,
    )
```

profile of v0, /device:TPU:0, one launch (start us, length us, event | category | flops | bytes accessed | tf_op | source)
XLA Modules:
  0.0 1636.9 jit_solution(982712403689798339)
XLA Ops:
  44.6 93.2 %all-gather.11.cloned.1.call-done = bf16[1536,6448]{0,1:T(8,128)(2,1)} async-done(((bf16[384,6448]{0,1:T(8,128)(2,1)}), bf16[1536,6448]{0,1:T(8,128)(2,1)}) %all-gather.11.cloned.1.call-update) | async-done | bytes 19808272 | tf_op jit(solution)/shard_map/all_gather | solution.py:179
  137.8 16.7 %convolution_convert_fusion.2 = bf16[512,6448]{1,0:T(8,128)(2,1)} fusion(bf16[1536,6448]{0,1:T(8,128)(2,1)} %all-gather.11.cloned.1.call-done, bf16[1,512,1536]{2,1,0:T(8,128)(2,1)S(1)} %copy-done.14, f32[1536]{0:T(1024)S(1)} %reshape.551, f32[512]{0:T(512)S(1)} %add_rsqrt_fusion), kind=kOutput, calls=%fused_computation.150 | convolution fusion | flops 10148274176 | bytes 27992064 | tf_op jit(solution)/shard_map/dot_general | solution.py:183
  205.0 210.1 %while.80 = (s32[]{:T(128)}, f32[48,64,128]{2,1,0:T(8,128)S(1)}, s32[]{:T(128)}, f32[48]{0:T(128)S(1)}, f32[2,256,48,64]{1,0,3,2:T(2,128)}, /*index=5*/f32[2,256...) while((s32[]{:T(128)}, f32[48,64,128]{2,1,0:T(8,128)S(1)}, ...), condition=%wide.region_4.5_spmd.clone, body=%wide.region_1.4_spmd.clone.sunk | while | flops 4951254016 | bytes 38503760 | solution.py:121
  208.6 16.5 %fusion.240 = f32[48,64,256]{2,1,0:T(8,128)} fusion(f32[48,256]{1,0:T(8,128)S(1)} %dynamic-slice_bitcast_fusion.17, f32[256,256]{1,0:T(8,128)S(1)} %fusion.238, f32[48,256]{1,0:T(8,128)S(1)} %get-tuple-element.1556, pred[256,256]{1,0:T(8,128)(4,1)S(1)} %fusion.239, f32[2,256,48,64]{1,3,2,0:T(8,128)} %get-tuple-element.1663, s32[]{:T(128)} %get-tuple-element.1634), kind=kOutput, calls=%fused_computation.6.clone.1 | convolution fusion | flops 2428502016 | bytes 6767104 | tf_op jit(solution)/shard_map/jvp()/while/body/eval_jaxpr/hts,shp->thp/dot_general | solution.py:84
  236.9 63.6 %dynamic_update_slice.95 = f32[2,256,48,64]{1,0,3,2:T(2,128)} dynamic-update-slice(f32[2,256,48,64]{1,0,3,2:T(2,128)} %get-tuple-element.1638, f32[1,256,48,64]{1,0,3,2:T(1,128)} %copy.397, s32[]{:T(128)} %get-tuple-element.1634, s32[]{:T(128)} %constant.198.clone.1..sunk.1, s32[]{:T(128)} %constant.198.clone.1..sunk.1, s32[]{:T(128)} %constant.198.clone.1..sunk.1) | dynamic-update-slice | bytes 6291460 | tf_op jit(solution)/shard_map/jvp()/while/body/jit(dynamic_update_index_in_dim)/dynamic_update_slice | solution.py:121
  313.4 16.5 %fusion.240 = f32[48,64,256]{2,1,0:T(8,128)} fusion(f32[48,256]{1,0:T(8,128)S(1)} %dynamic-slice_bitcast_fusion.17, f32[256,256]{1,0:T(8,128)S(1)} %fusion.238, f32[48,256]{1,0:T(8,128)S(1)} %get-tuple-element.1556, pred[256,256]{1,0:T(8,128)(4,1)S(1)} %fusion.239, f32[2,256,48,64]{1,3,2,0:T(8,128)} %get-tuple-element.1663, s32[]{:T(128)} %get-tuple-element.1634), kind=kOutput, calls=%fused_computation.6.clone.1 | convolution fusion | flops 2428502016 | bytes 6767104 | tf_op jit(solution)/shard_map/jvp()/while/body/eval_jaxpr/hts,shp->thp/dot_general | solution.py:84
  341.7 63.6 %dynamic_update_slice.95 = f32[2,256,48,64]{1,0,3,2:T(2,128)} dynamic-update-slice(f32[2,256,48,64]{1,0,3,2:T(2,128)} %get-tuple-element.1638, f32[1,256,48,64]{1,0,3,2:T(1,128)} %copy.397, s32[]{:T(128)} %get-tuple-element.1634, s32[]{:T(128)} %constant.198.clone.1..sunk.1, s32[]{:T(128)} %constant.198.clone.1..sunk.1, s32[]{:T(128)} %constant.198.clone.1..sunk.1) | dynamic-update-slice | bytes 6291460 | tf_op jit(solution)/shard_map/jvp()/while/body/jit(dynamic_update_index_in_dim)/dynamic_update_slice | solution.py:121
  425.2 18.4 %all-gather.4 = bf16[8,1,48]{2,1,0:T(2,128)(2,1)S(1)} all-gather(bf16[1,1,48]{2,1,0:T(2,128)(2,1)S(1)} %bitcast.512), channel_id=1, replica_groups=mesh['fsdp'=4,'ctx'=8] {'ctx'}, dimensions={0}, use_global_device_ids=true | all-gather | bytes 864 | tf_op jit(solution)/shard_map/all_gather | solution.py:29
  452.6 61.9 %all-gather.15.cloned.1.call-done = bf16[384,64,128]{2,1,0:T(8,128)(2,1)} async-done(((bf16[48,64,128]{2,1,0:T(8,128)(2,1)}), bf16[384,64,128]{2,1,0:T(8,128)(2,1)}) %all-gather.15.cloned.1.call-update) | async-done | bytes 6291472 | tf_op jit(solution)/shard_map/all_gather | solution.py:29
  514.7 13.1 multiply_add_fusion.4
  541.2 37.4 %all-gather.13.cloned.1.call-done = bf16[3072,1536]{1,0:T(8,128)(2,1)} async-done(((bf16[768,1536]{1,0:T(8,128)(2,1)}), bf16[3072,1536]{1,0:T(8,128)(2,1)}) %all-gather.13.cloned.1.call-update) | async-done | bytes 9437200 | tf_op jit(solution)/shard_map/all_gather | solution.py:190
  578.6 12.5 multiply_reduce_fusion.9
  645.4 70.8 %all-gather.17.cloned.1.call-done = bf16[384,64,128]{2,1,0:T(8,128)(2,1)} async-done(((bf16[48,64,128]{2,1,0:T(8,128)(2,1)}), bf16[384,64,128]{2,1,0:T(8,128)(2,1)}) %all-gather.17.cloned.1.call-update) | async-done | bytes 6291472 | tf_op jit(solution)/shard_map/all_gather | solution.py:49
  716.2 24.0 %while.81 = (s32[]{:T(128)}, f32[48,64,128]{2,1,0:T(8,128)}, s32[]{:T(128)}, bf16[8,48]{1,0:T(8,128)(2,1)S(1)}, bf16[8,48,64,128]{3,2,1,0:T(8,128)(2,1)}, /*index=5*/s32[]{:T(128)}, s32[]{:T(128)}, s32[]{:T(128)}, s32[]{:T(128)}) while((s32[]{:T(128)}, f32[48,64,128]{2,1,0:T(8,128)}, s32[]{:T(128)}, ...), condition=%wide.region_10.11_spmd.clone, body=%wide.region_9.10_spmd.clone.sunk | while | flops 1966136 | bytes 3932807 | solution.py:65
  749.2 248.0 %while.82 = (s32[]{:T(128)}, f32[48,64,128]{2,1,0:T(8,128)}, f32[48]{0:T(128)}, f32[2,256,48,64]{1,3,2,0:T(8,128)}, f32[2,256,128]{2,1,0:T(8,128)}, /*index=5*/f...) while((s32[]{:T(128)}, f32[48,64,128]{2,1,0:T(8,128)}, ...), condition=%wide.region_26.27_spmd.clone, body=%wide.region_13.26_spmd.clone.sunk | while | flops 11239392256 | bytes 115198616 | solution.py:121
  809.2 21.4 %fusion.264 = (f32[48,256]{1,0:T(8,128)S(1)}, f32[48,256]{1,0:T(8,128)S(1)}, f32[48,256]{1,0:T(8,128)}, f32[256,256]{1,0:T(8,128)}) fusion(f32[48,256]{1,0:T(8,128)S(1)} %bitcast.484, f32[256,256]{1,0:T(8,128)S(1)} %fusion.262, f32[48,256]{1,0:T(8,128)} %get-tuple-element.1594, pred[256,256]{1,0:T(8,128)(4,1)S(1)} %fusion.263, ...), kind=kOutput, calls=%fused_computation.72.clone.1 | convolution fusion | flops 2456711168 | bytes 7127040 | tf_op jit(solution)/shard_map/transpose(jvp())/while/body/eval_jaxpr/checkpoint/hts,shp->thp/dot_general | solution.py:84
  860.7 12.2 bitcast_dynamic-update-slice_fusion.7
  919.4 21.4 %fusion.264 = (f32[48,256]{1,0:T(8,128)S(1)}, f32[48,256]{1,0:T(8,128)S(1)}, f32[48,256]{1,0:T(8,128)}, f32[256,256]{1,0:T(8,128)}) fusion(f32[48,256]{1,0:T(8,128)S(1)} %bitcast.484, f32[256,256]{1,0:T(8,128)S(1)} %fusion.262, f32[48,256]{1,0:T(8,128)} %get-tuple-element.1594, pred[256,256]{1,0:T(8,128)(4,1)S(1)} %fusion.263, ...), kind=kOutput, calls=%fused_computation.72.clone.1 | convolution fusion | flops 2456711168 | bytes 7127040 | tf_op jit(solution)/shard_map/transpose(jvp())/while/body/eval_jaxpr/checkpoint/hts,shp->thp/dot_general | solution.py:84
  971.0 12.2 bitcast_dynamic-update-slice_fusion.7
  997.2 12.7 fusion.132
  1009.9 11.3 copy.299
  1075.3 16.4 convolution_convert_fusion
  1091.6 24.2 %copy.300 = bf16[1536,6448]{1,0:T(8,128)(2,1)} copy(bf16[1536,6448]{0,1:T(8,128)(2,1)} %convolution_convert_fusion) | data formatting | bytes 39616512
  1117.2 11.2 convolution_convert_fusion.1
  1130.3 133.6 %reduce-scatter.10.cloned.1.call-done = bf16[384,6448]{1,0:T(8,128)(2,1)} async-done(((bf16[1536,6448]{1,0:T(8,128)(2,1)}), bf16[384,6448]{1,0:T(8,128)(2,1)}) %reduce-scatter.10.cloned.1.call-update) | async-done | bytes 4952080
  1271.5 74.1 %reduce-scatter.8.cloned.1.call-done = bf16[768,1536]{1,0:T(8,128)(2,1)} async-done(((bf16[3072,1536]{1,0:T(8,128)(2,1)}), bf16[768,1536]{1,0:T(8,128)(2,1)}) %reduce-scatter.8.cloned.1.call-update) | async-done | bytes 2359312 | tf_op jit(solution)/shard_map/reduce_scatter | solution.py:291
  1348.0 20.0 %fusion.135 = f32[512,1536]{1,0:T(8,128)S(1)} fusion(bf16[1536,6448]{0,1:T(8,128)(2,1)} %all-gather.11.cloned.1.call-done, bf16[512,48]{1,0:T(8,128)(2,1)S(1)} %copy-done.49, bf16[3,3328]{1,0:T(4,128)(2,1)S(1)} %fusion.147, bf16[509,3328]{1,0:T(8,128)(2,1)} %copy-done.19, bf16[512,3072]{1,0:T(8,128)(2,1)} %get-tuple-element.1248), kind=kOutput, calls=%fused_computation.222 | convolution fusion | flops 10168238080 | bytes 29556736 | tf_op jit(solution)/shard_map/dot_general | solution.py:277
  1368.1 12.7 multiply_reduce_fusion.15
  1382.2 44.0 %all-reduce.20 = (f32[48]{0:T(128)S(1)}, f32[48]{0:T(128)S(1)}, f32[48]{0:T(128)S(1)}, f32[2]{0:T(128)S(1)}) all-reduce(f32[48]{0:T(128)S(1)} %copy-done.80, f32[48]{0:T(128)S(1)} %fusion.156, f32[48]{0:T(128)S(1)} %reduce_sum.376, f32[2]{0:T(128)S(1)} %pad_maximum_fusion.3), channel_id=1, replica_groups=mesh['fsdp'=4,'ctx'=8] {'fsdp','ctx'}, use_global_device_ids=true, to_apply=%region_42.43 | all-reduce | flops 146 | bytes 1168 | tf_op jit(solution)/shard_map/psum | solution.py:316
  1427.9 11.9 all-reduce.23
  1446.5 37.0 %all-reduce.21 = (bf16[832,4]{0,1:T(4,128)(2,1)S(1)}, bf16[832]{0:T(1024)(128)(2,1)S(1)}, bf16[768]{0:T(1024)(128)(2,1)S(1)}, bf16[384]{0:T(512)(128)(2,1)S(1)}) all-reduce(bf16[832,4]{0,1:T(4,128)(2,1)S(1)} %copy.303, bf16[832]{0:T(1024)(128)(2,1)S(1)} %dynamic-slice.5, ...), channel_id=1, replica_groups=mesh['fsdp'=4,'ctx'=8] {'ctx'}, use_global_device_ids=true, to_apply=%region_37.38 | all-reduce | flops 5312 | bytes 21248 | tf_op jit(solution)/shard_map/psum | solution.py:310
  1485.9 133.8 %all-reduce.27.cloned.1.call-done = (bf16[384,6448]{0,1:T(8,128)(2,1)}, bf16[768,1536]{1,0:T(8,128)(2,1)}) async-done(((bf16[384,6448]{0,1:T(8,128)(2,1)}, bf16[768,1536]{1,0:T(8,128)(2,1)}), (bf16[384,6448]{0,1:T(8,128)(2,1)}, bf16[768,1536]{1,0:T(8,128)(2,1)})) %all-reduce.27.cloned.1.call-update) | async-done | bytes 7311376 | tf_op jit(solution)/shard_map/psum | solution.py:308
  (527 shorter events, 487.0 us)
Async XLA Ops:
  7.2 130.6 %all-gather.11.cloned.1.call-start = ((), (), s32[]{:S(2)}) async-start(), calls=%async_computation.3 | async-start | bytes 24760320 | tf_op jit(solution)/shard_map/all_gather | solution.py:179
  7.9 506.6 %all-gather.15.cloned.1.call-start = ((), (), s32[]{:S(2)}) async-start(), calls=%async_computation.6 | async-start | bytes 7077888 | tf_op jit(solution)/shard_map/all_gather | solution.py:29
  8.7 33.3 %collective-permute-start = (s32[3]{0:T(128)S(1)}, s32[3]{0:T(128)S(1)}, u32[]{:S(2)}, u32[]{:S(2)}) collective-permute-start(s32[3]{0:T(128)S(1)} %slice_bitcast_fusion), channel_id=1, source_target_pairs={{0,1},{1,2},{2,3},{3,4},{4,5},{5,6},{6,7},{8,9},{9,10},{10,11},{11... | collective-permute-start | bytes 44 | tf_op jit(solution)/shard_map/ppermute | solution.py:23
  19.5 135.0 %copy-start.65 = (f32[1536]{0:T(1024)}, f32[1536]{0:T(1024)S(1)}, u32[]{:S(2)}) copy-start(f32[1536]{0:T(1024)S(1)} %reshape.551) | copy-start | bytes 18436
  33.8 120.7 %copy-start.83 = (bf16[48]{0:T(256)(128)(2,1)}, bf16[48]{0:T(256)(128)(2,1)S(1)}, u32[]{:S(2)}) copy-start(bf16[48]{0:T(256)(128)(2,1)S(1)} %get-tuple-element.1206) | copy-start | bytes 292
  39.5 119.4 %copy-start.76 = (f32[48]{0:T(128)}, f32[48]{0:T(128)S(1)}, u32[]{:S(2)}) copy-start(f32[48]{0:T(128)S(1)} %convert_element_type.241) | copy-start | bytes 580
  41.5 126.0 %copy-start.40 = (f32[3328]{0:T(1024)}, f32[3328]{0:T(1024)S(1)}, u32[]{:S(2)}) copy-start(f32[3328]{0:T(1024)S(1)} %get-tuple-element.1104) | copy-start | bytes 39940
  41.5 126.0 %copy-start.42 = (f32[3328]{0:T(1024)}, f32[3328]{0:T(1024)S(1)}, u32[]{:S(2)}) copy-start(f32[3328]{0:T(1024)S(1)} %get-tuple-element.1105) | copy-start | bytes 39940
  41.6 126.0 %copy-start.44 = (f32[3328]{0:T(1024)}, f32[3328]{0:T(1024)S(1)}, u32[]{:S(2)}) copy-start(f32[3328]{0:T(1024)S(1)} %get-tuple-element.1106) | copy-start | bytes 39940
  41.6 126.0 %copy-start.46 = (f32[3328]{0:T(1024)}, f32[3328]{0:T(1024)S(1)}, u32[]{:S(2)}) copy-start(f32[3328]{0:T(1024)S(1)} %get-tuple-element.1107) | copy-start | bytes 39940
  42.0 117.0 %copy-start.78 = (f32[48]{0:T(128)}, f32[48]{0:T(128)S(1)}, u32[]{:S(2)}) copy-start(f32[48]{0:T(128)S(1)} %convert_exponential_fusion) | copy-start | bytes 580
  42.0 112.5 %copy-start.73 = (f32[512]{0:T(512)}, f32[512]{0:T(512)S(1)}, u32[]{:S(2)}) copy-start(f32[512]{0:T(512)S(1)} %add_rsqrt_fusion) | copy-start | bytes 6148
  44.6 123.0 %copy-start.59 = (f32[512]{0:T(512)}, f32[512]{0:T(512)S(1)}, u32[]{:S(2)}) copy-start(f32[512]{0:T(512)S(1)} %get-tuple-element.1259) | copy-start | bytes 6148
  44.6 123.0 %copy-start.61 = (f32[512]{0:T(512)}, f32[512]{0:T(512)S(1)}, u32[]{:S(2)}) copy-start(f32[512]{0:T(512)S(1)} %get-tuple-element.1260) | copy-start | bytes 6148
  44.6 123.0 %copy-start.63 = (f32[512]{0:T(512)}, f32[512]{0:T(512)S(1)}, u32[]{:S(2)}) copy-start(f32[512]{0:T(512)S(1)} %get-tuple-element.1261) | copy-start | bytes 6148
  155.3 9.5 collective-permute-start.1
  205.0 212.5 %copy-start.81 = (bf16[768]{0:T(1024)(128)(2,1)S(1)}, bf16[768]{0:T(1024)(128)(2,1)}, u32[]{:S(2)}) copy-start(bf16[768]{0:T(1024)(128)(2,1)} %param.30) | copy-start | bytes 4612
  416.2 162.4 %all-gather.13.cloned.1.call-start = ((), (), s32[]{:S(2)}) async-start(), calls=%async_computation.4 | async-start | bytes 11796480 | tf_op jit(solution)/shard_map/all_gather | solution.py:190
  416.9 299.3 %all-gather.17.cloned.1.call-start = ((), (), s32[]{:S(2)}) async-start(), calls=%async_computation.7 | async-start | bytes 7077888 | tf_op jit(solution)/shard_map/all_gather | solution.py:49
  422.7 168.4 %copy-start.55 = (f32[4,1,768]{2,1,0:T(1,128)}, f32[4,1,768]{2,1,0:T(1,128)S(1)}, u32[]{:S(2)}) copy-start(f32[4,1,768]{2,1,0:T(1,128)S(1)} %convert_element_type.281) | copy-start | bytes 36868
  452.6 156.2 %copy-start.24 = (f32[512,48]{0,1:T(8,128)}, f32[512,48]{0,1:T(8,128)S(1)}, u32[]{:S(2)}) copy-start(f32[512,48]{0,1:T(8,128)S(1)} %exponential_multiply_fusion.4) | copy-start | bytes 294916
  514.7 225.5 %copy-start.2 = (f32[48,64,128]{2,1,0:T(8,128)}, f32[48,64,128]{2,1,0:T(8,128)S(1)}, u32[]{:S(2)}) copy-start(f32[48,64,128]{2,1,0:T(8,128)S(1)} %get-tuple-element.688) | copy-start | bytes 4718596
  617.1 646.9 %reduce-scatter.10.cloned.1.call-start = ((), (), s32[]{:S(2)}) async-start(), calls=%async_computation.8 | async-start | bytes 25067520
  1065.7 7.9 collective-permute-start.2
  1115.9 229.8 %reduce-scatter.8.cloned.1.call-start = ((), (), s32[]{:S(2)}) async-start(), calls=%async_computation.5 | async-start | bytes 11796480 | tf_op jit(solution)/shard_map/reduce_scatter | solution.py:291
  1128.5 317.0 %reduce-scatter.12.cloned.1.call-start = ((), (), s32[]{:S(2)}) async-start(), calls=%async_computation.9 | async-start | bytes 1064960
  1130.0 217.8 %copy-start.57 = (f32[3072]{0:T(1024)S(1)}, f32[3072]{0:T(1024)}, u32[]{:S(2)}) copy-start(f32[3072]{0:T(1024)} %get-tuple-element.1211) | copy-start | bytes 36868
  1130.0 218.0 %copy-start.82 = (f32[48]{0:T(128)S(1)}, f32[48]{0:T(128)}, u32[]{:S(2)}) copy-start(f32[48]{0:T(128)} %get-tuple-element.1249) | copy-start | bytes 580
  1130.0 218.0 %copy-start.84 = (bf16[48]{0:T(256)(128)(2,1)S(1)}, bf16[48]{0:T(256)(128)(2,1)}, u32[]{:S(2)}) copy-start(bf16[48]{0:T(256)(128)(2,1)} %copy-done.83) | copy-start | bytes 292
  1130.0 218.0 %copy-start.49 = (bf16[512,48]{1,0:T(8,128)(2,1)S(1)}, bf16[512,48]{1,0:T(8,128)(2,1)}, u32[]{:S(2)}) copy-start(bf16[512,48]{1,0:T(8,128)(2,1)} %copy-done.48) | copy-start | bytes 147460
  1130.0 489.6 %all-reduce.27.cloned.1.call-start = ((), (), s32[]{:S(2)}) async-start(), calls=%async_computation.10 | async-start | bytes 14622720 | tf_op jit(solution)/shard_map/psum | solution.py:308
  1368.1 59.8 %copy-start.75 = (bf16[3072]{0:T(1024)(128)(2,1)S(1)}, bf16[3072]{0:T(1024)(128)(2,1)}, u32[]{:S(2)}) copy-start(bf16[3072]{0:T(1024)(128)(2,1)} %get-tuple-element.1095) | copy-start | bytes 18436
  (98 other events, 1464.4 us)
Sparse Core Ops, SparseCore 0:
  9.6 128.1 all-gather.10
  416.3 98.1 all-gather.14
  516.1 62.4 all-gather.12
  617.2 99.0 all-gather.16
  1116.0 147.9 reduce-scatter.9
  1267.2 78.4 reduce-scatter.7
  1348.4 23.6 reduce-scatter.11
  1376.1 243.4 all-reduce.26
where the time goes:
time: 1660 us; the launch traced here: 1640 us
  waiting for transfers between devices  606 us (37%)
  local copies, waits for them, and re-layouts  345 us (21%)
  matrix products  310 us (19%)
  other arithmetic  174 us (10%)
  blocking collectives  135 us (8%)
  loops' own time  34.9 us (2%)
  between operations  20.9 us (1%)
    dynamic_update_slice x10, local copies, waits for them, and re-layouts, scan_ssd(): lax.scan(jax.checkpoint(block_step), initial, sliced)  142 us
    unnamed x10, waiting for transfers between devices  135 us
    psum x1, waiting for transfers between devices, on_device(): lax.psum(split_sums[0].astype(jnp.bfloat16), 'ctx').astype(jnp.float32)  134 us
    dot_general x6, matrix products, block_step(): y_diag = jnp.einsum('hts,shp->thp', mixing, xblock, precision=precise)  100 us
    all_gather x1, waiting for transfers between devices, on_device(): w_piece = lax.all_gather(in_matrix, 'fsdp', axis=0, tiled=True)  93.2 us
    reduce_scatter x1, waiting for transfers between devices, on_device(): lax.psum_scatter(d_out_matrix.astype(jnp.bfloat16), 'fsdp', scatter_dimen...  74.1 us
    all_gather x1, waiting for transfers between devices, prefix_2(): lax.all_gather(part.astype(kind), axis)  70.8 us
    all_gather x1, waiting for transfers between devices, prefix(): lax.all_gather(a.astype(kind), axis)  61.9 us
  transfers between devices with their start and end apart: 11, of which 7 were waited for; matrix products, arithmetic and copies ran while one was open for 9% of the time, Pallas kernels for 0%

commit v1 on v0

v1 whole, which is shorter than its diff:
```python
import functools

import jax
import jax.numpy as jnp
from jax import lax
from jax.experimental import pallas as pl
from jax.experimental.pallas import tpu as pltpu
from jax.sharding import PartitionSpec as P

D = 1536
HEADS = 48
HDIM = 64
STATE = 128
CONV = 4
INNER = 3072
XBC = 3328
PROJ = 6448

BLK = 256
GROUP = BLK // HDIM
STEPS = INNER // BLK
Q = 128
PAD = 8

epsilon = 1e-05
F32, BF16 = jnp.float32, jnp.bfloat16
HIGHEST = lax.Precision.HIGHEST
VMEM_LIMIT = 60 * 1024 * 1024


def dot(a, b):
    return jnp.dot(a, b, preferred_element_type=F32)


def dot_nt(a, b):
    return lax.dot_general(a, b, (((1,), (1,)), ((), ())), preferred_element_type=F32)


def iota(shape, dim):
    return lax.broadcasted_iota(jnp.int32, shape, dim)


def sigmoid(v):
    return 1.0 / (1.0 + jnp.exp(-v))


def in_two(a):
    high = a.astype(BF16)
    return high, (a - high.astype(F32)).astype(BF16)


def chosen(step):
    columns = step * GROUP + lax.shift_right_logical(iota((128, BLK), 1), 6)
    return (iota((128, BLK), 0) == columns).astype(BF16)


def chosen_back(step):
    heads = step * GROUP + lax.shift_right_logical(iota((BLK, 128), 0), 6)
    return (iota((BLK, 128), 1) == heads).astype(BF16)


def widen(per_head, select):
    high, low = in_two(per_head)
    return dot(high, select) + dot(low, select)


def halves(pair):
    first = iota(pair.shape, 1) < HDIM
    zero = jnp.zeros_like(pair)
    return jnp.concatenate([jnp.where(first, pair, zero), jnp.where(first, zero, pair)], axis=0)


def both(mask):
    return jnp.concatenate([mask, mask], axis=1)


def conv_rows(ext_ref, seg_ref, taps_ref, start, rows):
    own = seg_ref[start + PAD : start + PAD + rows, :]
    total = taps_ref[4:5, :] + taps_ref[3:4, :] * ext_ref[start + PAD : start + PAD + rows, :]
    for back in range(1, CONV):
        at = start + PAD - back
        same = both(seg_ref[at : at + rows, :] == own)
        total = total + jnp.where(
            same, taps_ref[3 - back : 4 - back, :] * ext_ref[at : at + rows, :], 0.0
        )
    return total


def chunk_flags(seg_ref, k):
    own = seg_ref[PAD + k * Q : PAD + (k + 1) * Q, :]
    before = seg_ref[PAD + k * Q - 1 : PAD + k * Q, :]
    last = seg_ref[PAD + (k + 1) * Q - 1 : PAD + (k + 1) * Q, :]
    return (own == before).astype(F32), (own == last).astype(F32)


def masked_scores(seg_ref, row_ref, b_rows, c_rows, k):
    own = seg_ref[PAD + k * Q : PAD + (k + 1) * Q, :]
    row = row_ref[0:1, k * Q : (k + 1) * Q]
    keep = (own == row) & (iota((Q, Q), 1) <= iota((Q, Q), 0))
    return jnp.where(keep, dot_nt(c_rows, b_rows), 0.0)


def front_kernel(
    x_ref, bc_ref, dtraw_ref, halo_ref, halo_bc_ref, taps_ref, taps_bc_ref, heads_ref, seg_ref, row_ref,
    xs_ref, y_ref, state_ref, b_ref, c_ref, dt_ref, run_ref, in_ref, keep_ref,
    ext, scores, run_t, b_t, enter, leave,
):
    step = pl.program_id(0)
    length = x_ref.shape[0]
    chunks = length // Q

    @pl.when(step == 0)
    def _():
        ext[0:PAD, :] = halo_bc_ref[...]
        ext[PAD:, :] = bc_ref[...].astype(F32)
        lane = iota((Q, 128), 1)
        lower = (iota((Q, Q), 1) <= iota((Q, Q), 0)).astype(F32)
        offset = jnp.zeros((1, 128), F32)
        for k in range(chunks):
            rows = slice(k * Q, (k + 1) * Q)
            total = conv_rows(ext, seg_ref, taps_bc_ref, k * Q, Q)
            active = total * sigmoid(total)
            b_rows, c_rows = active[:, :STATE], active[:, STATE:].astype(BF16)
            b_t[:, rows] = b_rows.T.astype(BF16)
            b_rows = b_rows.astype(BF16)
            b_ref[rows, :] = b_rows
            c_ref[rows, :] = c_rows
            scores[rows, :] = masked_scores(seg_ref, row_ref, b_rows, c_rows, k)
            raw = jnp.where(lane < HEADS, dtraw_ref[rows, :128].astype(F32), 0.0) + heads_ref[0:1, :]
            dt = jnp.maximum(raw, 0.0) + jnp.log1p(jnp.exp(-jnp.abs(raw)))
            log_decay = -dt * jnp.exp(heads_ref[1:2, :])
            running = jnp.dot(lower, log_decay, precision=HIGHEST, preferred_element_type=F32)
            dt_ref[rows, :] = dt
            run_ref[rows, :] = running
            run_t[k] = running.T
            carry, tail = chunk_flags(seg_ref, k)
            enter[rows, :] = jnp.exp(running) * carry
            leave[rows, :] = jnp.exp(running[Q - 1 : Q, :] - running) * tail
            same = (seg_ref[PAD + k * Q : PAD + (k + 1) * Q, :] == seg_ref[PAD - 1 : PAD, :]).astype(F32)
            whole = jnp.exp(running + offset) * same
            in_ref[rows, :] = whole
            offset = offset + running[Q - 1 : Q, :]
        keep_ref[...] = jnp.broadcast_to(whole[Q - 1 : Q, :], (8, 128))

    ext[0:PAD, :] = halo_ref[...]
    ext[PAD:, :] = x_ref[...].astype(F32)
    select = chosen(step)
    state = jnp.zeros((STATE, BLK), F32)
    for k in range(chunks):
        rows = slice(k * Q, (k + 1) * Q)
        total = conv_rows(ext, seg_ref, taps_ref, k * Q, Q)
        values = total * sigmoid(total)
        xs_ref[rows, :] = values.astype(BF16)
        scaled = (values * widen(dt_ref[rows, :], select)).astype(BF16)
        entering = widen(enter[rows, :], select)
        running = pltpu.roll(run_ref[rows, :], lax.rem(128 - step * GROUP, 128), 1)
        parts = []
        for pair in range(2):
            mixing = []
            for one in range(2):
                head = 2 * pair + one
                gap = running[:, head : head + 1] - run_t[k, pl.ds(step * GROUP + head, 1), :]
                mixing.append((jnp.exp(jnp.minimum(gap, 0.0)) * scores[rows, :]).astype(BF16))
            parts.append(
                dot(jnp.concatenate(mixing, axis=1), halves(scaled[:, pair * 128 : (pair + 1) * 128]))
            )
        inside = jnp.concatenate(parts, axis=1)
        y_ref[rows, :] = (inside + entering * dot(c_ref[rows, :], state.astype(BF16))).astype(BF16)
        weighted = (scaled.astype(F32) * widen(leave[rows, :], select)).astype(BF16)
        state = entering[Q - 1 : Q, :] * state + dot(b_t[:, rows], weighted)
    state_ref[...] = state.astype(BF16)


def front(projected, halo, taps, heads, seg_lanes, seg_row):
    length = projected.shape[0]
    whole = lambda *shape: pl.BlockSpec(shape, lambda j: (0,) * len(shape))
    columns = lambda rows, at: pl.BlockSpec((rows, BLK), at)
    return pl.pallas_call(
        front_kernel,
        grid=(STEPS,),
        in_specs=[
            columns(length, lambda j: (0, STEPS + j)),
            columns(length, lambda j: (0, 2 * STEPS)),
            columns(length, lambda j: (0, 2 * STEPS + 1)),
            columns(PAD, lambda j: (0, j)),
            columns(PAD, lambda j: (0, STEPS)),
            columns(8, lambda j: (0, j)),
            columns(8, lambda j: (0, STEPS)),
            whole(8, 128),
            whole(length + 2 * PAD, 128),
            whole(8, length),
        ],
        out_specs=[
            columns(length, lambda j: (0, j)),
            columns(length, lambda j: (0, j)),
            columns(STATE, lambda j: (0, j)),
            whole(length, 128),
            whole(length, 128),
            whole(length, 128),
            whole(length, 128),
            whole(length, 128),
            whole(8, 128),
        ],
        out_shape=[
            jax.ShapeDtypeStruct((length, INNER), BF16),
            jax.ShapeDtypeStruct((length, INNER), BF16),
            jax.ShapeDtypeStruct((STATE, INNER), BF16),
            jax.ShapeDtypeStruct((length, 128), BF16),
            jax.ShapeDtypeStruct((length, 128), BF16),
            jax.ShapeDtypeStruct((length, 128), F32),
            jax.ShapeDtypeStruct((length, 128), F32),
            jax.ShapeDtypeStruct((length, 128), F32),
            jax.ShapeDtypeStruct((8, 128), F32),
        ],
        scratch_shapes=[
            pltpu.VMEM((length + PAD, BLK), F32),
            pltpu.VMEM((length, Q), F32),
            pltpu.VMEM((length // Q, 128, Q), F32),
            pltpu.VMEM((128, length), BF16),
            pltpu.VMEM((length, 128), F32),
            pltpu.VMEM((length, 128), F32),
        ],
        compiler_params=pltpu.CompilerParams(vmem_limit_bytes=VMEM_LIMIT),
        cost_estimate=pl.CostEstimate(
            flops=6 * 10**9, bytes_accessed=16 * 10**6, transcendentals=10**7
        ),
        name="front",
    )(projected, projected, projected, halo, halo, taps, taps, heads, seg_lanes, seg_row)


def weights_of_parts(kept_ref, place, before):
    count = kept_ref.shape[0]
    result = [None] * count
    run = jnp.ones((1, 128), F32)
    for part in range(count - 1, -1, -1) if before else range(count):
        inside = (part < place) if before else (part > place)
        result[part] = jnp.where(inside, run, 0.0)
        run = run * jnp.where(inside, kept_ref[part, 0:1, :], 1.0)
    return result


def joined_states(states_ref, kept_ref, place, select, before):
    weights = weights_of_parts(kept_ref, place, before)
    count = len(weights)
    stacked = jnp.concatenate(weights + [jnp.zeros((-count % 8, 128), F32)] * (count % 8 > 0), axis=0)
    wide = widen(stacked, select)
    total = jnp.zeros((STATE, BLK), F32)
    for part in range(count):
        total = total + wide[part : part + 1, :] * states_ref[part].astype(F32)
    return total


def tail_kernel(
    place_ref, y_ref, xs_ref, gate_ref, states_ref, kept_ref, out_ref, c_ref, in_ref, heads_ref, gain_ref, g_ref, units_ref,
    mixer_ref, dproj_ref, dy_ref, sin_ref, dsin_ref, sums_ref, block_ref, stats_ref,
    full, dmix, squares, products, mixed, c_t,
):
    step = pl.program_id(0)
    length = y_ref.shape[0]
    group = lax.rem(step, STEPS)
    select = chosen(group)
    half = length // 2

    @pl.when(step == 0)
    def _():
        squares[...] = jnp.zeros_like(squares)
        products[...] = jnp.zeros_like(products)
        for k in range(length // Q):
            rows = slice(k * Q, (k + 1) * Q)
            c_t[:, rows] = c_ref[rows, :].astype(F32).T.astype(BF16)

    @pl.when(step < STEPS)
    def _():
        incoming = joined_states(states_ref, kept_ref, place_ref[0], select, True).astype(BF16)
        sin_ref[...] = incoming
        skip = widen(heads_ref[...], select)[2:3, :]
        for k in range(2):
            rows = slice(k * half, (k + 1) * half)
            y = y_ref[rows, :].astype(F32)
            y = y + widen(in_ref[rows, :], select) * dot(c_ref[rows, :], incoming)
            y = y + skip * xs_ref[rows, :].astype(F32)
            full[step, rows, :] = y
            gate = gate_ref[rows, :].astype(F32)
            gated = y * gate * sigmoid(gate)
            d_mixer = dot_nt(g_ref[rows, :], out_ref[...])
            dmix[step, rows, :] = d_mixer
            square = gated * gated
            product = gated * d_mixer * gain_ref[0:1, :]
            squares[rows, :] += square[:, :128] + square[:, 128:]
            products[rows, :] += product[:, :128] + product[:, 128:]

    @pl.when(step == STEPS)
    def _():
        norm = lax.rsqrt(jnp.sum(squares[...], axis=1, keepdims=True) * (1.0 / INNER) + epsilon)
        mean = norm * jnp.sum(products[...], axis=1, keepdims=True) * (1.0 / INNER)
        squares[...] = jnp.broadcast_to(norm, squares.shape)
        products[...] = jnp.broadcast_to(mean, products.shape)

    @pl.when(step >= STEPS)
    def _():
        gain = gain_ref[0:1, :]
        d_gain = jnp.zeros((1, BLK), F32)
        d_skip = jnp.zeros((1, BLK), F32)
        d_state = jnp.zeros((STATE, BLK), F32)
        for k in range(2):
            rows = slice(k * half, (k + 1) * half)
            norm, mean = both(squares[rows, :]), both(products[rows, :])
            y = full[group, rows, :]
            d_mixer = dmix[group, rows, :]
            gate = gate_ref[rows, :].astype(F32)
            sig = sigmoid(gate)
            silu = gate * sig
            unit = y * silu * norm
            low = (unit * gain).astype(BF16)
            mixer_ref[rows, :] = low
            part = dot(low, out_ref[...])

            @pl.when(step == STEPS)
            def _():
                mixed[rows, :] = part

            @pl.when(step > STEPS)
            def _():
                mixed[rows, :] += part

            d_gain = d_gain + jnp.sum(d_mixer * unit, axis=0, keepdims=True)
            d_gated = norm * (d_mixer * gain - unit * mean)
            dproj_ref[rows, :] = (d_gated * y * (sig * (1.0 + gate * (1.0 - sig)))).astype(BF16)
            dy = (d_gated * silu).astype(BF16)
            dy_ref[rows, :] = dy
            dy = dy.astype(F32)
            d_skip = d_skip + jnp.sum(dy * xs_ref[rows, :].astype(F32), axis=0, keepdims=True)
            d_state = d_state + dot(c_t[:, rows], (dy * widen(in_ref[rows, :], select)).astype(BF16))
        dsin_ref[...] = d_state.astype(BF16)
        sums_ref[...] = jnp.concatenate([d_gain, d_skip, jnp.zeros((6, BLK), F32)], axis=0)

    @pl.when(step == 2 * STEPS - 1)
    def _():
        total = units_ref[...].astype(F32) + mixed[...]
        block_ref[...] = total.astype(BF16)
        first = jnp.sum(total * total, axis=0, keepdims=True)
        second = jnp.sum(mixed[...] * mixed[...], axis=0, keepdims=True)
        stats_ref[...] = jnp.concatenate([first, second, jnp.zeros((6, D), F32)], axis=0)


def tail(place, y, xs, projected, states, kept, out_whole, c_rows, entering, heads, gain, cot, units):
    length = y.shape[0]
    count = states.shape[0]
    early = lambda rows: pl.BlockSpec((rows, BLK), lambda i: (0, jnp.minimum(i, STEPS - 1)))
    late = lambda rows: pl.BlockSpec((rows, BLK), lambda i: (0, jnp.maximum(i - STEPS, 0)))
    each = lambda rows: pl.BlockSpec((rows, BLK), lambda i: (0, lax.rem(i, STEPS)))
    whole = lambda *shape: pl.BlockSpec(shape, lambda i: (0,) * len(shape))
    return pl.pallas_call(
        tail_kernel,
        grid=(2 * STEPS,),
        in_specs=[
            pl.BlockSpec(memory_space=pltpu.SMEM),
            early(length),
            each(length),
            each(length),
            pl.BlockSpec((count, STATE, BLK), lambda i: (0, 0, jnp.minimum(i, STEPS - 1))),
            whole(count, 8, 128),
            pl.BlockSpec((BLK, D), lambda i: (lax.rem(i, STEPS), 0)),
            whole(length, 128),
            whole(length, 128),
            whole(8, 128),
            each(8),
            whole(length, D),
            whole(length, D),
        ],
        out_specs=[
            late(length),
            late(length),
            late(length),
            early(STATE),
            late(STATE),
            late(8),
            whole(length, D),
            whole(8, D),
        ],
        out_shape=[
            jax.ShapeDtypeStruct((length, INNER), BF16),
            jax.ShapeDtypeStruct((length, PROJ), BF16),
            jax.ShapeDtypeStruct((length, INNER), BF16),
            jax.ShapeDtypeStruct((STATE, INNER), BF16),
            jax.ShapeDtypeStruct((STATE, INNER), BF16),
            jax.ShapeDtypeStruct((8, INNER), F32),
            jax.ShapeDtypeStruct((length, D), BF16),
            jax.ShapeDtypeStruct((8, D), F32),
        ],
        scratch_shapes=[
            pltpu.VMEM((STEPS, length, BLK), F32),
            pltpu.VMEM((STEPS, length, BLK), F32),
            pltpu.VMEM((length, 128), F32),
            pltpu.VMEM((length, 128), F32),
            pltpu.VMEM((length, D), F32),
            pltpu.VMEM((128, length), BF16),
        ],
        compiler_params=pltpu.CompilerParams(vmem_limit_bytes=VMEM_LIMIT),
        cost_estimate=pl.CostEstimate(
            flops=12 * 10**9, bytes_accessed=50 * 10**6, transcendentals=4 * 10**6
        ),
        name="tail",
    )(place, y, xs, projected, states, kept, out_whole, c_rows, entering, heads, gain, cot, units)


def back_kernel(
    place_ref, x_ref, dtraw_ref, halo_ref, taps_ref, heads_ref, seg_ref, row_ref, b_ref, c_ref, dt_ref, run_ref,
    dy_ref, sin_ref, dstates_ref, kept_ref, given_ref,
    dproj_ref, dhalo_ref, dtaps_ref, dheads_ref,
    ext, pre, dact, dbuf, scores, dscores, run_t, b_t, c_t, enter, leave, d_b, d_c, suffix, prefix, d_dt, fixed, states,
):
    step = pl.program_id(0)
    length = x_ref.shape[0]
    chunks = length // Q

    @pl.when(step == 0)
    def _():
        for k in range(chunks):
            rows = slice(k * Q, (k + 1) * Q)
            b_rows, c_rows = b_ref[rows, :], c_ref[rows, :]
            b_t[:, rows] = b_rows.astype(F32).T.astype(BF16)
            c_t[:, rows] = c_rows.astype(F32).T.astype(BF16)
            scores[rows, :] = masked_scores(seg_ref, row_ref, b_rows, c_rows, k)
            running = run_ref[rows, :]
            run_t[k] = running.T
            carry, tail = chunk_flags(seg_ref, k)
            enter[rows, :] = jnp.exp(running) * carry
            leave[rows, :] = jnp.exp(running[Q - 1 : Q, :] - running) * tail
        for each in (dscores, d_b, d_c, suffix, prefix, d_dt, fixed):
            each[...] = jnp.zeros_like(each)
        dbuf[0:PAD, :] = jnp.zeros((PAD, BLK), F32)
        dbuf[PAD + length :, :] = jnp.zeros((PAD, BLK), F32)

    @pl.when(step <= STEPS)
    def _():
        ext[0:PAD, :] = halo_ref[...]
        ext[PAD:, :] = x_ref[...].astype(F32)
        for k in range(chunks):
            pre[k * Q : (k + 1) * Q, :] = conv_rows(ext, seg_ref, taps_ref, k * Q, Q)

    @pl.when(step < STEPS)
    def _():
        select = chosen(step)
        gather = chosen_back(step)
        skip = widen(heads_ref[...], select)[2:3, :]
        state = sin_ref[...].astype(F32)
        for k in range(chunks):
            rows = slice(k * Q, (k + 1) * Q)
            states[k] = state
            if k + 1 < chunks:
                total = pre[rows, :]
                scaled = total * sigmoid(total) * widen(dt_ref[rows, :], select)
                weighted = (scaled.astype(BF16).astype(F32) * widen(leave[rows, :], select)).astype(BF16)
                last = widen(enter[rows.stop - 8 : rows.stop, :], select)[7:8, :]
                state = last * state + dot(b_t[:, rows], weighted)
        d_state = joined_states(dstates_ref, kept_ref, place_ref[0], select, False)
        for k in range(chunks - 1, -1, -1):
            rows = slice(k * Q, (k + 1) * Q)
            total = pre[rows, :]
            values = total * sigmoid(total)
            step_size = widen(dt_ref[rows, :], select)
            entering = widen(enter[rows, :], select)
            leaving = widen(leave[rows, :], select)
            scaled = (values * step_size).astype(BF16)
            scaled_wide = scaled.astype(F32)
            dy = dy_ref[rows, :]
            dy_wide = dy.astype(F32)
            before = states[k]
            before_low = before.astype(BF16)
            d_low = d_state.astype(BF16)
            running = pltpu.roll(run_ref[rows, :], lax.rem(128 - step * GROUP, 128), 1)
            insides, backs = [], []
            d_score = dscores[rows, :]
            for pair in range(2):
                lanes = slice(pair * 128, (pair + 1) * 128)
                mixing, turned, decays = [], [], []
                for one in range(2):
                    head = 2 * pair + one
                    gap = running[:, head : head + 1] - run_t[k, pl.ds(step * GROUP + head, 1), :]
                    decay = jnp.exp(jnp.minimum(gap, 0.0))
                    mixed = decay * scores[rows, :]
                    decays.append(decay)
                    mixing.append(mixed.astype(BF16))
                    turned.append(mixed.T.astype(BF16))
                spread = halves(scaled[:, lanes])
                insides.append(dot(jnp.concatenate(mixing, axis=1), spread))
                backs.append(dot(jnp.concatenate(turned, axis=1), halves(dy[:, lanes])))
                products = dot_nt(dy[:, lanes], spread)
                d_score = d_score + decays[0] * products[:, :Q] + decays[1] * products[:, Q:]
            dscores[rows, :] = d_score
            inside = jnp.concatenate(insides, axis=1) + entering * dot(c_ref[rows, :], before_low)
            back_inside = jnp.concatenate(backs, axis=1)
            back_state = leaving * dot(b_ref[rows, :], d_low)
            high, low = in_two(dy_wide * inside - scaled_wide * back_inside)
            suffix[rows, :] += dot(high, gather) + dot(low, gather)
            prefix[rows, :] += dot((scaled_wide * back_state).astype(BF16), gather)
            back = back_inside + back_state
            d_dt[rows, :] += dot((values * back).astype(BF16), gather)
            entered = (dy_wide * entering).astype(BF16)
            d_c[rows, :] += dot_nt(entered, before_low)
            d_b[rows, :] += dot_nt((scaled_wide * leaving).astype(BF16), d_low)
            kept = entering[Q - 1 : Q, :]
            through = jnp.sum(before * d_state, axis=0, keepdims=True) * kept
            high, low = in_two(jnp.broadcast_to(through, (8, BLK)))
            fixed[k * 8 : (k + 1) * 8, :] += dot(high, gather) + dot(low, gather)
            d_state = kept * d_state + dot(c_t[:, rows], entered)
            dact[rows, :] = back * step_size + skip * dy_wide

    @pl.when(step == STEPS)
    def _():
        for k in range(chunks):
            rows = slice(k * Q, (k + 1) * Q)
            own = seg_ref[PAD + k * Q : PAD + (k + 1) * Q, :]
            keep = (own == row_ref[0:1, rows]) & (iota((Q, Q), 1) <= iota((Q, Q), 0))
            d_score = jnp.where(keep, dscores[rows, :], 0.0)
            dact[rows, STATE:] = d_c[rows, :] + dot(d_score.astype(BF16), b_ref[rows, :])
            dact[rows, :STATE] = d_b[rows, :] + dot(d_score.T.astype(BF16), c_ref[rows, :])

    @pl.when(step <= STEPS)
    def _():
        sums = [jnp.zeros((1, BLK), F32) for _ in range(CONV + 1)]
        for k in range(chunks):
            rows = slice(k * Q, (k + 1) * Q)
            total = pre[rows, :]
            sig = sigmoid(total)
            d_conv = dact[rows, :] * (sig * (1.0 + total * (1.0 - sig)))
            dbuf[PAD + k * Q : PAD + (k + 1) * Q, :] = d_conv
            sums[4] = sums[4] + jnp.sum(d_conv, axis=0, keepdims=True)
            own = seg_ref[PAD + k * Q : PAD + (k + 1) * Q, :]
            for shift in range(CONV):
                at = PAD + k * Q - shift
                term = d_conv * ext[at : at + Q, :]
                if shift:
                    term = jnp.where(both(seg_ref[at : at + Q, :] == own), term, 0.0)
                sums[3 - shift] = sums[3 - shift] + jnp.sum(term, axis=0, keepdims=True)
        dtaps_ref[...] = jnp.concatenate(sums + [jnp.zeros((3, BLK), F32)], axis=0)

        def returned(at, rows):
            own = seg_ref[at : at + rows, :]
            result = taps_ref[3:4, :] * dbuf[at : at + rows, :]
            for shift in range(1, CONV):
                same = both(seg_ref[at + shift : at + shift + rows, :] == own)
                result = result + jnp.where(
                    same, taps_ref[3 - shift : 4 - shift, :] * dbuf[at + shift : at + shift + rows, :], 0.0
                )
            return result

        dhalo_ref[...] = returned(0, PAD)
        for k in range(chunks):
            dproj_ref[k * Q : (k + 1) * Q, :] = returned(PAD + k * Q, Q).astype(BF16)

    @pl.when(step == STEPS + 1)
    def _():
        lower = (iota((Q, Q), 1) < iota((Q, Q), 0)).astype(F32)
        upper = (iota((Q, Q), 1) >= iota((Q, Q), 0)).astype(F32)
        lane = iota((Q, 128), 1)
        rate = jnp.exp(heads_ref[1:2, :])
        bias_sum = jnp.zeros((1, 128), F32)
        decay_sum = jnp.zeros((1, 128), F32)
        for k in range(chunks):
            rows = slice(k * Q, (k + 1) * Q)
            d_log = jnp.dot(upper, suffix[rows, :], precision=HIGHEST, preferred_element_type=F32)
            d_log = d_log + jnp.dot(lower, prefix[rows, :], precision=HIGHEST, preferred_element_type=F32)
            d_log = d_log + fixed[k * 8 : k * 8 + 1, :]
            raw = jnp.where(lane < HEADS, dtraw_ref[rows, :128].astype(F32), 0.0) + heads_ref[0:1, :]
            d_raw = jnp.where(lane < HEADS, (d_dt[rows, :] - rate * d_log) * sigmoid(raw), 0.0)
            bias_sum = bias_sum + jnp.sum(d_raw, axis=0, keepdims=True)
            decay_sum = decay_sum - jnp.sum(d_log * dt_ref[rows, :] * rate, axis=0, keepdims=True)
            dproj_ref[rows, :] = jnp.concatenate([d_raw, jnp.zeros_like(d_raw)], axis=1).astype(BF16)
        dheads_ref[...] = jnp.concatenate([bias_sum, decay_sum, jnp.zeros((6, 128), F32)], axis=0)


def back(place, projected, halo, taps, heads, seg_lanes, seg_row, b_rows, c_rows, dt, running, dy, incoming, dstates, kept, given):
    length = projected.shape[0]
    count = dstates.shape[0]
    whole = lambda *shape: pl.BlockSpec(shape, lambda j: (0,) * len(shape))
    upto = lambda last, first=0: lambda j: (0, first + jnp.minimum(j, last))
    return pl.pallas_call(
        back_kernel,
        grid=(STEPS + 2,),
        in_specs=[
            pl.BlockSpec(memory_space=pltpu.SMEM),
            pl.BlockSpec((length, BLK), upto(STEPS, STEPS)),
            pl.BlockSpec((length, BLK), lambda j: (0, 2 * STEPS + 1)),
            pl.BlockSpec((PAD, BLK), upto(STEPS)),
            pl.BlockSpec((8, BLK), upto(STEPS)),
            whole(8, 128),
            whole(length + 2 * PAD, 128),
            whole(8, length),
            whole(length, 128),
            whole(length, 128),
            whole(length, 128),
            whole(length, 128),
            pl.BlockSpec((length, BLK), upto(STEPS - 1)),
            pl.BlockSpec((STATE, BLK), upto(STEPS - 1)),
            pl.BlockSpec((count, STATE, BLK), lambda j: (0, 0, jnp.minimum(j, STEPS - 1))),
            whole(count, 8, 128),
            pl.BlockSpec(memory_space=pl.ANY),
        ],
        out_specs=[
            pl.BlockSpec((length, BLK), lambda j: (0, STEPS + j)),
            pl.BlockSpec((PAD, BLK), upto(STEPS)),
            pl.BlockSpec((8, BLK), upto(STEPS)),
            whole(8, 128),
        ],
        out_shape=[
            jax.ShapeDtypeStruct((length, PROJ), BF16),
            jax.ShapeDtypeStruct((PAD, XBC), F32),
            jax.ShapeDtypeStruct((8, XBC), F32),
            jax.ShapeDtypeStruct((8, 128), F32),
        ],
        scratch_shapes=[
            pltpu.VMEM((length + PAD, BLK), F32),
            pltpu.VMEM((length, BLK), F32),
            pltpu.VMEM((length, BLK), F32),
            pltpu.VMEM((length + 2 * PAD, BLK), F32),
            pltpu.VMEM((length, Q), F32),
            pltpu.VMEM((length, Q), F32),
            pltpu.VMEM((length // Q, 128, Q), F32),
            pltpu.VMEM((128, length), BF16),
            pltpu.VMEM((128, length), BF16),
            pltpu.VMEM((length, 128), F32),
            pltpu.VMEM((length, 128), F32),
            pltpu.VMEM((length, 128), F32),
            pltpu.VMEM((length, 128), F32),
            pltpu.VMEM((length, 128), F32),
            pltpu.VMEM((length, 128), F32),
            pltpu.VMEM((length, 128), F32),
            pltpu.VMEM((8 * (length // Q), 128), F32),
            pltpu.VMEM((length // Q, STATE, BLK), F32),
        ],
        input_output_aliases={16: 0},
        compiler_params=pltpu.CompilerParams(vmem_limit_bytes=VMEM_LIMIT),
        cost_estimate=pl.CostEstimate(
            flops=12 * 10**9, bytes_accessed=30 * 10**6, transcendentals=2 * 10**7
        ),
        name="back",
    )(
        place, projected, projected, halo, taps, heads, seg_lanes, seg_row, b_rows, c_rows, dt, running, dy, incoming, dstates, kept, given
    )


def passed_along(block, axis, distance):
    devices = range(lax.axis_size(axis))
    route = [(i - distance, i) for i in devices if i - distance in devices]
    return lax.ppermute(block, axis, route)


def pack_small(conv_taps, conv_bias, dt_bias, decay_log, skip_scale, mixer_gain, input_gain):
    width = conv_bias.shape[0]

    def line(*parts):
        flat = jnp.concatenate(parts)
        return jnp.pad(flat, (0, width - flat.shape[0]))[None]

    return jnp.concatenate(
        [
            conv_taps.T,
            conv_bias[None],
            line(mixer_gain),
            line(input_gain),
            line(dt_bias, decay_log, skip_scale),
        ],
        axis=0,
    )


def unpack_small(whole):
    shards, _, width = whole.shape
    joined = jnp.swapaxes(whole, 0, 1)
    taps = jnp.pad(joined[:5].reshape(5, shards * width).astype(F32), ((0, 3), (0, 0)))
    gain = joined[5, :, : INNER // shards].reshape(1, INNER).astype(F32)
    input_gain = joined[6, :, : D // shards].reshape(1, D).astype(F32)
    own = HEADS // shards
    heads = joined[7, :, : 3 * own].reshape(shards, 3, own).swapaxes(0, 1).reshape(3, HEADS)
    heads = jnp.pad(heads.astype(F32), ((0, 5), (0, 128 - HEADS)))
    return taps, jnp.pad(gain, ((0, 7), (0, 0))), input_gain, heads


def on_device(
    inputs,
    segment_ids,
    out_grad,
    in_matrix,
    out_matrix,
    conv_taps,
    conv_bias,
    dt_bias,
    decay_log,
    skip_scale,
    mixer_gain,
    input_gain,
):
    shards, parts = lax.axis_size("fsdp"), lax.axis_size("ctx")
    place = jnp.reshape(lax.axis_index("ctx"), (1,)).astype(jnp.int32)
    units_low, cot = inputs[0], out_grad[0]
    units = units_low.astype(F32)
    seg_ids = segment_ids[0]
    length = units.shape[0]
    small = lax.all_gather(
        pack_small(conv_taps, conv_bias, dt_bias, decay_log, skip_scale, mixer_gain, input_gain), "fsdp"
    )
    w_whole = lax.all_gather(in_matrix, "fsdp", axis=0, tiled=True)
    out_whole = lax.all_gather(out_matrix, "fsdp", axis=0, tiled=True)
    taps, gain, g_float, heads = unpack_small(small)
    rim_seg = passed_along(seg_ids[length - CONV + 1 :], "ctx", 1)
    seg_ext = jnp.concatenate(
        [
            jnp.full((PAD - CONV + 1,), -1, jnp.int32),
            rim_seg,
            seg_ids,
            jnp.full((PAD,), -2, jnp.int32),
        ]
    )
    seg_lanes = jnp.broadcast_to(seg_ext[:, None], (length + 2 * PAD, 128))
    seg_row = jnp.broadcast_to(seg_ids[None], (8, length))

    inv_rms = lax.rsqrt(jnp.mean(units * units, axis=-1, keepdims=True) + epsilon)
    base_rows = units * inv_rms
    part_rows = (base_rows * g_float).astype(BF16)
    projected = dot(part_rows, w_whole).astype(BF16)
    rim_rows = passed_along(projected[length - CONV + 1 :, INNER : INNER + XBC], "ctx", 1)
    halo = jnp.pad(rim_rows, ((PAD - CONV + 1, 0), (0, 0))).astype(F32)

    xs, y_local, state, b_rows, c_rows, dt, running, entering, keep = front(
        projected, halo, taps, heads, seg_lanes, seg_row
    )
    kept = lax.all_gather(keep, "ctx")
    states = lax.all_gather(state, "ctx")
    mixer_low, dproj, dy, incoming, d_incoming, column_sums, block_out, stats = tail(
        place, y_local, xs, projected, states, kept, out_whole, c_rows, entering, heads, gain, cot, units_low
    )
    dstates = lax.all_gather(d_incoming, "ctx")
    d_out_matrix = lax.dot_general(mixer_low, cot, (((0,), (0,)), ((), ())), preferred_element_type=F32)
    dproj, d_halo, d_taps, d_heads = back(
        place, projected, halo, taps, heads, seg_lanes, seg_row, b_rows, c_rows, dt, running, dy, incoming, dstates, kept, dproj
    )
    returned = passed_along(d_halo.astype(BF16), "ctx", -1)
    last = lax.slice(dproj, (length - PAD, INNER), (length, INNER + XBC))
    last = (last.astype(F32) + returned.astype(F32)).astype(BF16)
    dproj = lax.dynamic_update_slice(dproj, last, (length - PAD, INNER))

    d_in_matrix = lax.dot_general(part_rows, dproj, (((0,), (0,)), ((), ())), preferred_element_type=F32)
    d_normed = dot_nt(dproj, w_whole)
    d_input_gain = jnp.sum(d_normed * base_rows, axis=0)
    d_base = d_normed * g_float
    d_units = inv_rms * (d_base - base_rows * jnp.mean(d_base * base_rows, axis=-1, keepdims=True))
    input_grad = (cot.astype(F32) + d_units).astype(BF16)

    def scattered(grad):
        return lax.psum_scatter(grad.astype(BF16), "fsdp", scatter_dimension=0, tiled=True)

    d_in = lax.psum(scattered(d_in_matrix), "ctx").astype(F32)
    d_out = lax.psum(scattered(d_out_matrix), "ctx").astype(F32)
    row = jnp.concatenate(
        [
            d_taps[:5].reshape(-1),
            column_sums[0],
            d_input_gain,
            d_heads[0, :HEADS],
            d_heads[1, :HEADS],
            jnp.sum(column_sums[1].reshape(HEADS, HDIM), axis=1),
            jnp.sum(stats[:2], axis=1),
        ]
    )
    row = jnp.pad(row, (0, -row.shape[0] % 1024)).reshape(-1, 128)
    row = lax.psum(row, ("fsdp", "ctx")).reshape(-1)
    me = lax.axis_index("fsdp")

    def own(flat):
        size = flat.shape[-1] // shards
        return lax.dynamic_slice_in_dim(flat, me * size, size, flat.ndim - 1)

    at = 5 * XBC
    taps_sum = row[:at].reshape(5, XBC)
    gain_sum = row[at : at + INNER]
    input_gain_sum = row[at + INNER : at + INNER + D]
    at = at + INNER + D
    head_sums = row[at : at + 3 * HEADS].reshape(3, HEADS)
    stat_sums = row[at + 3 * HEADS : at + 3 * HEADS + 2]
    rms_stats = jnp.sqrt(stat_sums / (length * shards * parts * D))
    return (
        block_out[None],
        input_grad[None],
        d_in,
        d_out,
        own(taps_sum[:4]).T,
        own(taps_sum[4]),
        own(head_sums[0]),
        own(head_sums[1]),
        own(head_sums[2]),
        own(gain_sum),
        own(input_gain_sum),
        rms_stats,
    )


def solution(mesh):
    return jax.shard_map(
        on_device,
        mesh=mesh,
        in_specs=(
            P("fsdp", "ctx", None),
            P("fsdp", "ctx"),
            P("fsdp", "ctx", None),
            P("fsdp", None),
            P("fsdp", None),
            P("fsdp", None),
            P("fsdp"),
            P("fsdp"),
            P("fsdp"),
            P("fsdp"),
            P("fsdp"),
            P("fsdp"),
        ),
        out_specs=(
            P("fsdp", "ctx", None),
            P("fsdp", "ctx", None),
            P("fsdp", None),
            P("fsdp", None),
            P("fsdp", None),
            P("fsdp"),
            P("fsdp"),
            P("fsdp"),
            P("fsdp"),
            P("fsdp"),
            P("fsdp"),
            P(),
        ),
        check_vma=False,
    )
```

time: 1660 us -> 1180 us (0.71); the launches traced: 1640 us -> 1180 us
  local copies, waits for them, and re-layouts: 345 us -> 47.1 us
  matrix products: 310 us -> 65.6 us
  waiting for transfers between devices: 606 us -> 842 us
  other arithmetic: 174 us -> 21.7 us
  Pallas kernels: 0 us -> 139 us
  blocking collectives: 135 us -> 39.5 us
  loops' own time: 34.9 us -> 0 us
    dot_general x37 -> x4, matrix products: 310 us -> 65.6 us  [the longest x1 21.9 us: dot_nt(): lax.dot_general(a, b, (((1,), (1,)), ((), ())), preferred_element_type=F32)]
    psum x1 -> x2, waiting for transfers between devices: 134 us -> 361 us  [the longest x1 239 us: on_device(): d_in = lax.psum(scattered(d_in_matrix), 'ctx').astype(F32)]
    dynamic_update_slice x10 -> x0, local copies, waits for them, and re-layouts: 142 us -> none  [scan_ssd(): lax.scan(jax.checkpoint(block_step), initial, sliced)]
    pallas_call x0 -> x3, Pallas kernels: none -> 139 us  [the longest x1 65.1 us: back(): pl.pallas_call(back_kernel, grid=(STEPS + 2,), in_specs=[pl.BlockSpec(mem...]
    psum x2 -> x0, blocking collectives: 81 us -> none  [the longest x1 44 us: on_device(): lax.psum((d_dtb, d_decay, d_skip, square_sums), ('fsdp', 'ctx'))]
    reshape x7 -> x2, local copies, waits for them, and re-layouts: 56.7 us -> 0.64 us  [the longest x1 0.63 us: on_device(): row = jnp.pad(row, (0, -row.shape[0] % 1024)).reshape(-1, 128)]
    reduce_sum x11 -> x2, other arithmetic: 46.6 us -> 1.06 us  [the longest x1 0.94 us: on_device(): jnp.sum(stats[:2], axis=1)]
    another operation x4 -> x0, loops' own time: 34.9 us -> none  [the longest x2 34.9 us: scan_ssd(): lax.scan(jax.checkpoint(block_step), initial, sliced)]
  transfers between devices with their start and end apart: 11 -> 11, of which waited for: 7 -> 9; matrix products, arithmetic and copies ran while one was open for 9% -> 7% of each run, Pallas kernels for 0% -> 3%
where the time goes in v1:
time: 1180 us
  waiting for transfers between devices  842 us (71%)
  Pallas kernels  139 us (12%)
  matrix products  65.6 us (6%)
  local copies, waits for them, and re-layouts  47.1 us (4%)
  blocking collectives  39.5 us (3%)
  other arithmetic  21.7 us (2%)
  between operations  14.5 us (1%)
    psum x1, waiting for transfers between devices, on_device(): d_in = lax.psum(scattered(d_in_matrix), 'ctx').astype(F32)  239 us
    psum x1, waiting for transfers between devices, on_device(): row = lax.psum(row, ('fsdp', 'ctx')).reshape(-1)  122 us
    all_gather x1, waiting for transfers between devices, on_device(): w_whole = lax.all_gather(in_matrix, 'fsdp', axis=0, tiled=True)  116 us
    unnamed x9, waiting for transfers between devices  110 us
    all_gather x1, waiting for transfers between devices, on_device(): dstates = lax.all_gather(d_incoming, 'ctx')  97.3 us
    all_gather x1, waiting for transfers between devices, on_device(): states = lax.all_gather(state, 'ctx')  77 us
    reduce_scatter x1, waiting for transfers between devices, scattered(): lax.psum_scatter(grad.astype(BF16), 'fsdp', scatter_dimension=0, tiled=True)  74.1 us
    pallas_call x1, Pallas kernels, back(): pl.pallas_call(back_kernel, grid=(STEPS + 2,), in_specs=[pl.BlockSpec(mem...  65.1 us
  transfers between devices with their start and end apart: 11, of which 9 were waited for; matrix products, arithmetic and copies ran while one was open for 7% of the time, Pallas kernels for 3%

profile of v1, /device:TPU:0, one launch (start us, length us, event | category | flops | bytes accessed | tf_op | source)
XLA Modules:
  0.0 1179.4 jit_solution(9417733646479303453)
XLA Ops:
  8.9 4.8 collective-permute-start.1
  14.0 5.2 all-gather
  21.3 116.0 %all-gather.9.cloned.1.call-done = bf16[1536,6448]{0,1:T(8,128)(2,1)} async-done(((bf16[384,6448]{0,1:T(8,128)(2,1)}), bf16[1536,6448]{0,1:T(8,128)(2,1)}) %all-gather.9.cloned.1.call-update) | async-done | bytes 19808272 | tf_op jit(solution)/shard_map/all_gather | solution.py:704
  137.3 16.7 %convolution_convert_fusion.2.x_ref.bc_ref.dtraw_ref.gate_ref = bf16[512,6448]{1,0:T(8,128)(2,1)} fusion(bf16[1536,6448]{0,1:T(8,128)(2,1)} %all-gather.9.cloned.1.call-done, f32[1536]{0:T(1024)S(1)} %reshape.103, f32[512]{0:T(512)S(1)} %add_rsqrt_fusion, bf16[1,512,1536]{2,1,0:T(8,128)(2,1)S(1)} %copy-done), kind=kOutput, calls=%fused_computation.2 | convolution fusion | flops 10148274176 | bytes 27992064 | tf_op jit(solution)/shard_map/dot_general | solution.py:32
  154.8 3.4 collective-permute-start
  158.3 1.4 collective-permute-done
  161.8 31.2 %front.1 = (bf16[512,3072]{1,0:T(8,128)(2,1)}, bf16[512,3072]{1,0:T(8,128)(2,1)}, bf16[128,3072]{1,0:T(8,128)(2,1)}, bf16[512,128]{1,0:T(8,128)(2,1)}, bf16[512,...) custom-call(bf16[512,6448]{1,0:T(8,128)(2,1)} %convolution_convert_fusi, ...), custom_call_target="tpu_custom_call" | custom-call | flops 6000000000 | bytes 16000000 | tf_op jit(solution)/shard_map/front/pallas_call | solution.py:178
  193.8 34.3 %all-gather.2 = f32[64,128]{1,0:T(8,128)} all-gather(f32[8,128]{1,0:T(8,128)} %get-tuple-element.36), channel_id=4, replica_groups=mesh['fsdp'=4,'ctx'=8] {'ctx'}, dimensions={0}, use_global_device_ids=true | all-gather | bytes 36864 | tf_op jit(solution)/shard_map/all_gather | solution.py:729
  228.0 77.0 %all-gather.13.cloned.1.call-done = bf16[1024,3072]{1,0:T(8,128)(2,1)} async-done(((bf16[128,3072]{1,0:T(8,128)(2,1)}), bf16[1024,3072]{1,0:T(8,128)(2,1)}) %all-gather.13.cloned.1.call-update) | async-done | bytes 6291472 | tf_op jit(solution)/shard_map/all_gather | solution.py:730
  305.0 42.9 %tail.1 = (bf16[512,3072]{1,0:T(8,128)(2,1)}, bf16[512,6448]{1,0:T(8,128)(2,1)}, bf16[512,3072]{1,0:T(8,128)(2,1)}, bf16[128,3072]{1,0:T(8,128)(2,1)}, bf16[128,...) custom-call(s32[1]{0:T(128)} %bitcast.place_ref, ...), custom_call_target="tpu_custom_call" | custom-call | flops 12000000000 | bytes 50000000 | tf_op jit(solution)/shard_map/tail/pallas_call | solution.py:353
  348.0 97.3 %all-gather.15.cloned.1.call-done = bf16[1024,3072]{1,0:T(8,128)(2,1)} async-done(((bf16[128,3072]{1,0:T(8,128)(2,1)}), bf16[1024,3072]{1,0:T(8,128)(2,1)}) %all-gather.15.cloned.1.call-update) | async-done | bytes 6291472 | tf_op jit(solution)/shard_map/all_gather | solution.py:734
  445.3 65.1 %back.1 = (bf16[512,6448]{1,0:T(8,128)(2,1)}, f32[8,3328]{1,0:T(8,128)}, f32[8,3328]{1,0:T(8,128)}, f32[8,128]{1,0:T(8,128)}) custom-call(s32[1]{0:T(128)} %bitcast.place_ref, bf16[512,6448]{1,0:T(8,128)(2,1)} %convolution_convert_fusion.2.x_ref.bc_ref.dtraw_ref.gate_ref, ...), custom_call_target="tpu_custom_call", output_to_operand_aliasing={{0}: (16, {})} | custom-call | flops 12000000000 | bytes 30000000 | tf_op jit(solution)/shard_map/back/pallas_call | solution.py:579
  510.4 0.9 convert_element_type.108
  511.3 1.5 collective-permute-start.2
  512.8 4.5 collective-permute-done.2
  517.3 1.4 fusion.15
  518.7 16.8 %convolution_convert_fusion = bf16[1536,6448]{0,1:T(8,128)(2,1)} fusion(bf16[512,6448]{1,0:T(8,128)(2,1)} %fusion.15, f32[1536]{0:T(1024)S(1)} %reshape.103, f32[512]{0:T(512)S(1)} %add_rsqrt_fusion, bf16[1,512,1536]{2,1,0:T(8,128)(2,1)S(1)} %copy-done.1), kind=kOutput, calls=%fused_computation | convolution fusion | flops 10154876928 | bytes 27992064 | tf_op jit(solution)/shard_map/dot_general | solution.py:744
  535.6 24.5 %copy.34 = bf16[1536,6448]{1,0:T(8,128)(2,1)} copy(bf16[1536,6448]{0,1:T(8,128)(2,1)} %convolution_convert_fusion) | data formatting | bytes 39616512
  560.1 1.3 copy-done.3
  561.5 10.2 convolution_convert_fusion.1
  571.7 1.0 slice_reduce_fusion.1
  573.0 0.9 slice_reduce_fusion
  574.7 21.9 %fusion.10 = (f32[1536]{0:T(1024)S(1)}, f32[512]{0:T(512)S(1)}, f32[512,1536]{1,0:T(8,128)}) fusion(f32[512]{0:T(512)S(1)} %add_rsqrt_fusion, bf16[1,512,1536]{2,1,0:T(8,128)(2,1)S(1)} %copy-done.1, f32[1536]{0:T(1024)S(1)} %reshape.103, bf16[512,6448]{1,0:T(8,128)(2,1)} %fusion.15, bf16[1536,6448]{0,1:T(8,128)(2,1)} %all-gather.9.cloned.1.call-done), kind=kOutput, calls=%fused_computation.15 | convolution fusion | flops 10147330048 | bytes 31145984 | tf_op jit(solution)/shard_map/dot_general | solution.py:36
  597.6 108.9 %reduce-scatter.7.cloned.1.call-done = bf16[384,6448]{1,0:T(8,128)(2,1)} async-done(((bf16[1536,6448]{1,0:T(8,128)(2,1)}), bf16[384,6448]{1,0:T(8,128)(2,1)}) %reduce-scatter.7.cloned.1.call-update) | async-done | bytes 4952080
  706.5 7.6 copy.35
  714.1 74.1 %reduce-scatter.5.cloned.1.call-done = bf16[768,1536]{1,0:T(8,128)(2,1)} async-done(((bf16[3072,1536]{1,0:T(8,128)(2,1)}), bf16[768,1536]{1,0:T(8,128)(2,1)}) %reduce-scatter.5.cloned.1.call-update) | async-done | bytes 2359312 | tf_op jit(solution)/shard_map/reduce_scatter | solution.py:752
  788.2 4.0 fusion.12
  792.2 122.0 %all-reduce.12.cloned.1.call-done = f32[168,128]{1,0:T(8,128)} async-done(((f32[168,128]{1,0:T(8,128)}), f32[168,128]{1,0:T(8,128)}) %all-reduce.12.cloned.1.call-update) | async-done | bytes 86032 | tf_op jit(solution)/shard_map/psum | solution.py:768
  922.4 1.3 fusion.21
  923.7 239.0 %all-reduce.14.cloned.1.call-done = (bf16[384,6448]{0,1:T(8,128)(2,1)}, bf16[768,1536]{1,0:T(8,128)(2,1)}) async-done(((bf16[384,6448]{0,1:T(8,128)(2,1)}, bf16[768,1536]{1,0:T(8,128)(2,1)}), (bf16[384,6448]{0,1:T(8,128)(2,1)}, bf16[768,1536]{1,0:T(8,128)(2,1)})) %all-reduce.14.cloned.1.call-update) | async-done | bytes 7311376 | tf_op jit(solution)/shard_map/psum | solution.py:754
  1162.7 7.1 convert_element_type.113
  1169.7 2.8 convert_element_type.115
  (95 shorter events, 18.0 us)
Async XLA Ops:
  7.2 1.6 copy-start.5
  7.2 6.5 copy-start.7
  7.2 6.6 copy-start.9
  7.2 6.6 copy-start.12
  7.2 6.6 copy-start.11
  7.2 6.6 copy-start.10
  7.2 6.7 copy-start.8
  7.3 6.7 copy-start.6
  7.3 13.0 %copy-start = (bf16[1,512,1536]{2,1,0:T(8,128)(2,1)S(1)}, bf16[1,512,1536]{2,1,0:T(8,128)(2,1)}, u32[]{:S(2)}) copy-start(bf16[1,512,1536]{2,1,0:T(8,128)(2,1)} %param.12) | copy-start | bytes 4718596
  7.3 130.0 %all-gather.9.cloned.1.call-start = ((), (), s32[]{:S(2)}) async-start(), calls=%async_computation.2 | async-start | bytes 24760320 | tf_op jit(solution)/shard_map/all_gather | solution.py:704
  8.0 220.0 %all-gather.11.cloned.1.call-start = ((), (), s32[]{:S(2)}) async-start(), calls=%async_computation.3 | async-start | bytes 11796480 | tf_op jit(solution)/shard_map/all_gather | solution.py:705
  8.8 296.2 %all-gather.13.cloned.1.call-start = ((), (), s32[]{:S(2)}) async-start(), calls=%async_computation.6 | async-start | bytes 7077888 | tf_op jit(solution)/shard_map/all_gather | solution.py:730
  8.9 149.3 %collective-permute-start.1 = (s32[3]{0:T(128)S(1)}, s32[3]{0:T(128)S(1)}, u32[]{:S(2)}, u32[]{:S(2)}) collective-permute-start(s32[3]{0:T(128)S(1)} %slice_bitcast_fusion.6), channel_id=1, source_target_pairs={{0,1},{1,2},{2,3},{3,4},{4,5},{5,6},{6,7},{8,9},{9,10},{10,11},{11... | collective-permute-start | bytes 44 | tf_op jit(solution)/shard_map/ppermute | solution.py:647
  154.8 4.9 collective-permute-start
  193.0 252.2 %all-gather.15.cloned.1.call-start = ((), (), s32[]{:S(2)}) async-start(), calls=%async_computation.7 | async-start | bytes 7077888 | tf_op jit(solution)/shard_map/all_gather | solution.py:734
  347.9 358.6 %reduce-scatter.7.cloned.1.call-start = ((), (), s32[]{:S(2)}) async-start(), calls=%async_computation.8 | async-start | bytes 25067520
  445.3 73.5 %copy-start.1 = (bf16[1,512,1536]{2,1,0:T(8,128)(2,1)S(1)}, bf16[1,512,1536]{2,1,0:T(8,128)(2,1)}, u32[]{:S(2)}) copy-start(bf16[1,512,1536]{2,1,0:T(8,128)(2,1)} %param.12) | copy-start | bytes 4718596
  511.3 6.0 collective-permute-start.2
  560.1 1.4 copy-start.3
  560.1 228.1 %reduce-scatter.5.cloned.1.call-start = ((), (), s32[]{:S(2)}) async-start(), calls=%async_computation.4 | async-start | bytes 11796480 | tf_op jit(solution)/shard_map/reduce_scatter | solution.py:752
  571.7 2.3 copy-start.4
  571.7 342.5 %all-reduce.12.cloned.1.call-start = ((), (), s32[]{:S(2)}) async-start(), calls=%async_computation.5 | async-start | bytes 172032 | tf_op jit(solution)/shard_map/psum | solution.py:768
  597.3 565.3 %all-reduce.14.cloned.1.call-start = ((), (), s32[]{:S(2)}) async-start(), calls=%async_computation.9 | async-start | bytes 14622720 | tf_op jit(solution)/shard_map/psum | solution.py:754
  1162.7 7.1 copy-start.2
Sparse Core Ops, SparseCore 0:
  9.7 127.5 all-gather.8
  138.9 64.2 all-gather.10
  205.9 99.0 all-gather.12
  348.0 97.1 all-gather.14
  560.2 146.2 reduce-scatter.6
  709.7 78.4 reduce-scatter.4
  794.7 119.4 all-reduce.11
  918.8 243.7 all-reduce.13

commit v2 on v1

--- a/solution.py
+++ b/solution.py
@@ -312,7 +312,7 @@
             silu = gate * sig
             unit = y * silu * norm
             low = (unit * gain).astype(BF16)
-            mixer_ref[rows, :] = low
+            mixer_ref[:, rows] = (unit * gain).T.astype(BF16)
             part = dot(low, out_ref[...])
 
             @pl.when(step == STEPS)
@@ -369,7 +369,7 @@
             whole(length, D),
         ],
         out_specs=[
-            late(length),
+            pl.BlockSpec((BLK, length), lambda i: (jnp.maximum(i - STEPS, 0), 0)),
             late(length),
             late(length),
             early(STATE),
@@ -379,7 +379,7 @@
             whole(8, D),
         ],
         out_shape=[
-            jax.ShapeDtypeStruct((length, INNER), BF16),
+            jax.ShapeDtypeStruct((INNER, length), BF16),
             jax.ShapeDtypeStruct((length, PROJ), BF16),
             jax.ShapeDtypeStruct((length, INNER), BF16),
             jax.ShapeDtypeStruct((STATE, INNER), BF16),
@@ -641,6 +641,239 @@
     )
 
 
+WIDE = 512
+OUT_CHUNKS = 2 * D // WIDE
+IN_CHUNKS = -(-PROJ // WIDE)
+CHUNKS = OUT_CHUNKS + IN_CHUNKS
+LAGS = 8
+SHARD = D // 4
+PIECE = SHARD // 8
+SMALL_ROWS = 168
+
+
+def flipped(index, bit):
+    return index + bit - 2 * bit * lax.rem(index // bit, 2)
+
+
+def reduce_kernel(
+    lhs_in, lhs_out, rhs_in, rhs_out, small_ref,
+    din_ref, dout_ref, total_ref,
+    own, core_send, core_recv, y_recv, x_recv, z_recv, w_recv, final, small_send, small_recv,
+    send_sems, recv_sems, small_send_sems, small_recv_sems,
+):
+    step = pl.program_id(0)
+    shard, part = lax.axis_index("fsdp"), lax.axis_index("ctx")
+    core, y = lax.rem(shard, 2), shard // 2
+    x, z = lax.rem(part, 2), part // 2
+    near, far = lax.rem(z, 2), z // 2
+    peers = (
+        {"fsdp": flipped(shard, 1)},
+        {"fsdp": flipped(shard, 2)},
+        {"ctx": flipped(part, 1)},
+        {"ctx": flipped(part, 2)},
+        {"ctx": flipped(part, 4)},
+    )
+
+    def sent(stage, k, source, target, peer):
+        return pltpu.make_async_remote_copy(
+            src_ref=source,
+            dst_ref=target,
+            send_sem=send_sems.at[stage, k],
+            recv_sem=recv_sems.at[stage, k],
+            device_id=peers[peer],
+            device_id_type=pl.DeviceIdType.MESH,
+        )
+
+    copies = (
+        lambda k: sent(0, k, core_send.at[lax.rem(k, 2)], core_recv.at[k], 0),
+        lambda k: sent(1, k, core_recv.at[k, 1 - y], y_recv.at[k], 1),
+        lambda k: sent(2, k, y_recv.at[k, 1 - x], x_recv.at[k], 2),
+        lambda k: sent(3, k, x_recv.at[k, 1 - near], z_recv.at[k], 3),
+        lambda k: sent(4, k, z_recv.at[k, 1 - far], w_recv.at[k], 4),
+        lambda k: sent(5, k, final.at[k, x, near, far], final.at[k, x, near, far], 4),
+        lambda k: sent(6, k, final.at[k, x, near], final.at[k, x, near], 3),
+        lambda k: sent(7, k, final.at[k, x], final.at[k, x], 2),
+    )
+    arrivals = copies[:5] + (
+        lambda k: sent(5, k, final.at[k, x, near, 1 - far], final.at[k, x, near, 1 - far], 4),
+        lambda k: sent(6, k, final.at[k, x, 1 - near], final.at[k, x, 1 - near], 3),
+        lambda k: sent(7, k, final.at[k, 1 - x], final.at[k, 1 - x], 2),
+    )
+
+    def small_copy(stage):
+        return pltpu.make_async_remote_copy(
+            src_ref=small_send.at[stage],
+            dst_ref=small_recv.at[stage],
+            send_sem=small_send_sems.at[stage],
+            recv_sem=small_recv_sems.at[stage],
+            device_id=peers[stage],
+            device_id_type=pl.DeviceIdType.MESH,
+        )
+
+    @pl.when(step == 0)
+    def _():
+        barrier = pltpu.get_barrier_semaphore()
+        for peer in peers:
+            pl.semaphore_signal(barrier, inc=1, device_id=peer, device_id_type=pl.DeviceIdType.MESH)
+        pl.semaphore_wait(barrier, len(peers))
+        small_send[0] = small_ref[...]
+        small_copy(0).start()
+
+    for stage in range(5):
+
+        @pl.when(step == stage + 1)
+        def _():
+            small_copy(stage).wait()
+            total = small_send[stage] + small_recv[stage]
+            if stage < 4:
+                small_send[stage + 1] = total
+                small_copy(stage + 1).start()
+            else:
+                total_ref[...] = total
+
+    def partial(lhs_of, rhs):
+        for row in range(2):
+            value = dot(lhs_of(2 * row + 1 - core), rhs).astype(BF16)
+            core_send[lax.rem(step, 2), row] = value.reshape(2, 2, 2, PIECE, WIDE)
+        copies[0](step).start()
+        for row in range(2):
+            own[row] = dot(lhs_of(2 * row + core), rhs).reshape(2, 2, 2, PIECE, WIDE)
+
+    @pl.when(step < OUT_CHUNKS)
+    def _():
+        partial(lambda s: lhs_out[s, step // (D // WIDE)], rhs_out[...])
+
+    @pl.when((step >= OUT_CHUNKS) & (step < CHUNKS))
+    def _():
+        rhs = rhs_in[...]
+        columns = iota(rhs.shape, 1) + (step - OUT_CHUNKS) * WIDE
+        partial(lambda s: lhs_in[s], jnp.where(columns < PROJ, rhs, jnp.zeros_like(rhs)))
+
+    @pl.when(step < CHUNKS)
+    def _():
+        arrivals[0](step).wait_recv()
+        for row in (1 - y, y):
+            core_recv[step, row] = (own[row] + core_recv[step, row].astype(F32)).astype(BF16)
+        copies[1](step).start()
+
+    def stage(lag):
+        def decorate(body):
+            k = step - lag
+
+            @pl.when((k >= 0) & (k < CHUNKS))
+            def _():
+                body(k)
+
+        return decorate
+
+    def summed(a, b):
+        return (a.astype(F32) + b.astype(F32)).astype(BF16)
+
+    @stage(1)
+    def _(k):
+        arrivals[1](k).wait_recv()
+        kept = core_recv.at[k, y]
+        y_recv[k] = summed(y_recv[k], kept[...])
+        copies[2](k).start()
+        copies[0](k).wait_send()
+
+    @stage(2)
+    def _(k):
+        arrivals[2](k).wait_recv()
+        x_recv[k] = summed(x_recv[k], y_recv[k, x])
+        copies[3](k).start()
+
+    @stage(3)
+    def _(k):
+        arrivals[3](k).wait_recv()
+        z_recv[k] = summed(z_recv[k], x_recv[k, near])
+        copies[4](k).start()
+
+    @stage(4)
+    def _(k):
+        arrivals[4](k).wait_recv()
+        final[k, x, near, far] = summed(w_recv[k], z_recv[k, far])
+        copies[5](k).start()
+
+    @stage(5)
+    def _(k):
+        arrivals[5](k).wait_recv()
+        copies[6](k).start()
+
+    @stage(6)
+    def _(k):
+        arrivals[6](k).wait_recv()
+        copies[7](k).start()
+
+    @stage(7)
+    def _(k):
+        arrivals[7](k).wait_recv()
+        for one in range(1, 8):
+            copies[one](k).wait_send()
+        whole = final[k].reshape(SHARD, WIDE).astype(F32)
+
+        @pl.when(k < OUT_CHUNKS)
+        def _():
+            dout_ref[...] = whole
+
+        @pl.when(k >= OUT_CHUNKS)
+        def _():
+            din_ref[...] = whole
+
+
+def reduce(part_t, mixer_t, dproj, cot, small):
+    length = cot.shape[0]
+    per_half = D // WIDE
+    whole = lambda *shape: pl.BlockSpec(shape, lambda t: (0,) * len(shape))
+
+    def out_block(t):
+        k = jnp.clip(t - LAGS + 1, 0, OUT_CHUNKS - 1)
+        return (k // per_half, lax.rem(k, per_half))
+
+    slots = lambda *shape: pltpu.VMEM((CHUNKS, *shape, PIECE, WIDE), BF16)
+    return pl.pallas_call(
+        reduce_kernel,
+        grid=(CHUNKS + LAGS - 1,),
+        in_specs=[
+            whole(4, SHARD, length),
+            whole(4, 2, SHARD, length),
+            pl.BlockSpec((length, WIDE), lambda t: (0, jnp.clip(t - OUT_CHUNKS, 0, IN_CHUNKS - 1))),
+            pl.BlockSpec((length, WIDE), lambda t: (0, lax.rem(jnp.minimum(t, OUT_CHUNKS - 1), per_half))),
+            whole(SMALL_ROWS, 128),
+        ],
+        out_specs=[
+            pl.BlockSpec((SHARD, WIDE), lambda t: (0, jnp.clip(t - LAGS + 1 - OUT_CHUNKS, 0, IN_CHUNKS - 1))),
+            pl.BlockSpec((SHARD, WIDE), out_block),
+            whole(SMALL_ROWS, 128),
+        ],
+        out_shape=[
+            jax.ShapeDtypeStruct((SHARD, PROJ), F32),
+            jax.ShapeDtypeStruct((2 * SHARD, D), F32),
+            jax.ShapeDtypeStruct((SMALL_ROWS, 128), F32),
+        ],
+        scratch_shapes=[
+            pltpu.VMEM((2, 2, 2, 2, PIECE, WIDE), F32),
+            pltpu.VMEM((2, 2, 2, 2, 2, PIECE, WIDE), BF16),
+            slots(2, 2, 2, 2),
+            slots(2, 2, 2),
+            slots(2, 2),
+            slots(2),
+            slots(),
+            slots(2, 2, 2),
+            pltpu.VMEM((5, SMALL_ROWS, 128), F32),
+            pltpu.VMEM((5, SMALL_ROWS, 128), F32),
+            pltpu.SemaphoreType.DMA((8, CHUNKS)),
+            pltpu.SemaphoreType.DMA((8, CHUNKS)),
+            pltpu.SemaphoreType.DMA((5,)),
+            pltpu.SemaphoreType.DMA((5,)),
+        ],
+        compiler_params=pltpu.CompilerParams(
+            vmem_limit_bytes=VMEM_LIMIT, collective_id=0, has_side_effects=True
+        ),
+        name="reduce",
+    )(part_t, mixer_t, dproj, cot, small)
+
+
 def passed_along(block, axis, distance):
     devices = range(lax.axis_size(axis))
     route = [(i - distance, i) for i in devices if i - distance in devices]
@@ -728,11 +961,10 @@
     )
     kept = lax.all_gather(keep, "ctx")
     states = lax.all_gather(state, "ctx")
-    mixer_low, dproj, dy, incoming, d_incoming, column_sums, block_out, stats = tail(
+    mixer_t, dproj, dy, incoming, d_incoming, column_sums, block_out, stats = tail(
         place, y_local, xs, projected, states, kept, out_whole, c_rows, entering, heads, gain, cot, units_low
     )
     dstates = lax.all_gather(d_incoming, "ctx")
-    d_out_matrix = lax.dot_general(mixer_low, cot, (((0,), (0,)), ((), ())), preferred_element_type=F32)
     dproj, d_halo, d_taps, d_heads = back(
         place, projected, halo, taps, heads, seg_lanes, seg_row, b_rows, c_rows, dt, running, dy, incoming, dstates, kept, dproj
     )
@@ -741,18 +973,12 @@
     last = (last.astype(F32) + returned.astype(F32)).astype(BF16)
     dproj = lax.dynamic_update_slice(dproj, last, (length - PAD, INNER))
 
-    d_in_matrix = lax.dot_general(part_rows, dproj, (((0,), (0,)), ((), ())), preferred_element_type=F32)
     d_normed = dot_nt(dproj, w_whole)
     d_input_gain = jnp.sum(d_normed * base_rows, axis=0)
     d_base = d_normed * g_float
     d_units = inv_rms * (d_base - base_rows * jnp.mean(d_base * base_rows, axis=-1, keepdims=True))
     input_grad = (cot.astype(F32) + d_units).astype(BF16)
 
-    def scattered(grad):
-        return lax.psum_scatter(grad.astype(BF16), "fsdp", scatter_dimension=0, tiled=True)
-
-    d_in = lax.psum(scattered(d_in_matrix), "ctx").astype(F32)
-    d_out = lax.psum(scattered(d_out_matrix), "ctx").astype(F32)
     row = jnp.concatenate(
         [
             d_taps[:5].reshape(-1),
@@ -764,8 +990,22 @@
             jnp.sum(stats[:2], axis=1),
         ]
     )
-    row = jnp.pad(row, (0, -row.shape[0] % 1024)).reshape(-1, 128)
-    row = lax.psum(row, ("fsdp", "ctx")).reshape(-1)
+    row = jnp.pad(row, (0, SMALL_ROWS * 128 - row.shape[0])).reshape(SMALL_ROWS, 128)
+    if (shards, parts) == (4, 8):
+        d_in, d_out, row = reduce(
+            part_rows.T.reshape(4, SHARD, length), mixer_t.reshape(4, 2, SHARD, length), dproj, cot, row
+        )
+    else:
+        d_in = jnp.dot(part_rows.T, dproj, preferred_element_type=F32)
+        d_out = jnp.dot(mixer_t, cot, preferred_element_type=F32)
+
+        def scattered(grad):
+            return lax.psum_scatter(grad.astype(BF16), "fsdp", scatter_dimension=0, tiled=True)
+
+        d_in = lax.psum(scattered(d_in), "ctx").astype(F32)
+        d_out = lax.psum(scattered(d_out), "ctx").astype(F32)
+        row = lax.psum(row, ("fsdp", "ctx"))
+    row = row.reshape(-1)
     me = lax.axis_index("fsdp")
 
     def own(flat):

time: 1180 us -> 783 us (0.66)
  waiting for transfers between devices: 842 us -> 295 us
  Pallas kernels: 139 us -> 349 us
  matrix products: 65.6 us -> 32.7 us
  local copies, waits for them, and re-layouts: 47.1 us -> 29.7 us
    psum x2 -> x0, waiting for transfers between devices: 361 us -> none  [the longest x1 239 us: on_device(): d_in = lax.psum(scattered(d_in_matrix), 'ctx').astype(F32)]
    pallas_call x0 -> x1, Pallas kernels: none -> 209 us  [reduce(): pl.pallas_call(reduce_kernel, grid=(CHUNKS + LAGS - 1,), in_specs=[whole(...]
    unnamed x9 -> x4, waiting for transfers between devices: 110 us -> 1.41 us
    reduce_scatter x1 -> x0, waiting for transfers between devices: 74.1 us -> none  [scattered(): lax.psum_scatter(grad.astype(BF16), 'fsdp', scatter_dimension=0, tiled=True)]
    dot_general x2 -> x0, matrix products: 27 us -> none  [the longest x1 16.8 us: on_device(): lax.dot_general(part_rows, dproj, (((0,), (0,)), ((), ())), preferred_ele...]
    unnamed x30, local copies, waits for them, and re-layouts: 33.5 us -> 13.6 us
  transfers between devices with their start and end apart: 11 -> 7, of which waited for: 9 -> 5; matrix products, arithmetic and copies ran while one was open for 7% -> 3% of each run, Pallas kernels for 3% -> 4%
where the time goes in v2:
time: 783 us; the launch traced here: 782 us
  Pallas kernels  349 us (45%)
  waiting for transfers between devices  295 us (38%)
  blocking collectives  38.8 us (5%)
  matrix products  32.7 us (4%)
  local copies, waits for them, and re-layouts  29.7 us (4%)
  between operations  14.1 us (2%)
  other arithmetic  13.1 us (2%)
  starting transfers between devices  9.86 us (1%)
    pallas_call x1, Pallas kernels, reduce(): pl.pallas_call(reduce_kernel, grid=(CHUNKS + LAGS - 1,), in_specs=[whole(...  209 us
    all_gather x1, waiting for transfers between devices, on_device(): w_whole = lax.all_gather(in_matrix, 'fsdp', axis=0, tiled=True)  116 us
    all_gather x1, waiting for transfers between devices, on_device(): dstates = lax.all_gather(d_incoming, 'ctx')  95.2 us
    all_gather x1, waiting for transfers between devices, on_device(): states = lax.all_gather(state, 'ctx')  77.6 us
    pallas_call x1, Pallas kernels, back(): pl.pallas_call(back_kernel, grid=(STEPS + 2,), in_specs=[pl.BlockSpec(mem...  65 us
    pallas_call x1, Pallas kernels, tail(): pl.pallas_call(tail_kernel, grid=(2 * STEPS,), in_specs=[pl.BlockSpec(mem...  43.9 us
    all_gather x1, blocking collectives, on_device(): kept = lax.all_gather(keep, 'ctx')  33.6 us
    pallas_call x1, Pallas kernels, front(): pl.pallas_call(front_kernel, grid=(STEPS,), in_specs=[columns(length, lam...  31.2 us
  transfers between devices with their start and end apart: 7, of which 5 were waited for; matrix products, arithmetic and copies ran while one was open for 3% of the time, Pallas kernels for 4%

profile of v2, /device:TPU:0, one launch (start us, length us, event | category | flops | bytes accessed | tf_op | source)
XLA Modules:
  0.0 782.0 jit_solution(2254096611101612081)
XLA Ops:
  8.9 4.8 collective-permute-start.1
  14.0 5.2 all-gather
  21.3 116.0 %all-gather.9.cloned.1.call-done = bf16[1536,6448]{0,1:T(8,128)(2,1)} async-done(((bf16[384,6448]{0,1:T(8,128)(2,1)}), bf16[1536,6448]{0,1:T(8,128)(2,1)}) %all-gather.9.cloned.1.call-update) | async-done | bytes 19808272 | tf_op jit(solution)/shard_map/all_gather | solution.py:937
  137.3 16.7 %convolution_convert_fusion.x_ref.bc_ref.dtraw_ref.gate_ref = bf16[512,6448]{1,0:T(8,128)(2,1)} fusion(bf16[1536,6448]{0,1:T(8,128)(2,1)} %all-gather.9.cloned.1.call-done, f32[1536]{0:T(1024)S(1)} %reshape.111, f32[512]{0:T(512)S(1)} %add_rsqrt_fusion, bf16[1,512,1536]{2,1,0:T(8,128)(2,1)S(1)} %copy-done), kind=kOutput, calls=%fused_computation | convolution fusion | flops 10148274176 | bytes 27992064 | tf_op jit(solution)/shard_map/dot_general | solution.py:32
  154.0 0.8 slice.113
  154.8 3.4 collective-permute-start
  158.3 1.4 collective-permute-done
  160.4 0.9 broadcast_in_dim.35.seg_ref
  161.8 31.2 %front.1 = (bf16[512,3072]{1,0:T(8,128)(2,1)}, bf16[512,3072]{1,0:T(8,128)(2,1)}, bf16[128,3072]{1,0:T(8,128)(2,1)}, bf16[512,128]{1,0:T(8,128)(2,1)}, bf16[512,...) custom-call(bf16[512,6448]{1,0:T(8,128)(2,1)} %convolution_convert_fusi, ...), custom_call_target="tpu_custom_call" | custom-call | flops 6000000000 | bytes 16000000 | tf_op jit(solution)/shard_map/front/pallas_call | solution.py:178
  193.8 33.6 %all-gather.2 = f32[64,128]{1,0:T(8,128)} all-gather(f32[8,128]{1,0:T(8,128)} %get-tuple-element.39), channel_id=4, replica_groups=mesh['fsdp'=4,'ctx'=8] {'ctx'}, dimensions={0}, use_global_device_ids=true | all-gather | bytes 36864 | tf_op jit(solution)/shard_map/all_gather | solution.py:962
  227.3 77.6 %all-gather.13.cloned.1.call-done = bf16[1024,3072]{1,0:T(8,128)(2,1)} async-done(((bf16[128,3072]{1,0:T(8,128)(2,1)}), bf16[1024,3072]{1,0:T(8,128)(2,1)}) %all-gather.13.cloned.1.call-update) | async-done | bytes 6291472 | tf_op jit(solution)/shard_map/all_gather | solution.py:963
  305.0 43.9 %tail.1 = (bf16[3072,512]{1,0:T(8,128)(2,1)}, bf16[512,6448]{1,0:T(8,128)(2,1)}, bf16[512,3072]{1,0:T(8,128)(2,1)}, bf16[128,3072]{1,0:T(8,128)(2,1)}, bf16[128,...) custom-call(s32[1]{0:T(128)} %bitcast.place_ref, ...), custom_call_target="tpu_custom_call" | custom-call | flops 12000000000 | bytes 50000000 | tf_op jit(solution)/shard_map/tail/pallas_call | solution.py:353
  348.9 1.0 slice_reduce_fusion.1
  350.1 0.9 slice_reduce_fusion
  351.1 95.2 %all-gather.15.cloned.1.call-done = bf16[1024,3072]{1,0:T(8,128)(2,1)} async-done(((bf16[128,3072]{1,0:T(8,128)(2,1)}), bf16[1024,3072]{1,0:T(8,128)(2,1)}) %all-gather.15.cloned.1.call-update) | async-done | bytes 6291472 | tf_op jit(solution)/shard_map/all_gather | solution.py:967
  446.3 65.0 %back.1 = (bf16[512,6448]{1,0:T(8,128)(2,1)}, f32[8,3328]{1,0:T(8,128)}, f32[8,3328]{1,0:T(8,128)}, f32[8,128]{1,0:T(8,128)}) custom-call(s32[1]{0:T(128)} %bitcast.place_ref, bf16[512,6448]{1,0:T(8,128)(2,1)} %convolution_convert_fusion.x_ref.bc_ref.dtraw_ref.gate_ref, ...), custom_call_target="tpu_custom_call", output_to_operand_aliasing={{0}: (16, {})} | custom-call | flops 12000000000 | bytes 30000000 | tf_op jit(solution)/shard_map/back/pallas_call | solution.py:579
  511.3 0.9 convert_element_type.96
  512.2 1.5 collective-permute-start.2
  513.7 0.8 slice_bitcast_fusion.4
  514.5 0.9 reshape.108
  515.4 2.8 collective-permute-done.2
  518.2 1.4 fusion.15.rhs_in
  519.7 16.0 %fusion.24 = f32[512,1536]{1,0:T(8,128)S(1)} fusion(bf16[512,6448]{1,0:T(8,128)(2,1)} %fusion.15.rhs_in, bf16[1536,6448]{0,1:T(8,128)(2,1)} %all-gather.9.cloned.1.call-done), kind=kOutput, calls=%fused_computation.49 | convolution fusion | flops 10141827072 | bytes 29556736 | tf_op jit(solution)/shard_map/dot_general | solution.py:36
  535.7 1.1 fusion.10
  538.0 1.6 copy.35
  539.6 209.1 %reduce.5 = (f32[384,6448]{1,0:T(8,128)}, f32[768,1536]{1,0:T(8,128)}, f32[168,128]{1,0:T(8,128)}) custom-call(bf16[4,384,512]{2,1,0:T(8,128)(2,1)} %bitcast.58, bf16[4,2,384,512]{3,2,1,0:T(8,128)(2,1)} %bitcast.59, bf16[512,6448]{1,0:T(8,128)(2,1)} %fusion.15.rhs_in, bf16[512,1536]{1,0:T(8,128)(2,1)} %bitcast.57, f32[168,128]{1,0:T(8,128)} %pad_bitcast_fusion.small_ref), custom_call_target="tpu_custom_call" | custom-call | tf_op jit(solution)/shard_map/reduce/pallas_call | solution.py:834
  748.8 0.8 slice.101
  751.7 0.9 fusion.23
  752.6 1.3 fusion.21
  753.8 10.8 %copy.33 = f32[384,6448]{0,1:T(8,128)} copy(f32[384,6448]{1,0:T(8,128)} %get-tuple-element.74) | data formatting | bytes 19808256
  767.8 4.2 fusion.12
  773.3 2.2 copy.42
  (82 shorter events, 13.9 us)
Async XLA Ops:
  7.2 1.6 copy-start.5
  7.2 6.5 copy-start.7
  7.2 6.6 copy-start.9
  7.2 6.6 copy-start.12
  7.2 6.6 copy-start.11
  7.2 6.6 copy-start.10
  7.2 6.7 copy-start.8
  7.3 6.7 copy-start.6
  7.3 13.0 %copy-start = (bf16[1,512,1536]{2,1,0:T(8,128)(2,1)S(1)}, bf16[1,512,1536]{2,1,0:T(8,128)(2,1)}, u32[]{:S(2)}) copy-start(bf16[1,512,1536]{2,1,0:T(8,128)(2,1)} %param.12) | copy-start | bytes 4718596
  7.3 130.0 %all-gather.9.cloned.1.call-start = ((), (), s32[]{:S(2)}) async-start(), calls=%async_computation | async-start | bytes 24760320 | tf_op jit(solution)/shard_map/all_gather | solution.py:937
  8.0 219.3 %all-gather.11.cloned.1.call-start = ((), (), s32[]{:S(2)}) async-start(), calls=%async_computation.1 | async-start | bytes 11796480 | tf_op jit(solution)/shard_map/all_gather | solution.py:938
  8.8 296.2 %all-gather.13.cloned.1.call-start = ((), (), s32[]{:S(2)}) async-start(), calls=%async_computation.2 | async-start | bytes 7077888 | tf_op jit(solution)/shard_map/all_gather | solution.py:963
  8.9 149.3 %collective-permute-start.1 = (s32[3]{0:T(128)S(1)}, s32[3]{0:T(128)S(1)}, u32[]{:S(2)}, u32[]{:S(2)}) collective-permute-start(s32[3]{0:T(128)S(1)} %slice_bitcast_fusion.6), channel_id=1, source_target_pairs={{0,1},{1,2},{2,3},{3,4},{4,5},{5,6},{6,7},{8,9},{9,10},{10,11},{11... | collective-permute-start | bytes 44 | tf_op jit(solution)/shard_map/ppermute | solution.py:880
  154.8 4.9 collective-permute-start
  193.0 253.3 %all-gather.15.cloned.1.call-start = ((), (), s32[]{:S(2)}) async-start(), calls=%async_computation.3 | async-start | bytes 7077888 | tf_op jit(solution)/shard_map/all_gather | solution.py:967
  512.2 6.0 collective-permute-start.2
  519.7 16.0 %copy-start.1 = (bf16[1,512,1536]{2,1,0:T(8,128)(2,1)S(1)}, bf16[1,512,1536]{2,1,0:T(8,128)(2,1)}, u32[]{:S(2)}) copy-start(bf16[1,512,1536]{2,1,0:T(8,128)(2,1)} %param.12) | copy-start | bytes 4718596
  535.7 1.7 copy-start.2
  753.8 13.9 %copy-start.3 = (bf16[1,512,1536]{2,1,0:T(8,128)(2,1)S(1)}, bf16[1,512,1536]{2,1,0:T(8,128)(2,1)}, u32[]{:S(2)}) copy-start(bf16[1,512,1536]{2,1,0:T(8,128)(2,1)} %param.14) | copy-start | bytes 4718596
  767.8 5.6 copy-start.4
Sparse Core Ops, SparseCore 0:
  9.7 127.5 all-gather.8
  138.9 64.2 all-gather.10
  205.9 99.0 all-gather.12
  349.0 97.2 all-gather.14

commit v3 on v2

--- a/solution.py
+++ b/solution.py
@@ -26,6 +26,14 @@
 F32, BF16 = jnp.float32, jnp.bfloat16
 HIGHEST = lax.Precision.HIGHEST
 VMEM_LIMIT = 60 * 1024 * 1024
+
+
+def communicating(number, exchanging):
+    if not exchanging:
+        return pltpu.CompilerParams(vmem_limit_bytes=VMEM_LIMIT)
+    return pltpu.CompilerParams(
+        vmem_limit_bytes=VMEM_LIMIT, collective_id=number, has_side_effects=True
+    )
 
 
 def dot(a, b):
@@ -100,14 +108,105 @@
     return jnp.where(keep, dot_nt(c_rows, b_rows), 0.0)
 
 
+PARTS = 8
+SLAB = STATE // PARTS
+JOIN, DONE = 2, 4
+
+
+class Exchange:
+    def __init__(self, held, gathered, joined, incoming, sems):
+        self.held, self.gathered, self.joined, self.incoming, self.sems = held, gathered, joined, incoming, sems
+        self.me = lax.axis_index("ctx")
+
+    def others(self):
+        return [lax.rem(self.me + hop, PARTS) for hop in range(1, PARTS)]
+
+    def greet(self):
+        barrier = pltpu.get_barrier_semaphore()
+        for other in self.others():
+            pl.semaphore_signal(
+                barrier, inc=1, device_id={"ctx": other}, device_id_type=pl.DeviceIdType.MESH
+            )
+        pl.semaphore_wait(barrier, PARTS - 1)
+
+    def copy(self, source, target, kind, group, other):
+        return pltpu.make_async_remote_copy(
+            src_ref=source,
+            dst_ref=target,
+            send_sem=self.sems.at[2 * kind, group],
+            recv_sem=self.sems.at[2 * kind + 1, group],
+            device_id={"ctx": other},
+            device_id_type=pl.DeviceIdType.MESH,
+        )
+
+    def all_of(self, kind, group):
+        source, target = ((self.held, self.gathered), (self.joined, self.incoming))[kind]
+        some = pl.ds(0, PARTS - 1)
+        return self.copy(source.at[group, some], target.at[group, some], kind, group, self.others()[0])
+
+    def spread(self, group, state):
+        self.held[group] = state.astype(BF16).reshape(PARTS, SLAB, BLK)
+        self.gathered[group, self.me] = self.held[group, self.me]
+        for other in self.others():
+            self.copy(self.held.at[group, other], self.gathered.at[group, self.me], 0, group, other).start()
+
+    def join(self, group, kept, forward):
+        self.all_of(0, group).wait_recv()
+        total = jnp.zeros((SLAB, BLK), F32)
+        for part in range(PARTS) if forward else range(PARTS - 1, -1, -1):
+            self.joined[group, part] = total.astype(BF16)
+            total = kept[part : part + 1, :] * total + self.gathered[group, part].astype(F32)
+        self.incoming[group, self.me] = self.joined[group, self.me]
+        for other in self.others():
+            self.copy(self.joined.at[group, other], self.incoming.at[group, self.me], 1, group, other).start()
+
+    def finish(self, group):
+        self.all_of(1, group).wait_recv()
+        self.all_of(0, group).wait_send()
+        self.all_of(1, group).wait_send()
+        return self.incoming[group].reshape(STATE, BLK)
+
+
+def exchange_scratch():
+    return [pltpu.VMEM((STEPS, PARTS, SLAB, BLK), BF16) for _ in range(4)] + [pltpu.SemaphoreType.DMA((4, STEPS))]
+
+
+def first_rows(kept_ref):
+    return jnp.concatenate([kept_ref[part, 0:1, :] for part in range(PARTS)], axis=0)
+
+
+def joined_plainly(states, kept, place, forward):
+    factors = jnp.repeat(kept[:, 0, :HEADS], HDIM, axis=1)[:, None, :]
+    total = jnp.zeros(states.shape[1:], F32)
+    result = total
+    count = states.shape[0]
+    for part in range(count) if forward else range(count - 1, -1, -1):
+        result = jnp.where(place == part, total, result)
+        total = factors[part] * total + states[part].astype(F32)
+    return result.astype(BF16)
+
+
 def front_kernel(
     x_ref, bc_ref, dtraw_ref, halo_ref, halo_bc_ref, taps_ref, taps_bc_ref, heads_ref, seg_ref, row_ref,
     xs_ref, y_ref, state_ref, b_ref, c_ref, dt_ref, run_ref, in_ref, keep_ref,
-    ext, scores, run_t, b_t, enter, leave,
+    ext, scores, run_t, b_t, enter, leave, *parts,
 ):
     step = pl.program_id(0)
     length = x_ref.shape[0]
     chunks = length // Q
+    if parts:
+        exchange = Exchange(*parts[:5])
+        own_keep, keeps, keep_sends, keep_arrivals = parts[5:]
+
+        def keep_copy(hop):
+            return pltpu.make_async_remote_copy(
+                src_ref=own_keep,
+                dst_ref=keeps.at[exchange.me],
+                send_sem=keep_sends.at[hop],
+                recv_sem=keep_arrivals.at[hop],
+                device_id={"ctx": lax.rem(exchange.me + hop + 1, PARTS)},
+                device_id_type=pl.DeviceIdType.MESH,
+            )
 
     @pl.when(step == 0)
     def _():
@@ -140,8 +239,50 @@
             whole = jnp.exp(running + offset) * same
             in_ref[rows, :] = whole
             offset = offset + running[Q - 1 : Q, :]
-        keep_ref[...] = jnp.broadcast_to(whole[Q - 1 : Q, :], (8, 128))
-
+        keep = jnp.broadcast_to(whole[Q - 1 : Q, :], (8, 128))
+        if parts:
+            own_keep[...] = keep
+            keeps[exchange.me] = keep
+            exchange.greet()
+            for hop in range(PARTS - 1):
+                keep_copy(hop).start()
+        else:
+            keep_ref[0] = keep
+
+    @pl.when(step < STEPS)
+    def _():
+        state = local_scan(
+            step, x_ref, halo_ref, taps_ref, seg_ref, xs_ref, y_ref, c_ref, dt_ref, run_ref,
+            ext, scores, run_t, b_t, enter, leave,
+        )
+        if parts:
+            exchange.spread(step, state)
+        else:
+            state_ref[...] = state.astype(BF16)
+
+    if parts:
+
+        @pl.when(step == JOIN)
+        def _():
+            for hop in range(PARTS - 1):
+                keep_copy(hop).wait()
+            keep_ref[...] = keeps[...]
+
+        @pl.when((step >= JOIN) & (step < STEPS + JOIN))
+        def _():
+            group = step - JOIN
+            exchange.join(group, widen(first_rows(keeps), chosen(group)), True)
+
+        @pl.when(step >= DONE)
+        def _():
+            state_ref[...] = exchange.finish(step - DONE)
+
+
+def local_scan(
+    step, x_ref, halo_ref, taps_ref, seg_ref, xs_ref, y_ref, c_ref, dt_ref, run_ref,
+    ext, scores, run_t, b_t, enter, leave,
+):
+    chunks = x_ref.shape[0] // Q
     ext[0:PAD, :] = halo_ref[...]
     ext[PAD:, :] = x_ref[...].astype(F32)
     select = chosen(step)
@@ -168,38 +309,40 @@
         y_ref[rows, :] = (inside + entering * dot(c_ref[rows, :], state.astype(BF16))).astype(BF16)
         weighted = (scaled.astype(F32) * widen(leave[rows, :], select)).astype(BF16)
         state = entering[Q - 1 : Q, :] * state + dot(b_t[:, rows], weighted)
-    state_ref[...] = state.astype(BF16)
-
-
-def front(projected, halo, taps, heads, seg_lanes, seg_row):
+    return state
+
+
+def front(projected, halo, taps, heads, seg_lanes, seg_row, exchanging):
     length = projected.shape[0]
+    last = STEPS - 1
+    keeps = PARTS if exchanging else 1
     whole = lambda *shape: pl.BlockSpec(shape, lambda j: (0,) * len(shape))
     columns = lambda rows, at: pl.BlockSpec((rows, BLK), at)
     return pl.pallas_call(
         front_kernel,
-        grid=(STEPS,),
+        grid=(STEPS + DONE * exchanging,),
         in_specs=[
-            columns(length, lambda j: (0, STEPS + j)),
+            columns(length, lambda j: (0, STEPS + jnp.minimum(j, last))),
             columns(length, lambda j: (0, 2 * STEPS)),
             columns(length, lambda j: (0, 2 * STEPS + 1)),
-            columns(PAD, lambda j: (0, j)),
+            columns(PAD, lambda j: (0, jnp.minimum(j, last))),
             columns(PAD, lambda j: (0, STEPS)),
-            columns(8, lambda j: (0, j)),
+            columns(8, lambda j: (0, jnp.minimum(j, last))),
             columns(8, lambda j: (0, STEPS)),
             whole(8, 128),
             whole(length + 2 * PAD, 128),
             whole(8, length),
         ],
         out_specs=[
-            columns(length, lambda j: (0, j)),
-            columns(length, lambda j: (0, j)),
-            columns(STATE, lambda j: (0, j)),
+            columns(length, lambda j: (0, jnp.minimum(j, last))),
+            columns(length, lambda j: (0, jnp.minimum(j, last))),
+            columns(STATE, lambda j: (0, jnp.maximum(j - DONE * exchanging, 0))),
             whole(length, 128),
             whole(length, 128),
             whole(length, 128),
             whole(length, 128),
             whole(length, 128),
-            whole(8, 128),
+            whole(keeps, 8, 128),
         ],
         out_shape=[
             jax.ShapeDtypeStruct((length, INNER), BF16),
@@ -210,7 +353,7 @@
             jax.ShapeDtypeStruct((length, 128), F32),
             jax.ShapeDtypeStruct((length, 128), F32),
             jax.ShapeDtypeStruct((length, 128), F32),
-            jax.ShapeDtypeStruct((8, 128), F32),
+            jax.ShapeDtypeStruct((keeps, 8, 128), F32),
         ],
         scratch_shapes=[
             pltpu.VMEM((length + PAD, BLK), F32),
@@ -219,8 +362,18 @@
             pltpu.VMEM((128, length), BF16),
             pltpu.VMEM((length, 128), F32),
             pltpu.VMEM((length, 128), F32),
-        ],
-        compiler_params=pltpu.CompilerParams(vmem_limit_bytes=VMEM_LIMIT),
+        ]
+        + (
+            exchange_scratch()
+            + [
+                pltpu.VMEM((8, 128), F32),
+                pltpu.VMEM((PARTS, 8, 128), F32),
+                pltpu.SemaphoreType.DMA((PARTS - 1,)),
+                pltpu.SemaphoreType.DMA((PARTS - 1,)),
+            ]
+        )
+        * exchanging,
+        compiler_params=communicating(1, exchanging),
         cost_estimate=pl.CostEstimate(
             flops=6 * 10**9, bytes_accessed=16 * 10**6, transcendentals=10**7
         ),
@@ -228,38 +381,22 @@
     )(projected, projected, projected, halo, halo, taps, taps, heads, seg_lanes, seg_row)
 
 
-def weights_of_parts(kept_ref, place, before):
-    count = kept_ref.shape[0]
-    result = [None] * count
-    run = jnp.ones((1, 128), F32)
-    for part in range(count - 1, -1, -1) if before else range(count):
-        inside = (part < place) if before else (part > place)
-        result[part] = jnp.where(inside, run, 0.0)
-        run = run * jnp.where(inside, kept_ref[part, 0:1, :], 1.0)
-    return result
-
-
-def joined_states(states_ref, kept_ref, place, select, before):
-    weights = weights_of_parts(kept_ref, place, before)
-    count = len(weights)
-    stacked = jnp.concatenate(weights + [jnp.zeros((-count % 8, 128), F32)] * (count % 8 > 0), axis=0)
-    wide = widen(stacked, select)
-    total = jnp.zeros((STATE, BLK), F32)
-    for part in range(count):
-        total = total + wide[part : part + 1, :] * states_ref[part].astype(F32)
-    return total
-
-
 def tail_kernel(
-    place_ref, y_ref, xs_ref, gate_ref, states_ref, kept_ref, out_ref, c_ref, in_ref, heads_ref, gain_ref, g_ref, units_ref,
-    mixer_ref, dproj_ref, dy_ref, sin_ref, dsin_ref, sums_ref, block_ref, stats_ref,
-    full, dmix, squares, products, mixed, c_t,
+    y_ref, xs_ref, gate_ref, incoming_ref, kept_ref, out_ref, c_ref, in_ref, heads_ref, gain_ref, g_ref, units_ref,
+    mixer_ref, dproj_ref, dy_ref, dsin_ref, sums_ref, block_ref, stats_ref,
+    full, dmix, squares, products, mixed, c_t, *parts,
 ):
     step = pl.program_id(0)
     length = y_ref.shape[0]
-    group = lax.rem(step, STEPS)
+    group = jnp.where(step < STEPS, step, jnp.minimum(step - STEPS, STEPS - 1))
     select = chosen(group)
     half = length // 2
+    if parts:
+        exchange = Exchange(*parts)
+
+        @pl.when(step == 0)
+        def _():
+            exchange.greet()
 
     @pl.when(step == 0)
     def _():
@@ -271,8 +408,7 @@
 
     @pl.when(step < STEPS)
     def _():
-        incoming = joined_states(states_ref, kept_ref, place_ref[0], select, True).astype(BF16)
-        sin_ref[...] = incoming
+        incoming = incoming_ref[...]
         skip = widen(heads_ref[...], select)[2:3, :]
         for k in range(2):
             rows = slice(k * half, (k + 1) * half)
@@ -296,7 +432,7 @@
         squares[...] = jnp.broadcast_to(norm, squares.shape)
         products[...] = jnp.broadcast_to(mean, products.shape)
 
-    @pl.when(step >= STEPS)
+    @pl.when((step >= STEPS) & (step < 2 * STEPS))
     def _():
         gain = gain_ref[0:1, :]
         d_gain = jnp.zeros((1, BLK), F32)
@@ -331,7 +467,10 @@
             dy = dy.astype(F32)
             d_skip = d_skip + jnp.sum(dy * xs_ref[rows, :].astype(F32), axis=0, keepdims=True)
             d_state = d_state + dot(c_t[:, rows], (dy * widen(in_ref[rows, :], select)).astype(BF16))
-        dsin_ref[...] = d_state.astype(BF16)
+        if parts:
+            exchange.spread(group, d_state)
+        else:
+            dsin_ref[...] = d_state.astype(BF16)
         sums_ref[...] = jnp.concatenate([d_gain, d_skip, jnp.zeros((6, BLK), F32)], axis=0)
 
     @pl.when(step == 2 * STEPS - 1)
@@ -342,25 +481,37 @@
         second = jnp.sum(mixed[...] * mixed[...], axis=0, keepdims=True)
         stats_ref[...] = jnp.concatenate([first, second, jnp.zeros((6, D), F32)], axis=0)
 
-
-def tail(place, y, xs, projected, states, kept, out_whole, c_rows, entering, heads, gain, cot, units):
+    if parts:
+        at = step - STEPS
+
+        @pl.when((at >= JOIN) & (at < STEPS + JOIN))
+        def _():
+            done = at - JOIN
+            exchange.join(done, widen(first_rows(kept_ref), chosen(done)), False)
+
+        @pl.when(at >= DONE)
+        def _():
+            dsin_ref[...] = exchange.finish(at - DONE)
+
+
+def tail(y, xs, projected, incoming, kept, out_whole, c_rows, entering, heads, gain, cot, units, exchanging):
     length = y.shape[0]
-    count = states.shape[0]
+    group = lambda i: jnp.where(i < STEPS, i, jnp.minimum(i - STEPS, STEPS - 1))
+    second = lambda i: jnp.clip(i - STEPS, 0, STEPS - 1)
     early = lambda rows: pl.BlockSpec((rows, BLK), lambda i: (0, jnp.minimum(i, STEPS - 1)))
-    late = lambda rows: pl.BlockSpec((rows, BLK), lambda i: (0, jnp.maximum(i - STEPS, 0)))
-    each = lambda rows: pl.BlockSpec((rows, BLK), lambda i: (0, lax.rem(i, STEPS)))
+    late = lambda rows: pl.BlockSpec((rows, BLK), lambda i: (0, second(i)))
+    each = lambda rows: pl.BlockSpec((rows, BLK), lambda i: (0, group(i)))
     whole = lambda *shape: pl.BlockSpec(shape, lambda i: (0,) * len(shape))
     return pl.pallas_call(
         tail_kernel,
-        grid=(2 * STEPS,),
+        grid=(2 * STEPS + DONE * exchanging,),
         in_specs=[
-            pl.BlockSpec(memory_space=pltpu.SMEM),
             early(length),
             each(length),
             each(length),
-            pl.BlockSpec((count, STATE, BLK), lambda i: (0, 0, jnp.minimum(i, STEPS - 1))),
-            whole(count, 8, 128),
-            pl.BlockSpec((BLK, D), lambda i: (lax.rem(i, STEPS), 0)),
+            early(STATE),
+            whole(*kept.shape),
+            pl.BlockSpec((BLK, D), lambda i: (group(i), 0)),
             whole(length, 128),
             whole(length, 128),
             whole(8, 128),
@@ -369,11 +520,10 @@
             whole(length, D),
         ],
         out_specs=[
-            pl.BlockSpec((BLK, length), lambda i: (jnp.maximum(i - STEPS, 0), 0)),
+            pl.BlockSpec((BLK, length), lambda i: (second(i), 0)),
             late(length),
             late(length),
-            early(STATE),
-            late(STATE),
+            pl.BlockSpec((STATE, BLK), lambda i: (0, second(i - DONE * exchanging))),
             late(8),
             whole(length, D),
             whole(8, D),
@@ -382,7 +532,6 @@
             jax.ShapeDtypeStruct((INNER, length), BF16),
             jax.ShapeDtypeStruct((length, PROJ), BF16),
             jax.ShapeDtypeStruct((length, INNER), BF16),
-            jax.ShapeDtypeStruct((STATE, INNER), BF16),
             jax.ShapeDtypeStruct((STATE, INNER), BF16),
             jax.ShapeDtypeStruct((8, INNER), F32),
             jax.ShapeDtypeStruct((length, D), BF16),
@@ -395,18 +544,19 @@
             pltpu.VMEM((length, 128), F32),
             pltpu.VMEM((length, D), F32),
             pltpu.VMEM((128, length), BF16),
-        ],
-        compiler_params=pltpu.CompilerParams(vmem_limit_bytes=VMEM_LIMIT),
+        ]
+        + exchange_scratch() * exchanging,
+        compiler_params=communicating(2, exchanging),
         cost_estimate=pl.CostEstimate(
             flops=12 * 10**9, bytes_accessed=50 * 10**6, transcendentals=4 * 10**6
         ),
         name="tail",
-    )(place, y, xs, projected, states, kept, out_whole, c_rows, entering, heads, gain, cot, units)
+    )(y, xs, projected, incoming, kept, out_whole, c_rows, entering, heads, gain, cot, units)
 
 
 def back_kernel(
-    place_ref, x_ref, dtraw_ref, halo_ref, taps_ref, heads_ref, seg_ref, row_ref, b_ref, c_ref, dt_ref, run_ref,
-    dy_ref, sin_ref, dstates_ref, kept_ref, given_ref,
+    x_ref, dtraw_ref, halo_ref, taps_ref, heads_ref, seg_ref, row_ref, b_ref, c_ref, dt_ref, run_ref,
+    dy_ref, sin_ref, dout_ref, given_ref,
     dproj_ref, dhalo_ref, dtaps_ref, dheads_ref,
     ext, pre, dact, dbuf, scores, dscores, run_t, b_t, c_t, enter, leave, d_b, d_c, suffix, prefix, d_dt, fixed, states,
 ):
@@ -454,7 +604,7 @@
                 weighted = (scaled.astype(BF16).astype(F32) * widen(leave[rows, :], select)).astype(BF16)
                 last = widen(enter[rows.stop - 8 : rows.stop, :], select)[7:8, :]
                 state = last * state + dot(b_t[:, rows], weighted)
-        d_state = joined_states(dstates_ref, kept_ref, place_ref[0], select, False)
+        d_state = dout_ref[...].astype(F32)
         for k in range(chunks - 1, -1, -1):
             rows = slice(k * Q, (k + 1) * Q)
             total = pre[rows, :]
@@ -571,16 +721,14 @@
         dheads_ref[...] = jnp.concatenate([bias_sum, decay_sum, jnp.zeros((6, 128), F32)], axis=0)
 
 
-def back(place, projected, halo, taps, heads, seg_lanes, seg_row, b_rows, c_rows, dt, running, dy, incoming, dstates, kept, given):
+def back(projected, halo, taps, heads, seg_lanes, seg_row, b_rows, c_rows, dt, running, dy, incoming, outgoing, given):
     length = projected.shape[0]
-    count = dstates.shape[0]
     whole = lambda *shape: pl.BlockSpec(shape, lambda j: (0,) * len(shape))
     upto = lambda last, first=0: lambda j: (0, first + jnp.minimum(j, last))
     return pl.pallas_call(
         back_kernel,
         grid=(STEPS + 2,),
         in_specs=[
-            pl.BlockSpec(memory_space=pltpu.SMEM),
             pl.BlockSpec((length, BLK), upto(STEPS, STEPS)),
             pl.BlockSpec((length, BLK), lambda j: (0, 2 * STEPS + 1)),
             pl.BlockSpec((PAD, BLK), upto(STEPS)),
@@ -594,8 +742,7 @@
             whole(length, 128),
             pl.BlockSpec((length, BLK), upto(STEPS - 1)),
             pl.BlockSpec((STATE, BLK), upto(STEPS - 1)),
-            pl.BlockSpec((count, STATE, BLK), lambda j: (0, 0, jnp.minimum(j, STEPS - 1))),
-            whole(count, 8, 128),
+            pl.BlockSpec((STATE, BLK), upto(STEPS - 1)),
             pl.BlockSpec(memory_space=pl.ANY),
         ],
         out_specs=[
@@ -630,14 +777,14 @@
             pltpu.VMEM((8 * (length // Q), 128), F32),
             pltpu.VMEM((length // Q, STATE, BLK), F32),
         ],
-        input_output_aliases={16: 0},
+        input_output_aliases={14: 0},
         compiler_params=pltpu.CompilerParams(vmem_limit_bytes=VMEM_LIMIT),
         cost_estimate=pl.CostEstimate(
             flops=12 * 10**9, bytes_accessed=30 * 10**6, transcendentals=2 * 10**7
         ),
         name="back",
     )(
-        place, projected, projected, halo, taps, heads, seg_lanes, seg_row, b_rows, c_rows, dt, running, dy, incoming, dstates, kept, given
+        projected, projected, halo, taps, heads, seg_lanes, seg_row, b_rows, c_rows, dt, running, dy, incoming, outgoing, given
     )
 
 
@@ -926,7 +1073,7 @@
     input_gain,
 ):
     shards, parts = lax.axis_size("fsdp"), lax.axis_size("ctx")
-    place = jnp.reshape(lax.axis_index("ctx"), (1,)).astype(jnp.int32)
+    place = lax.axis_index("ctx")
     units_low, cot = inputs[0], out_grad[0]
     units = units_low.astype(F32)
     seg_ids = segment_ids[0]
@@ -956,17 +1103,20 @@
     rim_rows = passed_along(projected[length - CONV + 1 :, INNER : INNER + XBC], "ctx", 1)
     halo = jnp.pad(rim_rows, ((PAD - CONV + 1, 0), (0, 0))).astype(F32)
 
-    xs, y_local, state, b_rows, c_rows, dt, running, entering, keep = front(
-        projected, halo, taps, heads, seg_lanes, seg_row
-    )
-    kept = lax.all_gather(keep, "ctx")
-    states = lax.all_gather(state, "ctx")
-    mixer_t, dproj, dy, incoming, d_incoming, column_sums, block_out, stats = tail(
-        place, y_local, xs, projected, states, kept, out_whole, c_rows, entering, heads, gain, cot, units_low
-    )
-    dstates = lax.all_gather(d_incoming, "ctx")
+    here = (shards, parts) == (4, PARTS)
+    xs, y_local, incoming, b_rows, c_rows, dt, running, entering, kept = front(
+        projected, halo, taps, heads, seg_lanes, seg_row, here
+    )
+    if not here:
+        kept = lax.all_gather(kept[0], "ctx")
+        incoming = joined_plainly(lax.all_gather(incoming, "ctx"), kept, place, True)
+    mixer_t, dproj, dy, outgoing, column_sums, block_out, stats = tail(
+        y_local, xs, projected, incoming, kept, out_whole, c_rows, entering, heads, gain, cot, units_low, here
+    )
+    if not here:
+        outgoing = joined_plainly(lax.all_gather(outgoing, "ctx"), kept, place, False)
     dproj, d_halo, d_taps, d_heads = back(
-        place, projected, halo, taps, heads, seg_lanes, seg_row, b_rows, c_rows, dt, running, dy, incoming, dstates, kept, dproj
+        projected, halo, taps, heads, seg_lanes, seg_row, b_rows, c_rows, dt, running, dy, incoming, outgoing, dproj
     )
     returned = passed_along(d_halo.astype(BF16), "ctx", -1)
     last = lax.slice(dproj, (length - PAD, INNER), (length, INNER + XBC))
@@ -991,7 +1141,7 @@
         ]
     )
     row = jnp.pad(row, (0, SMALL_ROWS * 128 - row.shape[0])).reshape(SMALL_ROWS, 128)
-    if (shards, parts) == (4, 8):
+    if here:
         d_in, d_out, row = reduce(
             part_rows.T.reshape(4, SHARD, length), mixer_t.reshape(4, 2, SHARD, length), dproj, cot, row
         )

time: 783 us -> 612 us (0.78)
  waiting for transfers between devices: 295 us -> 119 us
  Pallas kernels: 349 us -> 386 us
  blocking collectives: 38.8 us -> 5.25 us
    all_gather x2 -> x0, waiting for transfers between devices: 173 us -> none  [the longest x1 95.2 us: on_device(): dstates = lax.all_gather(d_incoming, 'ctx')]
    pallas_call x3, Pallas kernels: 140 us -> 175 us  [the longest x1 63.3 us: back(): pl.pallas_call(back_kernel, grid=(STEPS + 2,), in_specs=[pl.BlockSpec((le...]
    all_gather x1 -> x0, blocking collectives: 33.6 us -> none  [on_device(): kept = lax.all_gather(keep, 'ctx')]
  transfers between devices with their start and end apart: 7 -> 5, of which waited for: 5 -> 3; matrix products, arithmetic and copies ran while one was open for 3% -> 4% of each run, Pallas kernels for 4% -> 8%
where the time goes in v3:
time: 612 us; the launch traced here: 611 us
  Pallas kernels  386 us (63%)
  waiting for transfers between devices  119 us (19%)
  matrix products  32.7 us (5%)
  local copies, waits for them, and re-layouts  30.9 us (5%)
  between operations  14.4 us (2%)
  other arithmetic  13.1 us (2%)
  starting transfers between devices  9.74 us (2%)
    pallas_call x1, Pallas kernels, reduce(): pl.pallas_call(reduce_kernel, grid=(CHUNKS + LAGS - 1,), in_specs=[whole(...  210 us
    all_gather x1, waiting for transfers between devices, on_device(): w_whole = lax.all_gather(in_matrix, 'fsdp', axis=0, tiled=True)  115 us
    pallas_call x1, Pallas kernels, back(): pl.pallas_call(back_kernel, grid=(STEPS + 2,), in_specs=[pl.BlockSpec((le...  63.3 us
    pallas_call x1, Pallas kernels, tail(): pl.pallas_call(tail_kernel, grid=(2 * STEPS + DONE * exchanging,), in_spe...  61.6 us
    pallas_call x1, Pallas kernels, front(): pl.pallas_call(front_kernel, grid=(STEPS + DONE * exchanging,), in_specs=...  50.4 us
    dot_general x1, matrix products, dot(): return jnp.dot(a, b, preferred_element_type=F32)  16.7 us
    dot_general x1, matrix products, dot_nt(): lax.dot_general(a, b, (((1,), (1,)), ((), ())), preferred_element_type=F32)  16 us
    unnamed x35, local copies, waits for them, and re-layouts  14.8 us
  transfers between devices with their start and end apart: 5, of which 3 were waited for; matrix products, arithmetic and copies ran while one was open for 4% of the time, Pallas kernels for 8%

profile of v3, /device:TPU:0, one launch (start us, length us, event | category | flops | bytes accessed | tf_op | source)
XLA Modules:
  0.0 610.6 jit_solution(10409397581233061613)
XLA Ops:
  8.8 4.8 collective-permute-start.1
  13.9 5.2 all-gather
  21.9 115.4 %all-gather.4.cloned.1.call-done = bf16[1536,6448]{0,1:T(8,128)(2,1)} async-done(((bf16[384,6448]{0,1:T(8,128)(2,1)}), bf16[1536,6448]{0,1:T(8,128)(2,1)}) %all-gather.4.cloned.1.call-update) | async-done | bytes 19808272 | tf_op jit(solution)/shard_map/all_gather | solution.py:1084
  137.3 16.7 %convolution_convert_fusion.x_ref.bc_ref.dtraw_ref.gate_ref = bf16[512,6448]{1,0:T(8,128)(2,1)} fusion(bf16[1536,6448]{0,1:T(8,128)(2,1)} %all-gather.4.cloned.1.call-done, f32[1536]{0:T(1024)S(1)} %reshape.107, f32[512]{0:T(512)S(1)} %add_rsqrt_fusion, bf16[1,512,1536]{2,1,0:T(8,128)(2,1)S(1)} %copy-done), kind=kOutput, calls=%fused_computation | convolution fusion | flops 10148274176 | bytes 27992064 | tf_op jit(solution)/shard_map/dot_general | solution.py:40
  154.0 0.8 slice.113
  154.8 3.6 collective-permute-start
  158.5 1.2 collective-permute-done
  160.4 0.8 broadcast_in_dim.35.seg_ref
  161.8 50.4 %front.1 = (bf16[512,3072]{1,0:T(8,128)(2,1)}, bf16[512,3072]{1,0:T(8,128)(2,1)}, bf16[128,3072]{1,0:T(8,128)(2,1)}, bf16[512,128]{1,0:T(8,128)(2,1)}, bf16[512,...) custom-call(bf16[512,6448]{1,0:T(8,128)(2,1)} %convolution_convert_f, ...), custom_call_target="tpu_custom_call" | custom-call | flops 6000000000 | bytes 16000000 | tf_op jit(solution)/shard_map/front/pallas_call | solution.py:321
  212.2 61.6 %tail.1 = (bf16[3072,512]{1,0:T(8,128)(2,1)}, bf16[512,6448]{1,0:T(8,128)(2,1)}, bf16[512,3072]{1,0:T(8,128)(2,1)}, bf16[128,3072]{1,0:T(8,128)(2,1)}, f32[8,307...) custom-call(bf16[512,3072]{1,0:T(8,128)(2,1)} %get-tuple-element.35.y_ref, ...), custom_call_target="tpu_custom_call" | custom-call | flops 12000000000 | bytes 50000000 | tf_op jit(solution)/shard_map/tail/pallas_call | solution.py:505
  273.8 63.3 %back.1 = (bf16[512,6448]{1,0:T(8,128)(2,1)}, f32[8,3328]{1,0:T(8,128)}, f32[8,3328]{1,0:T(8,128)}, f32[8,128]{1,0:T(8,128)}) custom-call(bf16[512,6448]{1,0:T(8,128)(2,1)} %convolution_convert_fusion.x_ref.bc_ref.dtraw_ref.gate_ref, bf16[512,6448]{1,0:T(8,128)(2,1)} %convolution_convert_fusion.x_ref.bc_ref.dtraw_ref.gate_ref, ...), custom_call_target="tpu_custom_call", output_to_operand_aliasing={{0}: (14, {})} | custom-call | flops 12000000000 | bytes 30000000 | tf_op jit(solution)/shard_map/back/pallas_call | solution.py:728
  337.1 0.9 convert_element_type.96
  338.0 1.3 collective-permute-start.2
  339.3 0.8 slice_bitcast_fusion.4
  340.0 1.0 slice_reduce_fusion.1
  341.0 0.9 slice_reduce_fusion
  342.0 0.9 reshape.104
  343.1 0.9 collective-permute-done.2
  344.0 1.4 fusion.15.rhs_in
  345.4 16.0 %fusion.24 = f32[512,1536]{1,0:T(8,128)S(1)} fusion(bf16[512,6448]{1,0:T(8,128)(2,1)} %fusion.15.rhs_in, bf16[1536,6448]{0,1:T(8,128)(2,1)} %all-gather.4.cloned.1.call-done), kind=kOutput, calls=%fused_computation.49 | convolution fusion | flops 10141827072 | bytes 29556736 | tf_op jit(solution)/shard_map/dot_general | solution.py:44
  361.4 1.1 fusion.10
  363.8 1.6 copy.35
  365.4 210.4 %reduce.5 = (f32[384,6448]{1,0:T(8,128)}, f32[768,1536]{1,0:T(8,128)}, f32[168,128]{1,0:T(8,128)}) custom-call(bf16[4,384,512]{2,1,0:T(8,128)(2,1)} %bitcast.54, bf16[4,2,384,512]{3,2,1,0:T(8,128)(2,1)} %bitcast.57, bf16[512,6448]{1,0:T(8,128)(2,1)} %fusion.15.rhs_in, bf16[512,1536]{1,0:T(8,128)(2,1)} %bitcast.53, f32[168,128]{1,0:T(8,128)} %pad_bitcast_fusion.small_ref), custom_call_target="tpu_custom_call" | custom-call | tf_op jit(solution)/shard_map/reduce/pallas_call | solution.py:981
  575.8 0.8 slice.101
  576.6 0.7 slice_bitcast_fusion
  577.3 0.7 slice_bitcast_fusion.1
  578.8 0.9 fusion.23
  579.6 1.3 fusion.21
  580.9 10.8 %copy.33 = f32[384,6448]{0,1:T(8,128)} copy(f32[384,6448]{1,0:T(8,128)} %get-tuple-element.72) | data formatting | bytes 19808256
  594.8 4.3 fusion.12
  600.4 1.1 copy.43
  601.6 2.2 copy.44
  (81 shorter events, 12.4 us)
Async XLA Ops:
  7.2 1.6 copy-start.5
  7.2 6.5 %copy-start.7 = (bf16[768]{0:T(1024)(128)(2,1)S(1)}, bf16[768]{0:T(1024)(128)(2,1)}, u32[]{:S(2)}) copy-start(bf16[768]{0:T(1024)(128)(2,1)} %param.22) | copy-start | bytes 4612
  7.2 6.5 %copy-start.9 = (bf16[384]{0:T(512)(128)(2,1)S(1)}, bf16[384]{0:T(512)(128)(2,1)}, u32[]{:S(2)}) copy-start(bf16[384]{0:T(512)(128)(2,1)} %param.23) | copy-start | bytes 2308
  7.2 6.5 %copy-start.12 = (bf16[12]{0:T(256)(128)(2,1)S(1)}, bf16[12]{0:T(256)(128)(2,1)}, u32[]{:S(2)}) copy-start(bf16[12]{0:T(256)(128)(2,1)} %param.19) | copy-start | bytes 76
  7.2 6.5 %copy-start.11 = (bf16[12]{0:T(256)(128)(2,1)S(1)}, bf16[12]{0:T(256)(128)(2,1)}, u32[]{:S(2)}) copy-start(bf16[12]{0:T(256)(128)(2,1)} %param.20) | copy-start | bytes 76
  7.2 6.5 %copy-start.10 = (bf16[12]{0:T(256)(128)(2,1)S(1)}, bf16[12]{0:T(256)(128)(2,1)}, u32[]{:S(2)}) copy-start(bf16[12]{0:T(256)(128)(2,1)} %param.21) | copy-start | bytes 76
  7.2 6.6 %copy-start.8 = (bf16[832]{0:T(1024)(128)(2,1)S(1)}, bf16[832]{0:T(1024)(128)(2,1)}, u32[]{:S(2)}) copy-start(bf16[832]{0:T(1024)(128)(2,1)} %param.18) | copy-start | bytes 4996
  7.3 6.6 %copy-start.6 = (bf16[832,4]{0,1:T(4,128)(2,1)S(1)}, bf16[832,4]{0,1:T(4,128)(2,1)}, u32[]{:S(2)}) copy-start(bf16[832,4]{0,1:T(4,128)(2,1)} %param.17) | copy-start | bytes 19972
  7.3 13.0 %copy-start = (bf16[1,512,1536]{2,1,0:T(8,128)(2,1)S(1)}, bf16[1,512,1536]{2,1,0:T(8,128)(2,1)}, u32[]{:S(2)}) copy-start(bf16[1,512,1536]{2,1,0:T(8,128)(2,1)} %param.12) | copy-start | bytes 4718596
  7.3 130.0 %all-gather.4.cloned.1.call-start = ((), (), s32[]{:S(2)}) async-start(), calls=%async_computation | async-start | bytes 24760320 | tf_op jit(solution)/shard_map/all_gather | solution.py:1084
  8.0 204.2 %all-gather.6.cloned.1.call-start = ((), (), s32[]{:S(2)}) async-start(), calls=%async_computation.1 | async-start | bytes 11796480 | tf_op jit(solution)/shard_map/all_gather | solution.py:1085
  8.8 149.6 %collective-permute-start.1 = (s32[3]{0:T(128)S(1)}, s32[3]{0:T(128)S(1)}, u32[]{:S(2)}, u32[]{:S(2)}) collective-permute-start(s32[3]{0:T(128)S(1)} %slice_bitcast_fusion.6), channel_id=1, source_target_pairs={{0,1},{1,2},{2,3},{3,4},{4,5},{5,6},{6,7},{8,9},{9,10},{10,11},{11... | collective-permute-start | bytes 44 | tf_op jit(solution)/shard_map/ppermute | solution.py:1027
  154.8 4.9 collective-permute-start
  338.0 6.0 collective-permute-start.2
  345.4 16.0 %copy-start.1 = (bf16[1,512,1536]{2,1,0:T(8,128)(2,1)S(1)}, bf16[1,512,1536]{2,1,0:T(8,128)(2,1)}, u32[]{:S(2)}) copy-start(bf16[1,512,1536]{2,1,0:T(8,128)(2,1)} %param.12) | copy-start | bytes 4718596
  361.4 1.7 copy-start.2
  580.9 13.9 %copy-start.3 = (bf16[1,512,1536]{2,1,0:T(8,128)(2,1)S(1)}, bf16[1,512,1536]{2,1,0:T(8,128)(2,1)}, u32[]{:S(2)}) copy-start(bf16[1,512,1536]{2,1,0:T(8,128)(2,1)} %param.14) | copy-start | bytes 4718596
  594.8 6.7 %slice-start = ((s8[4718592]{0:T(1024)(128)(4,1)}), s8[4194304]{0:T(1024)(128)(4,1)S(1)}, s32[]{:S(2)}) async-start(s8[4718592]{0:T(1024)(128)(4,1)} %bitcast.55), calls=%async_computation.2 | async-start | bytes 8388608
  594.8 5.6 copy-start.4
  594.8 6.7 %slice-start.1 = ((s8[4718592]{0:T(1024)(128)(4,1)}), s8[524288]{0:T(1024)(128)(4,1)S(1)}, s32[]{:S(2)}) async-start(s8[4718592]{0:T(1024)(128)(4,1)} %bitcast.55), calls=%async_computation.3 | async-start | bytes 1048576
Sparse Core Ops, SparseCore 0:
  9.7 127.5 all-gather.3
  138.9 64.2 all-gather.5

commit v4 on v3

--- a/solution.py
+++ b/solution.py
@@ -15,12 +15,18 @@
 INNER = 3072
 XBC = 3328
 PROJ = 6448
+WIDTH = 6656
 
 BLK = 256
 GROUP = BLK // HDIM
 STEPS = INNER // BLK
 Q = 128
 PAD = 8
+WIDE = 512
+SHARD = D // 4
+PIECE = SHARD // 8
+SMALL_WIDTH = 896
+AHEAD = 2
 
 epsilon = 1e-05
 F32, BF16 = jnp.float32, jnp.bfloat16
@@ -108,6 +114,274 @@
     return jnp.where(keep, dot_nt(c_rows, b_rows), 0.0)
 
 
+def flipped(index, bit):
+    return index + bit - 2 * bit * lax.rem(index // bit, 2)
+
+
+class Gather:
+    def __init__(self, target, loads, sends, arrivals):
+        self.target, self.loads, self.sends, self.arrivals = target, loads, sends, arrivals
+        shard, part = lax.axis_index("fsdp"), lax.axis_index("ctx")
+        self.own, self.other = shard, flipped(shard, 2)
+        self.sibling, self.opposite = flipped(shard, 1), flipped(flipped(shard, 2), 1)
+        x, near = lax.rem(part, 2), lax.rem(part // 2, 2)
+        self.mine, self.over_x, self.over_z = 2 * x + near, 2 * (1 - x) + near, 2 * x + 1 - near
+        self.across = 2 * (1 - x) + 1 - near
+        self.peers = {
+            "core": {"fsdp": flipped(shard, 1)},
+            "y": {"fsdp": flipped(shard, 2)},
+            "x": {"ctx": flipped(part, 1)},
+            "z": {"ctx": flipped(part, 2)},
+        }
+
+    def whole(self, shard, k):
+        return self.target.at[k, shard]
+
+    def quarter(self, shard, k, which):
+        rows = self.target.shape[2] // 4
+        return self.target.at[k, shard, pl.ds(pl.multiple_of(which * rows, rows), rows)]
+
+    def half(self, shard, k, which, second):
+        rows = self.target.shape[2] // 8
+        return self.target.at[k, shard, pl.ds(pl.multiple_of(which * 2 * rows + second * rows, rows), rows)]
+
+    def copy(self, place, kind, k, peer):
+        return pltpu.make_async_remote_copy(
+            src_ref=place,
+            dst_ref=place,
+            send_sem=self.sends.at[kind, k],
+            recv_sem=self.arrivals.at[kind, k],
+            device_id=self.peers[peer],
+            device_id_type=pl.DeviceIdType.MESH,
+        )
+
+    def outgoing(self, kind, k):
+        own, other = self.own, self.other
+        if kind == 0:
+            return self.copy(self.whole(own, k), kind, k, "core")
+        if kind == 1:
+            return self.copy(self.quarter(own, k, self.mine), kind, k, "y")
+        if kind == 2:
+            return self.copy(self.quarter(other, k, self.mine), kind, k, "x")
+        if kind == 3:
+            return self.copy(self.quarter(other, k, self.mine), kind, k, "z")
+        if kind == 4:
+            return self.copy(self.half(other, k, self.over_x, 0), kind, k, "z")
+        if kind == 5:
+            return self.copy(self.half(other, k, self.over_z, 1), kind, k, "x")
+        which = (self.mine, self.over_x, self.over_z, self.across)[kind - 6]
+        return self.copy(self.quarter(other, k, which), kind, k, "core")
+
+    def arrived(self, kind, k):
+        other, opposite = self.other, self.opposite
+        if kind == 0:
+            place = self.whole(self.sibling, k)
+        elif kind < 4:
+            place = self.quarter(other, k, (self.mine, self.over_x, self.over_z)[kind - 1])
+        elif kind < 6:
+            place = self.half(other, k, self.across, kind - 4)
+        else:
+            place = self.quarter(opposite, k, (self.mine, self.over_x, self.over_z, self.across)[kind - 6])
+        self.copy(place, kind, k, "core").wait_recv()
+
+    def load(self, k, source):
+        return pltpu.make_async_copy(source, self.whole(self.own, k), self.loads.at[k])
+
+    def begin(self, k):
+        self.load(k, self.whole(self.own, k)).wait()
+        self.outgoing(1, k).start()
+        self.outgoing(0, k).start()
+
+    def first(self, k):
+        self.arrived(1, k)
+        for kind in (2, 3, 6):
+            self.outgoing(kind, k).start()
+
+    def second(self, k):
+        self.arrived(2, k)
+        self.outgoing(4, k).start()
+        self.outgoing(7, k).start()
+        self.arrived(3, k)
+        self.outgoing(5, k).start()
+        self.outgoing(8, k).start()
+
+    def third(self, k):
+        self.arrived(4, k)
+        self.arrived(5, k)
+        self.outgoing(9, k).start()
+
+    def complete(self, k):
+        for kind in (0, 6, 7, 8, 9):
+            self.arrived(kind, k)
+
+    def drain(self, k):
+        for kind in range(10):
+            self.outgoing(kind, k).wait_send()
+
+
+def gather_sems(chunks):
+    return [
+        pltpu.SemaphoreType.DMA((chunks,)),
+        pltpu.SemaphoreType.DMA((10, chunks)),
+        pltpu.SemaphoreType.DMA((10, chunks)),
+    ]
+
+
+def project_kernel(
+    main_ref, rest_ref, units_ref, small_ref, seg_ref,
+    weight_ref, projected_ref, normed_t_ref, smalls_ref, halo_ref, seg_before_ref,
+    normed, gathered, own_small, smalls, own_seg, seg_before, edges, halos,
+    loads, sends, arrivals, stores, small_sends, small_arrivals, edge_sends, edge_arrivals,
+):
+    step = pl.program_id(0)
+    chunks = WIDTH // WIDE
+    length = units_ref.shape[0]
+    gather = Gather(gathered, loads, sends, arrivals)
+    shard, part = lax.axis_index("fsdp"), lax.axis_index("ctx")
+    others = ({"fsdp": flipped(shard, 1)}, {"fsdp": flipped(shard, 2)}, {"fsdp": flipped(flipped(shard, 1), 2)})
+    following, outer = lax.rem(part + 1, PARTS), lax.rem(part + PARTS - 1 + 2 * lax.rem(part, 2), PARTS)
+
+    def remote(source, target, send, arrival, peer):
+        return pltpu.make_async_remote_copy(
+            src_ref=source,
+            dst_ref=target,
+            send_sem=send,
+            recv_sem=arrival,
+            device_id=peer,
+            device_id_type=pl.DeviceIdType.MESH,
+        )
+
+    def small_copy(hop):
+        return remote(own_small, smalls.at[shard], small_sends.at[hop], small_arrivals.at[hop], others[hop])
+
+    def seg_copy():
+        return remote(own_seg, seg_before, small_sends.at[3], small_arrivals.at[3], {"ctx": following})
+
+    def edge_copy(k):
+        return remote(edges.at[k], halos.at[k], edge_sends.at[k], edge_arrivals.at[k], {"ctx": following})
+
+    def store(k):
+        columns = pl.ds(pl.multiple_of(k * WIDE, WIDE), WIDE)
+        return pltpu.make_async_copy(gathered.at[k], weight_ref.at[:, :, columns], stores.at[k])
+
+    @pl.when(step == 0)
+    def _():
+        barrier = pltpu.get_barrier_semaphore()
+        near = [*others, {"ctx": flipped(part, 1)}, {"ctx": flipped(part, 2)}, {"ctx": outer}]
+        for peer in near:
+            pl.semaphore_signal(barrier, inc=1, device_id=peer, device_id_type=pl.DeviceIdType.MESH)
+        for k in range(chunks):
+            gather.load(k, main_ref.at[:, k * WIDE : (k + 1) * WIDE] if k + 1 < chunks else rest_ref).start()
+        own_small[...] = small_ref[...]
+        own_seg[...] = seg_ref[...]
+        smalls[shard] = small_ref[...]
+        pl.semaphore_wait(barrier, len(near))
+        for hop in range(3):
+            small_copy(hop).start()
+        seg_copy().start()
+        for k in range(AHEAD):
+            gather.begin(k)
+        for hop in range(3):
+            small_copy(hop).wait()
+        seg_copy().wait()
+        smalls_ref[...] = smalls[...]
+        seg_before_ref[...] = jnp.where(part == 0, -1, seg_before[...])
+        gain = jnp.concatenate([smalls[s, 6:7, :SHARD] for s in range(4)], axis=1)
+        for k in range(length // Q):
+            rows = slice(k * Q, (k + 1) * Q)
+            units = units_ref[rows, :].astype(F32)
+            norm = lax.rsqrt(jnp.sum(units * units, axis=1, keepdims=True) * (1.0 / D) + epsilon)
+            value = units * norm * gain
+            normed[rows, :] = value.astype(BF16)
+            for s in range(4):
+                normed_t_ref[s, :, rows] = value[:, s * SHARD : (s + 1) * SHARD].T.astype(BF16)
+
+    def stage(lag):
+        def decorate(body):
+            k = step - lag
+
+            @pl.when((k >= 0) & (k < chunks))
+            def _():
+                body(k)
+
+        return decorate
+
+    stage(-AHEAD)(lambda k: pl.when(k >= AHEAD)(lambda: gather.begin(k)))
+    stage(0)(gather.first)
+    stage(1)(gather.second)
+    stage(2)(gather.third)
+
+    @stage(3)
+    def _(k):
+        gather.complete(k)
+        store(k).start()
+        low = dot(normed[...], gathered[k].reshape(D, WIDE)).astype(BF16)
+        projected_ref[...] = low
+        edges[k] = low[length - 16 :, :].astype(F32)[8:, :]
+        edge_copy(k).start()
+
+    @stage(4)
+    def _(k):
+        edge_copy(k).wait()
+        gather.drain(k)
+        store(k).wait()
+        halo_ref[...] = jnp.where(part == 0, 0.0, halos[k])
+
+
+def project(in_matrix, units, small, seg_ids):
+    length = units.shape[0]
+    chunks = WIDTH // WIDE
+    rest = jnp.pad(in_matrix[:, (chunks - 1) * WIDE :], ((0, 0), (0, WIDTH - PROJ)))
+    whole = lambda *shape: pl.BlockSpec(shape, lambda t: (0,) * len(shape))
+    column = lambda lag: lambda t: (0, jnp.clip(t - lag, 0, chunks - 1))
+    anywhere = pl.BlockSpec(memory_space=pl.ANY)
+    return pl.pallas_call(
+        project_kernel,
+        grid=(chunks + 4,),
+        in_specs=[
+            anywhere,
+            anywhere,
+            whole(length, D),
+            whole(8, SMALL_WIDTH),
+            whole(length // 128, 128),
+        ],
+        out_specs=[
+            anywhere,
+            pl.BlockSpec((length, WIDE), column(3)),
+            whole(4, SHARD, length),
+            whole(4, 8, SMALL_WIDTH),
+            pl.BlockSpec((PAD, WIDE), column(4)),
+            whole(length // 128, 128),
+        ],
+        out_shape=[
+            jax.ShapeDtypeStruct((4, SHARD, WIDTH), BF16),
+            jax.ShapeDtypeStruct((length, WIDTH), BF16),
+            jax.ShapeDtypeStruct((4, SHARD, length), BF16),
+            jax.ShapeDtypeStruct((4, 8, SMALL_WIDTH), F32),
+            jax.ShapeDtypeStruct((PAD, WIDTH), F32),
+            jax.ShapeDtypeStruct((length // 128, 128), jnp.int32),
+        ],
+        scratch_shapes=[
+            pltpu.VMEM((length, D), BF16),
+            pltpu.VMEM((chunks, 4, SHARD, WIDE), BF16),
+            pltpu.VMEM((8, SMALL_WIDTH), F32),
+            pltpu.VMEM((4, 8, SMALL_WIDTH), F32),
+            pltpu.VMEM((length // 128, 128), jnp.int32),
+            pltpu.VMEM((length // 128, 128), jnp.int32),
+            pltpu.VMEM((chunks, PAD, WIDE), F32),
+            pltpu.VMEM((chunks, PAD, WIDE), F32),
+            *gather_sems(chunks),
+            pltpu.SemaphoreType.DMA((chunks,)),
+            pltpu.SemaphoreType.DMA((4,)),
+            pltpu.SemaphoreType.DMA((4,)),
+            pltpu.SemaphoreType.DMA((chunks,)),
+            pltpu.SemaphoreType.DMA((chunks,)),
+        ],
+        compiler_params=communicating(3, True),
+        name="project",
+    )(in_matrix, rest, units, small, seg_ids.reshape(length // 128, 128))
+
+
 PARTS = 8
 SLAB = STATE // PARTS
 JOIN, DONE = 2, 4
@@ -121,13 +395,12 @@
     def others(self):
         return [lax.rem(self.me + hop, PARTS) for hop in range(1, PARTS)]
 
-    def greet(self):
+    def greet(self, *further):
         barrier = pltpu.get_barrier_semaphore()
-        for other in self.others():
-            pl.semaphore_signal(
-                barrier, inc=1, device_id={"ctx": other}, device_id_type=pl.DeviceIdType.MESH
-            )
-        pl.semaphore_wait(barrier, PARTS - 1)
+        peers = [{"ctx": other} for other in self.others()] + list(further)
+        for peer in peers:
+            pl.semaphore_signal(barrier, inc=1, device_id=peer, device_id_type=pl.DeviceIdType.MESH)
+        pl.semaphore_wait(barrier, len(peers))
 
     def copy(self, source, target, kind, group, other):
         return pltpu.make_async_remote_copy(
@@ -187,8 +460,8 @@
 
 
 def front_kernel(
-    x_ref, bc_ref, dtraw_ref, halo_ref, halo_bc_ref, taps_ref, taps_bc_ref, heads_ref, seg_ref, row_ref,
-    xs_ref, y_ref, state_ref, b_ref, c_ref, dt_ref, run_ref, in_ref, keep_ref,
+    x_ref, bc_ref, dtraw_ref, halo_ref, halo_bc_ref, taps_ref, taps_bc_ref, heads_ref, seg_ref, row_ref, shard_ref,
+    xs_ref, y_ref, state_ref, b_ref, c_ref, dt_ref, run_ref, in_ref, keep_ref, whole_ref,
     ext, scores, run_t, b_t, enter, leave, *parts,
 ):
     step = pl.program_id(0)
@@ -196,7 +469,13 @@
     chunks = length // Q
     if parts:
         exchange = Exchange(*parts[:5])
-        own_keep, keeps, keep_sends, keep_arrivals = parts[5:]
+        own_keep, keeps, keep_sends, keep_arrivals, gathered, loads, sends, arrivals, stores = parts[5:]
+        gather = Gather(gathered, loads, sends, arrivals)
+
+        def store(k):
+            columns = pl.ds(pl.multiple_of(k * WIDE, WIDE), WIDE)
+            return pltpu.make_async_copy(gathered.at[k], whole_ref.at[:, :, columns], stores.at[k])
+
 
         def keep_copy(hop):
             return pltpu.make_async_remote_copy(
@@ -243,9 +522,13 @@
         if parts:
             own_keep[...] = keep
             keeps[exchange.me] = keep
-            exchange.greet()
+            exchange.greet(gather.peers["core"], gather.peers["y"])
             for hop in range(PARTS - 1):
                 keep_copy(hop).start()
+            for k in range(D // WIDE):
+                gather.load(k, shard_ref.at[:, k * WIDE : (k + 1) * WIDE]).start()
+            for k in range(D // WIDE):
+                gather.begin(k)
         else:
             keep_ref[0] = keep
 
@@ -276,6 +559,21 @@
         @pl.when(step >= DONE)
         def _():
             state_ref[...] = exchange.finish(step - DONE)
+
+        def complete(k):
+            gather.complete(k)
+            store(k).start()
+
+        def drain(k):
+            gather.drain(k)
+            store(k).wait()
+
+        for lag, advance in enumerate((gather.first, gather.second, gather.third, complete, drain)):
+            k = step - 2 - 2 * lag
+
+            @pl.when((k >= 0) & (k < D // WIDE))
+            def _():
+                advance(k)
 
 
 def local_scan(
@@ -312,7 +610,7 @@
     return state
 
 
-def front(projected, halo, taps, heads, seg_lanes, seg_row, exchanging):
+def front(projected, halo, taps, heads, seg_lanes, seg_row, out_matrix, exchanging):
     length = projected.shape[0]
     last = STEPS - 1
     keeps = PARTS if exchanging else 1
@@ -325,13 +623,14 @@
             columns(length, lambda j: (0, STEPS + jnp.minimum(j, last))),
             columns(length, lambda j: (0, 2 * STEPS)),
             columns(length, lambda j: (0, 2 * STEPS + 1)),
-            columns(PAD, lambda j: (0, jnp.minimum(j, last))),
-            columns(PAD, lambda j: (0, STEPS)),
+            columns(PAD, lambda j: (0, STEPS + jnp.minimum(j, last))),
+            columns(PAD, lambda j: (0, 2 * STEPS)),
             columns(8, lambda j: (0, jnp.minimum(j, last))),
             columns(8, lambda j: (0, STEPS)),
             whole(8, 128),
             whole(length + 2 * PAD, 128),
             whole(8, length),
+            pl.BlockSpec(memory_space=pl.ANY),
         ],
         out_specs=[
             columns(length, lambda j: (0, jnp.minimum(j, last))),
@@ -343,6 +642,7 @@
             whole(length, 128),
             whole(length, 128),
             whole(keeps, 8, 128),
+            pl.BlockSpec(memory_space=pl.ANY),
         ],
         out_shape=[
             jax.ShapeDtypeStruct((length, INNER), BF16),
@@ -354,6 +654,7 @@
             jax.ShapeDtypeStruct((length, 128), F32),
             jax.ShapeDtypeStruct((length, 128), F32),
             jax.ShapeDtypeStruct((keeps, 8, 128), F32),
+            jax.ShapeDtypeStruct((4, *out_matrix.shape), BF16),
         ],
         scratch_shapes=[
             pltpu.VMEM((length + PAD, BLK), F32),
@@ -370,6 +671,9 @@
                 pltpu.VMEM((PARTS, 8, 128), F32),
                 pltpu.SemaphoreType.DMA((PARTS - 1,)),
                 pltpu.SemaphoreType.DMA((PARTS - 1,)),
+                pltpu.VMEM((D // WIDE, 4, 2 * SHARD, WIDE), BF16),
+                *gather_sems(D // WIDE),
+                pltpu.SemaphoreType.DMA((D // WIDE,)),
             ]
         )
         * exchanging,
@@ -378,7 +682,7 @@
             flops=6 * 10**9, bytes_accessed=16 * 10**6, transcendentals=10**7
         ),
         name="front",
-    )(projected, projected, projected, halo, halo, taps, taps, heads, seg_lanes, seg_row)
+    )(projected, projected, projected, halo, halo, taps, taps, heads, seg_lanes, seg_row, out_matrix)
 
 
 def tail_kernel(
@@ -530,7 +834,7 @@
         ],
         out_shape=[
             jax.ShapeDtypeStruct((INNER, length), BF16),
-            jax.ShapeDtypeStruct((length, PROJ), BF16),
+            jax.ShapeDtypeStruct((length, WIDTH), BF16),
             jax.ShapeDtypeStruct((length, INNER), BF16),
             jax.ShapeDtypeStruct((STATE, INNER), BF16),
             jax.ShapeDtypeStruct((8, INNER), F32),
@@ -731,7 +1035,7 @@
         in_specs=[
             pl.BlockSpec((length, BLK), upto(STEPS, STEPS)),
             pl.BlockSpec((length, BLK), lambda j: (0, 2 * STEPS + 1)),
-            pl.BlockSpec((PAD, BLK), upto(STEPS)),
+            pl.BlockSpec((PAD, BLK), upto(STEPS, STEPS)),
             pl.BlockSpec((8, BLK), upto(STEPS)),
             whole(8, 128),
             whole(length + 2 * PAD, 128),
@@ -752,7 +1056,7 @@
             whole(8, 128),
         ],
         out_shape=[
-            jax.ShapeDtypeStruct((length, PROJ), BF16),
+            jax.ShapeDtypeStruct((length, WIDTH), BF16),
             jax.ShapeDtypeStruct((PAD, XBC), F32),
             jax.ShapeDtypeStruct((8, XBC), F32),
             jax.ShapeDtypeStruct((8, 128), F32),
@@ -788,18 +1092,11 @@
     )
 
 
-WIDE = 512
 OUT_CHUNKS = 2 * D // WIDE
-IN_CHUNKS = -(-PROJ // WIDE)
+IN_CHUNKS = WIDTH // WIDE
 CHUNKS = OUT_CHUNKS + IN_CHUNKS
 LAGS = 8
-SHARD = D // 4
-PIECE = SHARD // 8
 SMALL_ROWS = 168
-
-
-def flipped(index, bit):
-    return index + bit - 2 * bit * lax.rem(index // bit, 2)
 
 
 def reduce_kernel(
@@ -892,9 +1189,7 @@
 
     @pl.when((step >= OUT_CHUNKS) & (step < CHUNKS))
     def _():
-        rhs = rhs_in[...]
-        columns = iota(rhs.shape, 1) + (step - OUT_CHUNKS) * WIDE
-        partial(lambda s: lhs_in[s], jnp.where(columns < PROJ, rhs, jnp.zeros_like(rhs)))
+        partial(lambda s: lhs_in[s], rhs_in[...])
 
     @pl.when(step < CHUNKS)
     def _():
@@ -957,7 +1252,7 @@
         arrivals[7](k).wait_recv()
         for one in range(1, 8):
             copies[one](k).wait_send()
-        whole = final[k].reshape(SHARD, WIDE).astype(F32)
+        whole = final[k].reshape(SHARD, WIDE)
 
         @pl.when(k < OUT_CHUNKS)
         def _():
@@ -994,8 +1289,8 @@
             whole(SMALL_ROWS, 128),
         ],
         out_shape=[
-            jax.ShapeDtypeStruct((SHARD, PROJ), F32),
-            jax.ShapeDtypeStruct((2 * SHARD, D), F32),
+            jax.ShapeDtypeStruct((SHARD, PROJ), BF16),
+            jax.ShapeDtypeStruct((2 * SHARD, D), BF16),
             jax.ShapeDtypeStruct((SMALL_ROWS, 128), F32),
         ],
         scratch_shapes=[
@@ -1034,7 +1329,7 @@
         flat = jnp.concatenate(parts)
         return jnp.pad(flat, (0, width - flat.shape[0]))[None]
 
-    return jnp.concatenate(
+    rows = jnp.concatenate(
         [
             conv_taps.T,
             conv_bias[None],
@@ -1044,12 +1339,13 @@
         ],
         axis=0,
     )
-
-
-def unpack_small(whole):
-    shards, _, width = whole.shape
+    return jnp.pad(rows.astype(F32), ((0, 0), (0, SMALL_WIDTH - width)))
+
+
+def unpack_small(whole, width):
+    shards = whole.shape[0]
     joined = jnp.swapaxes(whole, 0, 1)
-    taps = jnp.pad(joined[:5].reshape(5, shards * width).astype(F32), ((0, 3), (0, 0)))
+    taps = jnp.pad(joined[:5, :, :width].reshape(5, shards * width).astype(F32), ((0, 3), (0, 0)))
     gain = joined[5, :, : INNER // shards].reshape(1, INNER).astype(F32)
     input_gain = joined[6, :, : D // shards].reshape(1, D).astype(F32)
     own = HEADS // shards
@@ -1078,13 +1374,25 @@
     units = units_low.astype(F32)
     seg_ids = segment_ids[0]
     length = units.shape[0]
-    small = lax.all_gather(
-        pack_small(conv_taps, conv_bias, dt_bias, decay_log, skip_scale, mixer_gain, input_gain), "fsdp"
-    )
-    w_whole = lax.all_gather(in_matrix, "fsdp", axis=0, tiled=True)
-    out_whole = lax.all_gather(out_matrix, "fsdp", axis=0, tiled=True)
-    taps, gain, g_float, heads = unpack_small(small)
-    rim_seg = passed_along(seg_ids[length - CONV + 1 :], "ctx", 1)
+    here = (shards, parts) == (4, PARTS)
+    small = pack_small(conv_taps, conv_bias, dt_bias, decay_log, skip_scale, mixer_gain, input_gain)
+    inv_rms = lax.rsqrt(jnp.mean(units * units, axis=-1, keepdims=True) + epsilon)
+    base_rows = units * inv_rms
+    if here:
+        w_whole, projected, normed_t, smalls, halo, seg_before = project(in_matrix, units_low, small, seg_ids)
+        w_whole = w_whole.reshape(D, WIDTH)
+        rim_seg = seg_before.reshape(length)[length - CONV + 1 :]
+        taps, gain, g_float, heads = unpack_small(smalls, conv_bias.shape[0])
+    else:
+        w_whole = jnp.pad(in_matrix, ((0, 0), (0, WIDTH - PROJ)))
+        w_whole = lax.all_gather(w_whole, "fsdp", axis=0, tiled=True)
+        rim_seg = passed_along(seg_ids[length - CONV + 1 :], "ctx", 1)
+        taps, gain, g_float, heads = unpack_small(lax.all_gather(small, "fsdp"), conv_bias.shape[0])
+        normed = (base_rows * g_float).astype(BF16)
+        normed_t = normed.T
+        projected = dot(normed, w_whole).astype(BF16)
+        rim_rows = passed_along(projected[length - CONV + 1 :], "ctx", 1)
+        halo = jnp.pad(rim_rows, ((PAD - CONV + 1, 0), (0, 0))).astype(F32)
     seg_ext = jnp.concatenate(
         [
             jnp.full((PAD - CONV + 1,), -1, jnp.int32),
@@ -1096,18 +1404,12 @@
     seg_lanes = jnp.broadcast_to(seg_ext[:, None], (length + 2 * PAD, 128))
     seg_row = jnp.broadcast_to(seg_ids[None], (8, length))
 
-    inv_rms = lax.rsqrt(jnp.mean(units * units, axis=-1, keepdims=True) + epsilon)
-    base_rows = units * inv_rms
-    part_rows = (base_rows * g_float).astype(BF16)
-    projected = dot(part_rows, w_whole).astype(BF16)
-    rim_rows = passed_along(projected[length - CONV + 1 :, INNER : INNER + XBC], "ctx", 1)
-    halo = jnp.pad(rim_rows, ((PAD - CONV + 1, 0), (0, 0))).astype(F32)
-
-    here = (shards, parts) == (4, PARTS)
-    xs, y_local, incoming, b_rows, c_rows, dt, running, entering, kept = front(
-        projected, halo, taps, heads, seg_lanes, seg_row, here
+    xs, y_local, incoming, b_rows, c_rows, dt, running, entering, kept, out_whole = front(
+        projected, halo, taps, heads, seg_lanes, seg_row, out_matrix, here
     )
+    out_whole = out_whole.reshape(-1, D)
     if not here:
+        out_whole = lax.all_gather(out_matrix, "fsdp", axis=0, tiled=True)
         kept = lax.all_gather(kept[0], "ctx")
         incoming = joined_plainly(lax.all_gather(incoming, "ctx"), kept, place, True)
     mixer_t, dproj, dy, outgoing, column_sums, block_out, stats = tail(
@@ -1142,11 +1444,10 @@
     )
     row = jnp.pad(row, (0, SMALL_ROWS * 128 - row.shape[0])).reshape(SMALL_ROWS, 128)
     if here:
-        d_in, d_out, row = reduce(
-            part_rows.T.reshape(4, SHARD, length), mixer_t.reshape(4, 2, SHARD, length), dproj, cot, row
-        )
+        d_in, d_out, row = reduce(normed_t, mixer_t.reshape(4, 2, SHARD, length), dproj, cot, row)
+        d_in, d_out = d_in.astype(F32), d_out.astype(F32)
     else:
-        d_in = jnp.dot(part_rows.T, dproj, preferred_element_type=F32)
+        d_in = jnp.dot(normed_t, dproj, preferred_element_type=F32)[:, :PROJ]
         d_out = jnp.dot(mixer_t, cot, preferred_element_type=F32)
 
         def scattered(grad):

time: 612 us -> 548 us (0.90)
  waiting for transfers between devices: 119 us -> 0.01 us
  Pallas kernels: 386 us -> 471 us
  matrix products: 32.7 us -> 18.2 us
  between operations: 14.4 us -> 0.77 us
  local copies, waits for them, and re-layouts: 30.9 us -> 40.7 us
  starting transfers between devices: 9.74 us -> 1.28 us
    all_gather x2 -> x0, waiting for transfers between devices: 115 us -> none  [the longest x1 115 us: on_device(): w_whole = lax.all_gather(in_matrix, 'fsdp', axis=0, tiled=True)]
    pallas_call x0 -> x1, Pallas kernels: none -> 71.3 us  [project(): pl.pallas_call(project_kernel, grid=(chunks + 4,), in_specs=[anywhere, an...]
    dot_general x1 -> x0, matrix products: 16.7 us -> none  [dot(): return jnp.dot(a, b, preferred_element_type=F32)]
    pallas_call x1, Pallas kernels: 50.4 us -> 65.4 us  [front(): pl.pallas_call(front_kernel, grid=(STEPS + DONE * exchanging,), in_specs=...]
    ppermute x3 -> x1, starting transfers between devices: 9.67 us -> 1.28 us  [passed_along(): return lax.ppermute(block, axis, route)]
    unnamed x35 -> x11, local copies, waits for them, and re-layouts: 14.8 us -> 16.5 us
  transfers between devices with their start and end apart: 5 -> 1, of which waited for: 3 -> 0; matrix products, arithmetic and copies ran while one was open for 4% -> 1% of each run, Pallas kernels for 8% -> 0%
where the time goes in v4:
time: 548 us; the launch traced here: 547 us
  Pallas kernels  471 us (86%)
  local copies, waits for them, and re-layouts  40.7 us (7%)
  matrix products  18.2 us (3%)
  other arithmetic  15.1 us (3%)
    pallas_call x1, Pallas kernels, reduce(): pl.pallas_call(reduce_kernel, grid=(CHUNKS + LAGS - 1,), in_specs=[whole(...  210 us
    pallas_call x1, Pallas kernels, project(): pl.pallas_call(project_kernel, grid=(chunks + 4,), in_specs=[anywhere, an...  71.3 us
    pallas_call x1, Pallas kernels, front(): pl.pallas_call(front_kernel, grid=(STEPS + DONE * exchanging,), in_specs=...  65.4 us
    pallas_call x1, Pallas kernels, back(): pl.pallas_call(back_kernel, grid=(STEPS + 2,), in_specs=[pl.BlockSpec((le...  63.4 us
    pallas_call x1, Pallas kernels, tail(): pl.pallas_call(tail_kernel, grid=(2 * STEPS + DONE * exchanging,), in_spe...  60.4 us
    dot_general x1, matrix products, dot_nt(): lax.dot_general(a, b, (((1,), (1,)), ((), ())), preferred_element_type=F32)  18.2 us
    unnamed x11, local copies, waits for them, and re-layouts  16.5 us
  transfers between devices with their start and end apart: 1, of which 0 were waited for; matrix products, arithmetic and copies ran while one was open for 1% of the time, Pallas kernels for 0%

profile of v4, /device:TPU:0, one launch (start us, length us, event | category | flops | bytes accessed | tf_op | source)
XLA Modules:
  0.0 546.5 jit_solution(13664018465025930747)
XLA Ops:
  0.6 0.8 fusion.16
  3.5 0.7 concatenate.13
  4.8 7.5 %copy.31.main_ref = bf16[384,6448]{1,0:T(8,128)(2,1)} copy(bf16[384,6448]{0,1:T(8,128)(2,1)} %param.15) | data formatting | bytes 9904128 | tf_op args[3]
  12.4 1.0 slice.108
  13.4 0.8 pad.38.rest_ref
  14.1 71.3 %project.1 = (bf16[4,384,6656]{2,1,0:T(8,128)(2,1)}, bf16[512,6656]{1,0:T(8,128)(2,1)}, bf16[4,384,512]{2,1,0:T(8,128)(2,1)}, f32[4,8,896]{2,1,0:T(8,128)}, f32[8,6656]{1,0:T(8,128)}, /*index=5*/s32[4,128]{1,0:T(4,128)}) custom-call(bf16[384,6448]{1,0:T(8,128)(2,1)} %copy.31.main_ref, bf16[384,512]{1,0:T(8,128)(2,1)} %pad.38.rest_ref, ...), custom_call_target="tpu_custom_call" | custom-call | tf_op jit(solution)/shard_map/project/pallas_call | solution.py:338
  85.4 0.7 slice_reduce_fusion.3
  86.1 0.9 slice.111
  87.1 0.7 slice.87
  88.0 0.9 copy.32
  91.6 0.8 broadcast_in_dim.35.seg_ref
  92.4 65.4 %front.1 = (bf16[512,3072]{1,0:T(8,128)(2,1)}, bf16[512,3072]{1,0:T(8,128)(2,1)}, bf16[128,3072]{1,0:T(8,128)(2,1)}, bf16[512,128]{1,0:T(8,128)(2,1)}, bf16[512,...) custom-call(bf16[512,6656]{1,0:T(8,128)(2,1)} %get-tuple-element.42., ...), custom_call_target="tpu_custom_call" | custom-call | flops 6000000000 | bytes 16000000 | tf_op jit(solution)/shard_map/front/pallas_call | solution.py:619
  157.8 60.4 %tail.1 = (bf16[3072,512]{1,0:T(8,128)(2,1)}, bf16[512,6656]{1,0:T(8,128)(2,1)}, bf16[512,3072]{1,0:T(8,128)(2,1)}, bf16[128,3072]{1,0:T(8,128)(2,1)}, f32[8,307...) custom-call(bf16[512,3072]{1,0:T(8,128)(2,1)} %get-tuple-element.46.y_ref, ...), custom_call_target="tpu_custom_call" | custom-call | flops 12000000000 | bytes 50000000 | tf_op jit(solution)/shard_map/tail/pallas_call | solution.py:809
  218.3 63.4 %back.1 = (bf16[512,6656]{1,0:T(8,128)(2,1)}, f32[8,3328]{1,0:T(8,128)}, f32[8,3328]{1,0:T(8,128)}, f32[8,128]{1,0:T(8,128)}) custom-call(bf16[512,6656]{1,0:T(8,128)(2,1)} %get-tuple-element.42.x_ref.bc_ref.dtraw_ref.gate_ref, bf16[512,6656]{1,0:T(8,128)(2,1)} %get-tuple-element.42.x_ref.bc_ref.dtraw_ref.gate_ref, ...), custom_call_target="tpu_custom_call", output_to_operand_aliasing={{0}: (14, {})} | custom-call | flops 12000000000 | bytes 30000000 | tf_op jit(solution)/shard_map/back/pallas_call | solution.py:1032
  281.6 0.9 convert_element_type.49
  282.5 1.3 collective-permute-start
  284.2 0.8 slice_reduce_fusion.2
  285.1 0.8 slice_bitcast_fusion.3
  285.8 1.0 slice_reduce_fusion.1
  286.8 0.9 slice_reduce_fusion
  288.0 0.9 reshape.89
  288.9 1.4 fusion.11.rhs_in
  290.3 18.2 %fusion.8 = (f32[1536]{0:T(1024)S(1)}, f32[512]{0:T(512)S(1)}, f32[512,1536]{1,0:T(8,128)}) fusion(f32[512]{0:T(512)S(1)} %add_rsqrt_fusion, bf16[1,512,1536]{2,1,0:T(8,128)(2,1)S(1)} %copy-done, f32[1536]{0:T(1024)S(1)} %mul.58, bf16[512,6656]{1,0:T(8,128)(2,1)} %fusion.11.rhs_in, bf16[1536,6656]{1,0:T(8,128)(2,1)} %bitcast.60), kind=kOutput, calls=%fused_computation.10 | convolution fusion | flops 10474485760 | bytes 31997952 | tf_op jit(solution)/shard_map/dot_general | solution.py:50
  309.3 210.1 %reduce.11 = (bf16[384,6448]{1,0:T(8,128)(2,1)}, bf16[768,1536]{1,0:T(8,128)(2,1)}, f32[168,128]{1,0:T(8,128)}) custom-call(bf16[4,384,512]{2,1,0:T(8,128)(2,1)} %get-tuple-element.63.lhs_in, bf16[4,2,384,512]{3,2,1,0:T(8,128)(2,1)} %bitcast.44, bf16[512,6656]{1,0:T(8,128)(2,1)} %fusion.11.rhs_in, bf16[512,1536]{1,0:T(8,128)(2,1)} %bitcast.43, ...), custom_call_target="tpu_custom_call" | custom-call | tf_op jit(solution)/shard_map/reduce/pallas_call | solution.py:1276
  519.4 1.3 fusion.17
  520.7 0.9 fusion.18
  522.2 0.7 slice_bitcast_fusion.1
  523.7 0.8 slice.97
  527.6 4.5 convert_element_type.54
  532.1 7.9 %copy.34 = f32[384,6448]{0,1:T(8,128)} copy(bf16[384,6448]{1,0:T(8,128)(2,1)} %get-tuple-element.69) | data formatting | bytes 14856192
  540.0 4.1 fusion.10
  545.4 1.1 copy.38
  (45 shorter events, 12.8 us)
Async XLA Ops:
  14.1 76.8 %copy-start.3 = (s32[1,512]{1,0:T(1,128)S(1)}, s32[1,512]{1,0:T(1,128)}, u32[]{:S(2)}) copy-start(s32[1,512]{1,0:T(1,128)} %param.13) | copy-start | bytes 6148
  218.2 65.6 %copy-start = (bf16[1,512,1536]{2,1,0:T(8,128)(2,1)S(1)}, bf16[1,512,1536]{2,1,0:T(8,128)(2,1)}, u32[]{:S(2)}) copy-start(bf16[1,512,1536]{2,1,0:T(8,128)(2,1)} %param.12) | copy-start | bytes 4718596
  282.5 6.3 %collective-permute-start = (bf16[8,3328]{1,0:T(8,128)(2,1)S(1)}, bf16[8,3328]{1,0:T(8,128)(2,1)S(1)}, u32[]{:S(2)}, u32[]{:S(2)}) collective-permute-start(bf16[8,3328]{1,0:T(8,128)(2,1)S(1)} %convert_element_type.49), channel_id=1, source_target_pairs={{1,0},{2,1},{3,2},{4,3},{5,4},{6,5},{7,6},{9,8},{10,9},{11,10},{12... | collective-permute-start | bytes 159752 | tf_op jit(solution)/shard_map/ppermute | solution.py:1322
  532.1 7.9 %copy-start.1 = (bf16[1,512,1536]{2,1,0:T(8,128)(2,1)S(1)}, bf16[1,512,1536]{2,1,0:T(8,128)(2,1)}, u32[]{:S(2)}) copy-start(bf16[1,512,1536]{2,1,0:T(8,128)(2,1)} %param.14) | copy-start | bytes 4718596
  540.0 5.4 copy-start.2

commit v5 on v4

--- a/solution.py
+++ b/solution.py
@@ -119,8 +119,9 @@
 
 
 class Gather:
-    def __init__(self, target, loads, sends, arrivals):
-        self.target, self.loads, self.sends, self.arrivals = target, loads, sends, arrivals
+    def __init__(self, locate, rows, loads, sends, arrivals):
+        self.locate, self.rows = locate, rows
+        self.loads, self.sends, self.arrivals = loads, sends, arrivals
         shard, part = lax.axis_index("fsdp"), lax.axis_index("ctx")
         self.own, self.other = shard, flipped(shard, 2)
         self.sibling, self.opposite = flipped(shard, 1), flipped(flipped(shard, 2), 1)
@@ -135,15 +136,13 @@
         }
 
     def whole(self, shard, k):
-        return self.target.at[k, shard]
+        return self.locate(k, shard, 0, self.rows)
 
     def quarter(self, shard, k, which):
-        rows = self.target.shape[2] // 4
-        return self.target.at[k, shard, pl.ds(pl.multiple_of(which * rows, rows), rows)]
+        return self.locate(k, shard, which * (self.rows // 4), self.rows // 4)
 
     def half(self, shard, k, which, second):
-        rows = self.target.shape[2] // 8
-        return self.target.at[k, shard, pl.ds(pl.multiple_of(which * 2 * rows + second * rows, rows), rows)]
+        return self.locate(k, shard, (2 * which + second) * (self.rows // 8), self.rows // 8)
 
     def copy(self, place, kind, k, peer):
         return pltpu.make_async_remote_copy(
@@ -236,7 +235,12 @@
     step = pl.program_id(0)
     chunks = WIDTH // WIDE
     length = units_ref.shape[0]
-    gather = Gather(gathered, loads, sends, arrivals)
+
+    def locate(k, s, start, size):
+        rows, columns = pl.multiple_of(start, size), pl.multiple_of(s * SHARD, SHARD)
+        return gathered.at[k, pl.ds(rows, size), pl.ds(columns, SHARD)]
+
+    gather = Gather(locate, WIDE, loads, sends, arrivals)
     shard, part = lax.axis_index("fsdp"), lax.axis_index("ctx")
     others = ({"fsdp": flipped(shard, 1)}, {"fsdp": flipped(shard, 2)}, {"fsdp": flipped(flipped(shard, 1), 2)})
     following, outer = lax.rem(part + 1, PARTS), lax.rem(part + PARTS - 1 + 2 * lax.rem(part, 2), PARTS)
@@ -261,8 +265,8 @@
         return remote(edges.at[k], halos.at[k], edge_sends.at[k], edge_arrivals.at[k], {"ctx": following})
 
     def store(k):
-        columns = pl.ds(pl.multiple_of(k * WIDE, WIDE), WIDE)
-        return pltpu.make_async_copy(gathered.at[k], weight_ref.at[:, :, columns], stores.at[k])
+        rows = pl.ds(pl.multiple_of(k * WIDE, WIDE), WIDE)
+        return pltpu.make_async_copy(gathered.at[k], weight_ref.at[rows], stores.at[k])
 
     @pl.when(step == 0)
     def _():
@@ -271,7 +275,7 @@
         for peer in near:
             pl.semaphore_signal(barrier, inc=1, device_id=peer, device_id_type=pl.DeviceIdType.MESH)
         for k in range(chunks):
-            gather.load(k, main_ref.at[:, k * WIDE : (k + 1) * WIDE] if k + 1 < chunks else rest_ref).start()
+            gather.load(k, main_ref.at[k * WIDE : (k + 1) * WIDE, :] if k + 1 < chunks else rest_ref).start()
         own_small[...] = small_ref[...]
         own_seg[...] = seg_ref[...]
         smalls[shard] = small_ref[...]
@@ -315,7 +319,7 @@
     def _(k):
         gather.complete(k)
         store(k).start()
-        low = dot(normed[...], gathered[k].reshape(D, WIDE)).astype(BF16)
+        low = dot_nt(normed[...], gathered[k]).astype(BF16)
         projected_ref[...] = low
         edges[k] = low[length - 16 :, :].astype(F32)[8:, :]
         edge_copy(k).start()
@@ -331,7 +335,8 @@
 def project(in_matrix, units, small, seg_ids):
     length = units.shape[0]
     chunks = WIDTH // WIDE
-    rest = jnp.pad(in_matrix[:, (chunks - 1) * WIDE :], ((0, 0), (0, WIDTH - PROJ)))
+    turned = in_matrix.T
+    rest = jnp.pad(turned[(chunks - 1) * WIDE :], ((0, WIDTH - PROJ), (0, 0)))
     whole = lambda *shape: pl.BlockSpec(shape, lambda t: (0,) * len(shape))
     column = lambda lag: lambda t: (0, jnp.clip(t - lag, 0, chunks - 1))
     anywhere = pl.BlockSpec(memory_space=pl.ANY)
@@ -354,7 +359,7 @@
             whole(length // 128, 128),
         ],
         out_shape=[
-            jax.ShapeDtypeStruct((4, SHARD, WIDTH), BF16),
+            jax.ShapeDtypeStruct((WIDTH, D), BF16),
             jax.ShapeDtypeStruct((length, WIDTH), BF16),
             jax.ShapeDtypeStruct((4, SHARD, length), BF16),
             jax.ShapeDtypeStruct((4, 8, SMALL_WIDTH), F32),
@@ -363,7 +368,7 @@
         ],
         scratch_shapes=[
             pltpu.VMEM((length, D), BF16),
-            pltpu.VMEM((chunks, 4, SHARD, WIDE), BF16),
+            pltpu.VMEM((chunks, WIDE, D), BF16),
             pltpu.VMEM((8, SMALL_WIDTH), F32),
             pltpu.VMEM((4, 8, SMALL_WIDTH), F32),
             pltpu.VMEM((length // 128, 128), jnp.int32),
@@ -379,7 +384,7 @@
         ],
         compiler_params=communicating(3, True),
         name="project",
-    )(in_matrix, rest, units, small, seg_ids.reshape(length // 128, 128))
+    )(turned, rest, units, small, seg_ids.reshape(length // 128, 128))
 
 
 PARTS = 8
@@ -470,7 +475,13 @@
     if parts:
         exchange = Exchange(*parts[:5])
         own_keep, keeps, keep_sends, keep_arrivals, gathered, loads, sends, arrivals, stores = parts[5:]
-        gather = Gather(gathered, loads, sends, arrivals)
+        gather = Gather(
+            lambda k, s, start, size: gathered.at[k, s, pl.ds(pl.multiple_of(start, size), size)],
+            gathered.shape[2],
+            loads,
+            sends,
+            arrivals,
+        )
 
         def store(k):
             columns = pl.ds(pl.multiple_of(k * WIDE, WIDE), WIDE)
@@ -858,13 +869,13 @@
     )(y, xs, projected, incoming, kept, out_whole, c_rows, entering, heads, gain, cot, units)
 
 
-def back_kernel(
-    x_ref, dtraw_ref, halo_ref, taps_ref, heads_ref, seg_ref, row_ref, b_ref, c_ref, dt_ref, run_ref,
-    dy_ref, sin_ref, dout_ref, given_ref,
-    dproj_ref, dhalo_ref, dtaps_ref, dheads_ref,
-    ext, pre, dact, dbuf, scores, dscores, run_t, b_t, c_t, enter, leave, d_b, d_c, suffix, prefix, d_dt, fixed, states,
-):
-    step = pl.program_id(0)
+def back_steps(step, given, scratch, write, write_halo, write_taps, write_heads):
+    (
+        x_ref, dtraw_ref, halo_ref, taps_ref, heads_ref, seg_ref, row_ref, b_ref, c_ref, dt_ref, run_ref, dy_ref, sin_ref, dout_ref,
+    ) = given
+    (
+        ext, pre, dact, dbuf, scores, dscores, run_t, b_t, c_t, enter, leave, d_b, d_c, suffix, prefix, d_dt, fixed, states,
+    ) = scratch
     length = x_ref.shape[0]
     chunks = length // Q
 
@@ -988,7 +999,7 @@
                 if shift:
                     term = jnp.where(both(seg_ref[at : at + Q, :] == own), term, 0.0)
                 sums[3 - shift] = sums[3 - shift] + jnp.sum(term, axis=0, keepdims=True)
-        dtaps_ref[...] = jnp.concatenate(sums + [jnp.zeros((3, BLK), F32)], axis=0)
+        write_taps(jnp.concatenate(sums + [jnp.zeros((3, BLK), F32)], axis=0))
 
         def returned(at, rows):
             own = seg_ref[at : at + rows, :]
@@ -1000,9 +1011,9 @@
                 )
             return result
 
-        dhalo_ref[...] = returned(0, PAD)
+        write_halo(returned(0, PAD))
         for k in range(chunks):
-            dproj_ref[k * Q : (k + 1) * Q, :] = returned(PAD + k * Q, Q).astype(BF16)
+            write(slice(k * Q, (k + 1) * Q), returned(PAD + k * Q, Q).astype(BF16))
 
     @pl.when(step == STEPS + 1)
     def _():
@@ -1021,39 +1032,78 @@
             d_raw = jnp.where(lane < HEADS, (d_dt[rows, :] - rate * d_log) * sigmoid(raw), 0.0)
             bias_sum = bias_sum + jnp.sum(d_raw, axis=0, keepdims=True)
             decay_sum = decay_sum - jnp.sum(d_log * dt_ref[rows, :] * rate, axis=0, keepdims=True)
-            dproj_ref[rows, :] = jnp.concatenate([d_raw, jnp.zeros_like(d_raw)], axis=1).astype(BF16)
-        dheads_ref[...] = jnp.concatenate([bias_sum, decay_sum, jnp.zeros((6, 128), F32)], axis=0)
-
-
-def back(projected, halo, taps, heads, seg_lanes, seg_row, b_rows, c_rows, dt, running, dy, incoming, outgoing, given):
-    length = projected.shape[0]
+            write(rows, jnp.concatenate([d_raw, jnp.zeros_like(d_raw)], axis=1).astype(BF16))
+        write_heads(jnp.concatenate([bias_sum, decay_sum, jnp.zeros((6, 128), F32)], axis=0))
+
+
+def back_kernel(*refs):
+    given, (_, dproj_ref, dhalo_ref, dtaps_ref, dheads_ref), scratch = refs[:14], refs[14:19], refs[19:]
+
+    def write(rows, value):
+        dproj_ref[rows, :] = value
+
+    def write_halo(value):
+        dhalo_ref[...] = value
+
+    def write_taps(value):
+        dtaps_ref[...] = value
+
+    def write_heads(value):
+        dheads_ref[...] = value
+
+    back_steps(pl.program_id(0), given, scratch, write, write_halo, write_taps, write_heads)
+
+
+def back_scratch(length):
+    return [
+        pltpu.VMEM((length + PAD, BLK), F32),
+        pltpu.VMEM((length, BLK), F32),
+        pltpu.VMEM((length, BLK), F32),
+        pltpu.VMEM((length + 2 * PAD, BLK), F32),
+        pltpu.VMEM((length, Q), F32),
+        pltpu.VMEM((length, Q), F32),
+        pltpu.VMEM((length // Q, 128, Q), F32),
+        pltpu.VMEM((128, length), BF16),
+        pltpu.VMEM((128, length), BF16),
+        *[pltpu.VMEM((length, 128), F32) for _ in range(7)],
+        pltpu.VMEM((8 * (length // Q), 128), F32),
+        pltpu.VMEM((length // Q, STATE, BLK), F32),
+    ]
+
+
+def back_inputs(length):
     whole = lambda *shape: pl.BlockSpec(shape, lambda j: (0,) * len(shape))
+    upto = lambda last, first=0: lambda j: (0, first + jnp.minimum(j, last))
+    return [
+        pl.BlockSpec((length, BLK), upto(STEPS, STEPS)),
+        pl.BlockSpec((length, BLK), lambda j: (0, 2 * STEPS + 1)),
+        pl.BlockSpec((PAD, BLK), upto(STEPS, STEPS)),
+        pl.BlockSpec((8, BLK), upto(STEPS)),
+        whole(8, 128),
+        whole(length + 2 * PAD, 128),
+        whole(8, length),
+        whole(length, 128),
+        whole(length, 128),
+        whole(length, 128),
+        whole(length, 128),
+        pl.BlockSpec((length, BLK), upto(STEPS - 1)),
+        pl.BlockSpec((STATE, BLK), upto(STEPS - 1)),
+        pl.BlockSpec((STATE, BLK), upto(STEPS - 1)),
+    ]
+
+
+def back(given, dproj):
+    length = dproj.shape[0]
     upto = lambda last, first=0: lambda j: (0, first + jnp.minimum(j, last))
     return pl.pallas_call(
         back_kernel,
         grid=(STEPS + 2,),
-        in_specs=[
-            pl.BlockSpec((length, BLK), upto(STEPS, STEPS)),
-            pl.BlockSpec((length, BLK), lambda j: (0, 2 * STEPS + 1)),
-            pl.BlockSpec((PAD, BLK), upto(STEPS, STEPS)),
-            pl.BlockSpec((8, BLK), upto(STEPS)),
-            whole(8, 128),
-            whole(length + 2 * PAD, 128),
-            whole(8, length),
-            whole(length, 128),
-            whole(length, 128),
-            whole(length, 128),
-            whole(length, 128),
-            pl.BlockSpec((length, BLK), upto(STEPS - 1)),
-            pl.BlockSpec((STATE, BLK), upto(STEPS - 1)),
-            pl.BlockSpec((STATE, BLK), upto(STEPS - 1)),
-            pl.BlockSpec(memory_space=pl.ANY),
-        ],
+        in_specs=[*back_inputs(length), pl.BlockSpec(memory_space=pl.ANY)],
         out_specs=[
             pl.BlockSpec((length, BLK), lambda j: (0, STEPS + j)),
             pl.BlockSpec((PAD, BLK), upto(STEPS)),
             pl.BlockSpec((8, BLK), upto(STEPS)),
-            whole(8, 128),
+            pl.BlockSpec((8, 128), lambda j: (0, 0)),
         ],
         out_shape=[
             jax.ShapeDtypeStruct((length, WIDTH), BF16),
@@ -1061,51 +1111,45 @@
             jax.ShapeDtypeStruct((8, XBC), F32),
             jax.ShapeDtypeStruct((8, 128), F32),
         ],
-        scratch_shapes=[
-            pltpu.VMEM((length + PAD, BLK), F32),
-            pltpu.VMEM((length, BLK), F32),
-            pltpu.VMEM((length, BLK), F32),
-            pltpu.VMEM((length + 2 * PAD, BLK), F32),
-            pltpu.VMEM((length, Q), F32),
-            pltpu.VMEM((length, Q), F32),
-            pltpu.VMEM((length // Q, 128, Q), F32),
-            pltpu.VMEM((128, length), BF16),
-            pltpu.VMEM((128, length), BF16),
-            pltpu.VMEM((length, 128), F32),
-            pltpu.VMEM((length, 128), F32),
-            pltpu.VMEM((length, 128), F32),
-            pltpu.VMEM((length, 128), F32),
-            pltpu.VMEM((length, 128), F32),
-            pltpu.VMEM((length, 128), F32),
-            pltpu.VMEM((length, 128), F32),
-            pltpu.VMEM((8 * (length // Q), 128), F32),
-            pltpu.VMEM((length // Q, STATE, BLK), F32),
-        ],
+        scratch_shapes=back_scratch(length),
         input_output_aliases={14: 0},
         compiler_params=pltpu.CompilerParams(vmem_limit_bytes=VMEM_LIMIT),
-        cost_estimate=pl.CostEstimate(
-            flops=12 * 10**9, bytes_accessed=30 * 10**6, transcendentals=2 * 10**7
-        ),
         name="back",
-    )(
-        projected, projected, halo, taps, heads, seg_lanes, seg_row, b_rows, c_rows, dt, running, dy, incoming, outgoing, given
-    )
+    )(*given, dproj)
 
 
 OUT_CHUNKS = 2 * D // WIDE
+GATE_CHUNKS = INNER // WIDE
 IN_CHUNKS = WIDTH // WIDE
 CHUNKS = OUT_CHUNKS + IN_CHUNKS
 LAGS = 8
-SMALL_ROWS = 168
-
-
-def reduce_kernel(
-    lhs_in, lhs_out, rhs_in, rhs_out, small_ref,
-    din_ref, dout_ref, total_ref,
-    own, core_send, core_recv, y_recv, x_recv, z_recv, w_recv, final, small_send, small_recv,
-    send_sems, recv_sems, small_send_sems, small_recv_sems,
-):
+RING = 8
+
+
+def small_sums(taps, columns, input_gain, heads, stats):
+    fill = lambda width: jnp.zeros((1, width), F32)
+    squares = [jnp.broadcast_to(jnp.sum(stats[i : i + 1], axis=1, keepdims=True), (1, 128)) for i in range(2)]
+    return jnp.concatenate(
+        [
+            taps[:5],
+            jnp.concatenate([columns[0:1], fill(XBC - INNER)], axis=1),
+            jnp.concatenate([columns[1:2], fill(XBC - INNER)], axis=1),
+            jnp.concatenate([input_gain, heads[0:1], heads[1:2], *squares, fill(XBC - D - 512)], axis=1),
+        ],
+        axis=0,
+    )
+
+
+def finish_kernel(*refs):
+    given, refs = refs[:14], refs[14:]
+    lhs_in, lhs_out, gate_ref, weight_ref, cot_ref, units_ref, gain_ref, columns_ref, stats_ref = refs[:9]
+    din_ref, dout_ref, input_grad_ref, total_ref = refs[9:13]
+    scratch, refs = refs[13:31], refs[31:]
+    grads, edges, halos, taps, heads, d_normed = refs[:6]
+    own, core_send, core_recv, y_recv, x_recv, z_recv, w_recv, final, small_send, small_recv = refs[6:16]
+    send_sems, recv_sems, small_send_sems, small_recv_sems, edge_sends, edge_arrivals = refs[16:]
     step = pl.program_id(0)
+    length = cot_ref.shape[0]
     shard, part = lax.axis_index("fsdp"), lax.axis_index("ctx")
     core, y = lax.rem(shard, 2), shard // 2
     x, z = lax.rem(part, 2), part // 2
@@ -1117,63 +1161,58 @@
         {"ctx": flipped(part, 2)},
         {"ctx": flipped(part, 4)},
     )
-
-    def sent(stage, k, source, target, peer):
+    preceding, outer = lax.rem(part + PARTS - 1, PARTS), lax.rem(part + PARTS - 1 + 2 * lax.rem(part, 2), PARTS)
+
+    def remote(source, target, send, arrival, peer):
         return pltpu.make_async_remote_copy(
             src_ref=source,
             dst_ref=target,
-            send_sem=send_sems.at[stage, k],
-            recv_sem=recv_sems.at[stage, k],
-            device_id=peers[peer],
+            send_sem=send,
+            recv_sem=arrival,
+            device_id=peer,
             device_id_type=pl.DeviceIdType.MESH,
         )
 
+    def ring(k):
+        return lax.rem(k, RING)
+
+    def sent(stage, k, source, target, peer):
+        return remote(source, target, send_sems.at[stage, k], recv_sems.at[stage, k], peers[peer])
+
     copies = (
-        lambda k: sent(0, k, core_send.at[lax.rem(k, 2)], core_recv.at[k], 0),
-        lambda k: sent(1, k, core_recv.at[k, 1 - y], y_recv.at[k], 1),
-        lambda k: sent(2, k, y_recv.at[k, 1 - x], x_recv.at[k], 2),
-        lambda k: sent(3, k, x_recv.at[k, 1 - near], z_recv.at[k], 3),
-        lambda k: sent(4, k, z_recv.at[k, 1 - far], w_recv.at[k], 4),
-        lambda k: sent(5, k, final.at[k, x, near, far], final.at[k, x, near, far], 4),
-        lambda k: sent(6, k, final.at[k, x, near], final.at[k, x, near], 3),
-        lambda k: sent(7, k, final.at[k, x], final.at[k, x], 2),
+        lambda k: sent(0, k, core_send.at[lax.rem(k, 2)], core_recv.at[ring(k)], 0),
+        lambda k: sent(1, k, core_recv.at[ring(k), 1 - y], y_recv.at[ring(k)], 1),
+        lambda k: sent(2, k, y_recv.at[ring(k), 1 - x], x_recv.at[ring(k)], 2),
+        lambda k: sent(3, k, x_recv.at[ring(k), 1 - near], z_recv.at[ring(k)], 3),
+        lambda k: sent(4, k, z_recv.at[ring(k), 1 - far], w_recv.at[ring(k)], 4),
+        lambda k: sent(5, k, final.at[ring(k), x, near, far], final.at[ring(k), x, near, far], 4),
+        lambda k: sent(6, k, final.at[ring(k), x, near], final.at[ring(k), x, near], 3),
+        lambda k: sent(7, k, final.at[ring(k), x], final.at[ring(k), x], 2),
     )
     arrivals = copies[:5] + (
-        lambda k: sent(5, k, final.at[k, x, near, 1 - far], final.at[k, x, near, 1 - far], 4),
-        lambda k: sent(6, k, final.at[k, x, 1 - near], final.at[k, x, 1 - near], 3),
-        lambda k: sent(7, k, final.at[k, 1 - x], final.at[k, 1 - x], 2),
+        lambda k: sent(5, k, final.at[ring(k), x, near, 1 - far], final.at[ring(k), x, near, 1 - far], 4),
+        lambda k: sent(6, k, final.at[ring(k), x, 1 - near], final.at[ring(k), x, 1 - near], 3),
+        lambda k: sent(7, k, final.at[ring(k), 1 - x], final.at[ring(k), 1 - x], 2),
     )
 
     def small_copy(stage):
-        return pltpu.make_async_remote_copy(
-            src_ref=small_send.at[stage],
-            dst_ref=small_recv.at[stage],
-            send_sem=small_send_sems.at[stage],
-            recv_sem=small_recv_sems.at[stage],
-            device_id=peers[stage],
-            device_id_type=pl.DeviceIdType.MESH,
+        return remote(
+            small_send.at[stage], small_recv.at[stage], small_send_sems.at[stage], small_recv_sems.at[stage], peers[stage]
         )
 
+    def edge_copy(block):
+        return remote(
+            edges.at[block], halos.at[block], edge_sends.at[block], edge_arrivals.at[block], {"ctx": preceding}
+        )
+
     @pl.when(step == 0)
     def _():
         barrier = pltpu.get_barrier_semaphore()
-        for peer in peers:
+        greeted = [*peers, {"ctx": outer}]
+        for peer in greeted:
             pl.semaphore_signal(barrier, inc=1, device_id=peer, device_id_type=pl.DeviceIdType.MESH)
-        pl.semaphore_wait(barrier, len(peers))
-        small_send[0] = small_ref[...]
-        small_copy(0).start()
-
-    for stage in range(5):
-
-        @pl.when(step == stage + 1)
-        def _():
-            small_copy(stage).wait()
-            total = small_send[stage] + small_recv[stage]
-            if stage < 4:
-                small_send[stage + 1] = total
-                small_copy(stage + 1).start()
-            else:
-                total_ref[...] = total
+        pl.semaphore_wait(barrier, len(greeted))
+        d_normed[...] = jnp.zeros_like(d_normed)
 
     def partial(lhs_of, rhs):
         for row in range(2):
@@ -1183,19 +1222,55 @@
         for row in range(2):
             own[row] = dot(lhs_of(2 * row + core), rhs).reshape(2, 2, 2, PIECE, WIDE)
 
+    def in_chunk(rhs):
+        partial(lambda s: lhs_in[s], rhs)
+        d_normed[...] += dot(rhs, weight_ref[...])
+
     @pl.when(step < OUT_CHUNKS)
     def _():
-        partial(lambda s: lhs_out[s, step // (D // WIDE)], rhs_out[...])
-
-    @pl.when((step >= OUT_CHUNKS) & (step < CHUNKS))
-    def _():
-        partial(lambda s: lhs_in[s], rhs_in[...])
+        columns = lax.rem(step, D // WIDE) * WIDE
+        rhs = cot_ref[:, pl.ds(pl.multiple_of(columns, WIDE), WIDE)]
+        partial(lambda s: lhs_out[s, step // (D // WIDE)], rhs)
+
+    @pl.when((step >= OUT_CHUNKS) & (step < OUT_CHUNKS + GATE_CHUNKS))
+    def _():
+        in_chunk(gate_ref[...])
+
+    @pl.when((step >= OUT_CHUNKS + GATE_CHUNKS) & (step < CHUNKS))
+    def _():
+        first = 2 * (step - OUT_CHUNKS - GATE_CHUNKS)
+        for block in (first, first + 1):
+
+            @pl.when(block <= STEPS)
+            def _():
+                edge_copy(block).wait()
+                tail = slice(length - 16, length)
+                more = jnp.where(part == PARTS - 1, 0.0, halos[block])
+                more = jnp.concatenate([jnp.zeros_like(more), more], axis=0)
+                grads[block, tail, :] = (grads[block, tail, :].astype(F32) + more).astype(BF16)
+
+        in_chunk(jnp.concatenate([grads[first], grads[first + 1]], axis=1))
+
+    def write(rows, value):
+        grads[step, rows, :] = value
+
+    def write_halo(value):
+        edges[step] = value
+        edge_copy(step).start()
+
+    def write_taps(value):
+        taps[step] = value
+
+    def write_heads(value):
+        heads[...] = value
+
+    back_steps(step, given, scratch, write, write_halo, write_taps, write_heads)
 
     @pl.when(step < CHUNKS)
     def _():
         arrivals[0](step).wait_recv()
         for row in (1 - y, y):
-            core_recv[step, row] = (own[row] + core_recv[step, row].astype(F32)).astype(BF16)
+            core_recv[ring(step), row] = (own[row] + core_recv[ring(step), row].astype(F32)).astype(BF16)
         copies[1](step).start()
 
     def stage(lag):
@@ -1204,7 +1279,7 @@
 
             @pl.when((k >= 0) & (k < CHUNKS))
             def _():
-                body(k)
+                body(k, ring(k))
 
         return decorate
 
@@ -1212,47 +1287,50 @@
         return (a.astype(F32) + b.astype(F32)).astype(BF16)
 
     @stage(1)
-    def _(k):
+    def _(k, at):
         arrivals[1](k).wait_recv()
-        kept = core_recv.at[k, y]
-        y_recv[k] = summed(y_recv[k], kept[...])
+        y_recv[at] = summed(y_recv[at], core_recv[at, y])
         copies[2](k).start()
         copies[0](k).wait_send()
 
     @stage(2)
-    def _(k):
+    def _(k, at):
         arrivals[2](k).wait_recv()
-        x_recv[k] = summed(x_recv[k], y_recv[k, x])
+        x_recv[at] = summed(x_recv[at], y_recv[at, x])
         copies[3](k).start()
 
     @stage(3)
-    def _(k):
+    def _(k, at):
         arrivals[3](k).wait_recv()
-        z_recv[k] = summed(z_recv[k], x_recv[k, near])
+        z_recv[at] = summed(z_recv[at], x_recv[at, near])
         copies[4](k).start()
+        copies[1](k).wait_send()
 
     @stage(4)
-    def _(k):
+    def _(k, at):
         arrivals[4](k).wait_recv()
-        final[k, x, near, far] = summed(w_recv[k], z_recv[k, far])
+        final[at, x, near, far] = summed(w_recv[at], z_recv[at, far])
         copies[5](k).start()
+        copies[2](k).wait_send()
 
     @stage(5)
-    def _(k):
+    def _(k, at):
         arrivals[5](k).wait_recv()
         copies[6](k).start()
+        copies[3](k).wait_send()
 
     @stage(6)
-    def _(k):
+    def _(k, at):
         arrivals[6](k).wait_recv()
         copies[7](k).start()
+        copies[4](k).wait_send()
 
     @stage(7)
-    def _(k):
+    def _(k, at):
         arrivals[7](k).wait_recv()
-        for one in range(1, 8):
+        for one in (5, 6, 7):
             copies[one](k).wait_send()
-        whole = final[k].reshape(SHARD, WIDE)
+        whole = final[at].reshape(SHARD, WIDE)
 
         @pl.when(k < OUT_CHUNKS)
         def _():
@@ -1260,40 +1338,85 @@
 
         @pl.when(k >= OUT_CHUNKS)
         def _():
-            din_ref[...] = whole
-
-
-def reduce(part_t, mixer_t, dproj, cot, small):
+            din_ref[...] = whole.astype(F32).T.astype(BF16)
+
+    @pl.when(step == CHUNKS)
+    def _():
+        input_gain = jnp.zeros((1, D), F32)
+        for k in range(length // Q):
+            rows = slice(k * Q, (k + 1) * Q)
+            units = units_ref[rows, :].astype(F32)
+            norm = lax.rsqrt(jnp.sum(units * units, axis=1, keepdims=True) * (1.0 / D) + epsilon)
+            base = units * norm
+            grad = d_normed[rows, :]
+            input_gain = input_gain + jnp.sum(grad * base, axis=0, keepdims=True)
+            scaled = grad * gain_ref[0:1, :]
+            mean = jnp.sum(scaled * base, axis=1, keepdims=True) * (1.0 / D)
+            input_grad_ref[rows, :] = (cot_ref[rows, :].astype(F32) + norm * (scaled - base * mean)).astype(BF16)
+        whole = jnp.concatenate([taps[block] for block in range(STEPS + 1)], axis=1)
+        small_send[0] = small_sums(whole, columns_ref[...], input_gain, heads[...], stats_ref[...])
+        small_copy(0).start()
+
+    for stage_of_small in range(5):
+
+        @pl.when(step == CHUNKS + 1 + stage_of_small)
+        def _():
+            small_copy(stage_of_small).wait()
+            total = small_send[stage_of_small] + small_recv[stage_of_small]
+            if stage_of_small < 4:
+                small_send[stage_of_small + 1] = total
+                small_copy(stage_of_small + 1).start()
+            else:
+                total_ref[...] = total
+
+
+def finish(given, normed_t, mixer_t, dproj, w_turned, cot, units, input_gain, column_sums, stats):
     length = cot.shape[0]
     per_half = D // WIDE
-    whole = lambda *shape: pl.BlockSpec(shape, lambda t: (0,) * len(shape))
+    once = pl.Buffered(1)
+    whole = lambda *shape: pl.BlockSpec(shape, lambda t: (0,) * len(shape), pipeline_mode=once)
+    in_chunk = lambda t: jnp.clip(t - OUT_CHUNKS, 0, IN_CHUNKS - 1)
 
     def out_block(t):
         k = jnp.clip(t - LAGS + 1, 0, OUT_CHUNKS - 1)
         return (k // per_half, lax.rem(k, per_half))
 
-    slots = lambda *shape: pltpu.VMEM((CHUNKS, *shape, PIECE, WIDE), BF16)
+    slots = lambda *shape: pltpu.VMEM((RING, *shape, PIECE, WIDE), BF16)
     return pl.pallas_call(
-        reduce_kernel,
+        finish_kernel,
         grid=(CHUNKS + LAGS - 1,),
         in_specs=[
+            *back_inputs(length),
             whole(4, SHARD, length),
             whole(4, 2, SHARD, length),
-            pl.BlockSpec((length, WIDE), lambda t: (0, jnp.clip(t - OUT_CHUNKS, 0, IN_CHUNKS - 1))),
-            pl.BlockSpec((length, WIDE), lambda t: (0, lax.rem(jnp.minimum(t, OUT_CHUNKS - 1), per_half))),
-            whole(SMALL_ROWS, 128),
+            pl.BlockSpec((length, WIDE), lambda t: (0, jnp.minimum(in_chunk(t), GATE_CHUNKS - 1))),
+            pl.BlockSpec((WIDE, D), lambda t: (in_chunk(t), 0)),
+            whole(length, D),
+            whole(length, D),
+            whole(1, D),
+            whole(8, INNER),
+            whole(8, D),
         ],
         out_specs=[
-            pl.BlockSpec((SHARD, WIDE), lambda t: (0, jnp.clip(t - LAGS + 1 - OUT_CHUNKS, 0, IN_CHUNKS - 1))),
+            pl.BlockSpec((WIDE, SHARD), lambda t: (in_chunk(t - LAGS + 1), 0)),
             pl.BlockSpec((SHARD, WIDE), out_block),
-            whole(SMALL_ROWS, 128),
+            pl.BlockSpec((length, D), lambda t: (0, 0)),
+            pl.BlockSpec((8, XBC), lambda t: (0, 0)),
         ],
         out_shape=[
-            jax.ShapeDtypeStruct((SHARD, PROJ), BF16),
+            jax.ShapeDtypeStruct((PROJ, SHARD), BF16),
             jax.ShapeDtypeStruct((2 * SHARD, D), BF16),
-            jax.ShapeDtypeStruct((SMALL_ROWS, 128), F32),
+            jax.ShapeDtypeStruct((length, D), BF16),
+            jax.ShapeDtypeStruct((8, XBC), F32),
         ],
         scratch_shapes=[
+            *back_scratch(length),
+            pltpu.VMEM((STEPS + 2, length, BLK), BF16),
+            pltpu.VMEM((STEPS + 1, PAD, BLK), F32),
+            pltpu.VMEM((STEPS + 1, PAD, BLK), F32),
+            pltpu.VMEM((STEPS + 1, 8, BLK), F32),
+            pltpu.VMEM((8, 128), F32),
+            pltpu.VMEM((length, D), F32),
             pltpu.VMEM((2, 2, 2, 2, PIECE, WIDE), F32),
             pltpu.VMEM((2, 2, 2, 2, 2, PIECE, WIDE), BF16),
             slots(2, 2, 2, 2),
@@ -1302,18 +1425,18 @@
             slots(2),
             slots(),
             slots(2, 2, 2),
-            pltpu.VMEM((5, SMALL_ROWS, 128), F32),
-            pltpu.VMEM((5, SMALL_ROWS, 128), F32),
+            pltpu.VMEM((5, 8, XBC), F32),
+            pltpu.VMEM((5, 8, XBC), F32),
             pltpu.SemaphoreType.DMA((8, CHUNKS)),
             pltpu.SemaphoreType.DMA((8, CHUNKS)),
             pltpu.SemaphoreType.DMA((5,)),
             pltpu.SemaphoreType.DMA((5,)),
-        ],
-        compiler_params=pltpu.CompilerParams(
-            vmem_limit_bytes=VMEM_LIMIT, collective_id=0, has_side_effects=True
-        ),
-        name="reduce",
-    )(part_t, mixer_t, dproj, cot, small)
+            pltpu.SemaphoreType.DMA((STEPS + 1,)),
+            pltpu.SemaphoreType.DMA((STEPS + 1,)),
+        ],
+        compiler_params=communicating(0, True),
+        name="finish",
+    )(*given, normed_t, mixer_t, dproj, w_turned, cot, units, input_gain, column_sums, stats)
 
 
 def passed_along(block, axis, distance):
@@ -1371,19 +1494,18 @@
     shards, parts = lax.axis_size("fsdp"), lax.axis_size("ctx")
     place = lax.axis_index("ctx")
     units_low, cot = inputs[0], out_grad[0]
-    units = units_low.astype(F32)
     seg_ids = segment_ids[0]
-    length = units.shape[0]
+    length = units_low.shape[0]
     here = (shards, parts) == (4, PARTS)
     small = pack_small(conv_taps, conv_bias, dt_bias, decay_log, skip_scale, mixer_gain, input_gain)
-    inv_rms = lax.rsqrt(jnp.mean(units * units, axis=-1, keepdims=True) + epsilon)
-    base_rows = units * inv_rms
     if here:
-        w_whole, projected, normed_t, smalls, halo, seg_before = project(in_matrix, units_low, small, seg_ids)
-        w_whole = w_whole.reshape(D, WIDTH)
+        w_turned, projected, normed_t, smalls, halo, seg_before = project(in_matrix, units_low, small, seg_ids)
         rim_seg = seg_before.reshape(length)[length - CONV + 1 :]
         taps, gain, g_float, heads = unpack_small(smalls, conv_bias.shape[0])
     else:
+        units = units_low.astype(F32)
+        inv_rms = lax.rsqrt(jnp.mean(units * units, axis=-1, keepdims=True) + epsilon)
+        base_rows = units * inv_rms
         w_whole = jnp.pad(in_matrix, ((0, 0), (0, WIDTH - PROJ)))
         w_whole = lax.all_gather(w_whole, "fsdp", axis=0, tiled=True)
         rim_seg = passed_along(seg_ids[length - CONV + 1 :], "ctx", 1)
@@ -1417,72 +1539,56 @@
     )
     if not here:
         outgoing = joined_plainly(lax.all_gather(outgoing, "ctx"), kept, place, False)
-    dproj, d_halo, d_taps, d_heads = back(
-        projected, halo, taps, heads, seg_lanes, seg_row, b_rows, c_rows, dt, running, dy, incoming, outgoing, dproj
+    given = (
+        projected, projected, halo, taps, heads, seg_lanes, seg_row, b_rows, c_rows, dt, running, dy, incoming, outgoing,
     )
-    returned = passed_along(d_halo.astype(BF16), "ctx", -1)
-    last = lax.slice(dproj, (length - PAD, INNER), (length, INNER + XBC))
-    last = (last.astype(F32) + returned.astype(F32)).astype(BF16)
-    dproj = lax.dynamic_update_slice(dproj, last, (length - PAD, INNER))
-
-    d_normed = dot_nt(dproj, w_whole)
-    d_input_gain = jnp.sum(d_normed * base_rows, axis=0)
-    d_base = d_normed * g_float
-    d_units = inv_rms * (d_base - base_rows * jnp.mean(d_base * base_rows, axis=-1, keepdims=True))
-    input_grad = (cot.astype(F32) + d_units).astype(BF16)
-
-    row = jnp.concatenate(
-        [
-            d_taps[:5].reshape(-1),
-            column_sums[0],
-            d_input_gain,
-            d_heads[0, :HEADS],
-            d_heads[1, :HEADS],
-            jnp.sum(column_sums[1].reshape(HEADS, HDIM), axis=1),
-            jnp.sum(stats[:2], axis=1),
-        ]
-    )
-    row = jnp.pad(row, (0, SMALL_ROWS * 128 - row.shape[0])).reshape(SMALL_ROWS, 128)
     if here:
-        d_in, d_out, row = reduce(normed_t, mixer_t.reshape(4, 2, SHARD, length), dproj, cot, row)
-        d_in, d_out = d_in.astype(F32), d_out.astype(F32)
+        d_in, d_out, input_grad, total = finish(
+            given, normed_t, mixer_t.reshape(4, 2, SHARD, length), dproj, w_turned, cot, units_low, g_float, column_sums, stats
+        )
+        d_in, d_out = d_in.T.astype(F32), d_out.astype(F32)
     else:
+        dproj, d_halo, d_taps, d_heads = back(given, dproj)
+        returned = passed_along(d_halo.astype(BF16), "ctx", -1)
+        last = lax.slice(dproj, (length - PAD, INNER), (length, INNER + XBC))
+        last = (last.astype(F32) + returned.astype(F32)).astype(BF16)
+        dproj = lax.dynamic_update_slice(dproj, last, (length - PAD, INNER))
+        d_normed = dot_nt(dproj, w_whole)
+        d_input_gain = jnp.sum(d_normed * base_rows, axis=0)
+        d_base = d_normed * g_float
+        d_units = inv_rms * (d_base - base_rows * jnp.mean(d_base * base_rows, axis=-1, keepdims=True))
+        input_grad = (cot.astype(F32) + d_units).astype(BF16)
+
+        def scattered(grad):
+            return lax.psum_scatter(grad.astype(BF16), "fsdp", scatter_dimension=0, tiled=True)
+
         d_in = jnp.dot(normed_t, dproj, preferred_element_type=F32)[:, :PROJ]
         d_out = jnp.dot(mixer_t, cot, preferred_element_type=F32)
-
-        def scattered(grad):
-            return lax.psum_scatter(grad.astype(BF16), "fsdp", scatter_dimension=0, tiled=True)
-
         d_in = lax.psum(scattered(d_in), "ctx").astype(F32)
         d_out = lax.psum(scattered(d_out), "ctx").astype(F32)
-        row = lax.psum(row, ("fsdp", "ctx"))
-    row = row.reshape(-1)
+        total = lax.psum(small_sums(d_taps, column_sums, d_input_gain[None], d_heads, stats), ("fsdp", "ctx"))
     me = lax.axis_index("fsdp")
 
     def own(flat):
         size = flat.shape[-1] // shards
         return lax.dynamic_slice_in_dim(flat, me * size, size, flat.ndim - 1)
 
-    at = 5 * XBC
-    taps_sum = row[:at].reshape(5, XBC)
-    gain_sum = row[at : at + INNER]
-    input_gain_sum = row[at + INNER : at + INNER + D]
-    at = at + INNER + D
-    head_sums = row[at : at + 3 * HEADS].reshape(3, HEADS)
-    stat_sums = row[at + 3 * HEADS : at + 3 * HEADS + 2]
+    skip_sums = jnp.sum(total[6, :INNER].reshape(HEADS, HDIM), axis=1)
+    at = D + 256
+    stat_sums = jnp.stack([total[7, at], total[7, at + 128]])
     rms_stats = jnp.sqrt(stat_sums / (length * shards * parts * D))
     return (
         block_out[None],
         input_grad[None],
         d_in,
         d_out,
-        own(taps_sum[:4]).T,
-        own(taps_sum[4]),
-        own(head_sums[0]),
-        own(head_sums[1]),
-        own(head_sums[2]),
-        own(gain_sum),
-        own(input_gain_sum),
+        own(total[:4]).T,
+        own(total[4]),
+        own(total[7, D : D + HEADS]),
+        own(total[7, D + 128 : D + 128 + HEADS]),
+        own(skip_sums),
+        own(total[5, :INNER]),
+        own(total[7, :D]),
         rms_stats,
     )
 

time: 548 us -> 452 us (0.82)
  Pallas kernels: 471 us -> 411 us
  matrix products: 18.2 us -> 0 us
  local copies, waits for them, and re-layouts: 40.7 us -> 26.1 us
    pallas_call x2 -> x1, Pallas kernels: 273 us -> 215 us  [finish(): pl.pallas_call(finish_kernel, grid=(CHUNKS + LAGS - 1,), in_specs=[*back_...]
    dot_general x1 -> x0, matrix products: 18.2 us -> none  [dot_nt(): lax.dot_general(a, b, (((1,), (1,)), ((), ())), preferred_element_type=F32)]
    unnamed x11 -> x10, local copies, waits for them, and re-layouts: 16.5 us -> 3.13 us
  transfers between devices with their start and end apart: 1 -> 0, of which waited for: 0 -> 0; matrix products, arithmetic and copies ran while one was open for 1% -> 0% of each run, Pallas kernels for 0% -> 0%
where the time goes in v5:
time: 452 us; the launch traced here: 451 us
  Pallas kernels  411 us (91%)
  local copies, waits for them, and re-layouts  26.1 us (6%)
  other arithmetic  12.6 us (3%)
    pallas_call x1, Pallas kernels, finish(): pl.pallas_call(finish_kernel, grid=(CHUNKS + LAGS - 1,), in_specs=[*back_...  215 us
    pallas_call x1, Pallas kernels, project(): pl.pallas_call(project_kernel, grid=(chunks + 4,), in_specs=[anywhere, an...  71.3 us
    pallas_call x1, Pallas kernels, front(): pl.pallas_call(front_kernel, grid=(STEPS + DONE * exchanging,), in_specs=...  65.2 us
    pallas_call x1, Pallas kernels, tail(): pl.pallas_call(tail_kernel, grid=(2 * STEPS + DONE * exchanging,), in_spe...  60.2 us
    convert_element_type x2, other arithmetic, on_device(): d_in, d_out = (d_in.T.astype(F32), d_out.astype(F32))  9.18 us

profile of v5, /device:TPU:0, one launch (start us, length us, event | category | flops | bytes accessed | tf_op | source)
XLA Modules:
  0.0 450.9 jit_solution(15337280478254492170)
XLA Ops:
  0.6 0.8 fusion.4
  1.4 0.7 pad.35
  2.1 0.7 pad.36
  2.8 0.7 broadcast_in_dim.29
  3.5 0.7 concatenate.10
  4.8 1.3 broadcast_in_dim.34.row_ref.refs_6_
  6.1 1.0 slice.60
  7.1 0.8 pad.34.rest_ref
  7.9 71.3 %project.1 = (bf16[6656,1536]{1,0:T(8,128)(2,1)}, bf16[512,6656]{1,0:T(8,128)(2,1)}, bf16[4,384,512]{2,1,0:T(8,128)(2,1)}, f32[4,8,896]{2,1,0:T(8,128)}, f32[8,6656]{1,0:T(8,128)}, /*index=5*/s32[4,128]{1,0:T(4,128)}) custom-call(bf16[6448,384]{1,0:T(8,128)(2,1)} %bitcast.30, bf16[512,384]{1,0:T(8,128)(2,1)} %pad.34.rest_ref, bf16[512,1536]{1,0:T(8,128)(2,1)} %bitcast.26, ...), custom_call_target="tpu_custom_call" | custom-call | tf_op jit(solution)/shard_map/project/pallas_call | solution.py:343
  79.2 0.8 slice.48
  80.0 0.7 slice_reduce_fusion.1
  81.6 1.4 slice.64
  83.0 0.9 slice.63
  83.9 0.9 copy.26
  86.3 0.8 broadcast_in_dim.33.seg_ref.refs_5_
  87.1 65.2 %front.1 = (bf16[512,3072]{1,0:T(8,128)(2,1)}, bf16[512,3072]{1,0:T(8,128)(2,1)}, bf16[128,3072]{1,0:T(8,128)(2,1)}, bf16[512,128]{1,0:T(8,128)(2,1)}, bf16[512,...) custom-call(bf16[512,6656]{1,0:T(8,128)(2,1)} %get-tuple-element.39., ...), custom_call_target="tpu_custom_call" | custom-call | flops 6000000000 | bytes 16000000 | tf_op jit(solution)/shard_map/front/pallas_call | solution.py:630
  152.3 60.2 %tail.1 = (bf16[3072,512]{1,0:T(8,128)(2,1)}, bf16[512,6656]{1,0:T(8,128)(2,1)}, bf16[512,3072]{1,0:T(8,128)(2,1)}, bf16[128,3072]{1,0:T(8,128)(2,1)}, f32[8,307...) custom-call(bf16[512,3072]{1,0:T(8,128)(2,1)} %get-tuple-element.43.y_ref, ...), custom_call_target="tpu_custom_call" | custom-call | flops 12000000000 | bytes 50000000 | tf_op jit(solution)/shard_map/tail/pallas_call | solution.py:820
  212.5 214.7 %finish.1 = (bf16[6448,384]{1,0:T(8,128)(2,1)}, bf16[768,1536]{1,0:T(8,128)(2,1)}, bf16[512,1536]{1,0:T(8,128)(2,1)}, f32[8,3328]{1,0:T(8,128)}) custom-call(bf16[512,6656]{1,0:T(8,128)(2,1)} %get-tuple-element.39.x_ref.bc_ref.dtraw_ref.gate_ref.refs_0_.refs_1_, bf16[512,6656]{1,0:T(8,128)(2,1)} %get-tuple-element.39.x_ref.bc_ref.dtraw_ref.gate_ref.refs_0_.refs_1_, ...), custom_call_target="tpu_custom_call" | custom-call | tf_op jit(solution)/shard_map/finish/pallas_call | solution.py:1385
  427.2 1.2 fusion.8
  428.4 1.9 fusion.7
  430.3 0.7 fusion.10
  431.6 0.8 slice.57
  433.0 0.9 slice.52
  433.9 0.7 dynamic-slice_reduce_fusion
  434.6 1.0 fusion.9
  435.6 0.9 slice.51
  436.5 0.7 dynamic-slice_bitcast_fusion
  438.6 4.6 %convert_element_type.28 = f32[768,1536]{1,0:T(8,128)} convert(bf16[768,1536]{1,0:T(8,128)(2,1)} %get-tuple-element.64) | non-fusion elementwise | flops 1179648 | bytes 7077888 | tf_op jit(solution)/shard_map/convert_element_type | solution.py:1549
  443.2 4.5 %convert_bitcast_fusion = f32[384,6448]{0,1:T(8,128)} fusion(bf16[6448,384]{1,0:T(8,128)(2,1)S(1)} %copy-done), kind=kLoop, calls=%fused_computation | loop fusion | flops 2476032 | bytes 14856192 | tf_op jit(solution)/shard_map/convert_element_type | solution.py:1549
  447.8 1.1 copy.30
  448.9 0.8 copy-done.2
  449.7 1.1 copy.31
  (27 shorter events, 5.5 us)
Async XLA Ops:
  7.9 72.9 %copy-start.3 = (s32[1,512]{1,0:T(1,128)S(1)}, s32[1,512]{1,0:T(1,128)}, u32[]{:S(2)}) copy-start(s32[1,512]{1,0:T(1,128)} %param.13) | copy-start | bytes 6148
  438.6 4.7 %copy-start = (bf16[6448,384]{1,0:T(8,128)(2,1)S(1)}, bf16[6448,384]{1,0:T(8,128)(2,1)}, u32[]{:S(2)}) copy-start(bf16[6448,384]{1,0:T(8,128)(2,1)} %get-tuple-element.63) | copy-start | bytes 14856196
  443.2 4.5 %copy-start.1 = (bf16[512,1536]{1,0:T(8,128)(2,1)S(1)}, bf16[512,1536]{1,0:T(8,128)(2,1)}, u32[]{:S(2)}) copy-start(bf16[512,1536]{1,0:T(8,128)(2,1)} %get-tuple-element.50) | copy-start | bytes 4718596
  447.8 2.0 copy-start.2

commit v6 on v5

--- a/solution.py
+++ b/solution.py
@@ -34,9 +34,7 @@
 VMEM_LIMIT = 60 * 1024 * 1024
 
 
-def communicating(number, exchanging):
-    if not exchanging:
-        return pltpu.CompilerParams(vmem_limit_bytes=VMEM_LIMIT)
+def communicating(number):
     return pltpu.CompilerParams(
         vmem_limit_bytes=VMEM_LIMIT, collective_id=number, has_side_effects=True
     )
@@ -112,6 +110,17 @@
     row = row_ref[0:1, k * Q : (k + 1) * Q]
     keep = (own == row) & (iota((Q, Q), 1) <= iota((Q, Q), 0))
     return jnp.where(keep, dot_nt(c_rows, b_rows), 0.0)
+
+
+def remote(source, target, send, arrival, peer):
+    return pltpu.make_async_remote_copy(
+        src_ref=source,
+        dst_ref=target,
+        send_sem=send,
+        recv_sem=arrival,
+        device_id=peer,
+        device_id_type=pl.DeviceIdType.MESH,
+    )
 
 
 def flipped(index, bit):
@@ -226,167 +235,6 @@
     ]
 
 
-def project_kernel(
-    main_ref, rest_ref, units_ref, small_ref, seg_ref,
-    weight_ref, projected_ref, normed_t_ref, smalls_ref, halo_ref, seg_before_ref,
-    normed, gathered, own_small, smalls, own_seg, seg_before, edges, halos,
-    loads, sends, arrivals, stores, small_sends, small_arrivals, edge_sends, edge_arrivals,
-):
-    step = pl.program_id(0)
-    chunks = WIDTH // WIDE
-    length = units_ref.shape[0]
-
-    def locate(k, s, start, size):
-        rows, columns = pl.multiple_of(start, size), pl.multiple_of(s * SHARD, SHARD)
-        return gathered.at[k, pl.ds(rows, size), pl.ds(columns, SHARD)]
-
-    gather = Gather(locate, WIDE, loads, sends, arrivals)
-    shard, part = lax.axis_index("fsdp"), lax.axis_index("ctx")
-    others = ({"fsdp": flipped(shard, 1)}, {"fsdp": flipped(shard, 2)}, {"fsdp": flipped(flipped(shard, 1), 2)})
-    following, outer = lax.rem(part + 1, PARTS), lax.rem(part + PARTS - 1 + 2 * lax.rem(part, 2), PARTS)
-
-    def remote(source, target, send, arrival, peer):
-        return pltpu.make_async_remote_copy(
-            src_ref=source,
-            dst_ref=target,
-            send_sem=send,
-            recv_sem=arrival,
-            device_id=peer,
-            device_id_type=pl.DeviceIdType.MESH,
-        )
-
-    def small_copy(hop):
-        return remote(own_small, smalls.at[shard], small_sends.at[hop], small_arrivals.at[hop], others[hop])
-
-    def seg_copy():
-        return remote(own_seg, seg_before, small_sends.at[3], small_arrivals.at[3], {"ctx": following})
-
-    def edge_copy(k):
-        return remote(edges.at[k], halos.at[k], edge_sends.at[k], edge_arrivals.at[k], {"ctx": following})
-
-    def store(k):
-        rows = pl.ds(pl.multiple_of(k * WIDE, WIDE), WIDE)
-        return pltpu.make_async_copy(gathered.at[k], weight_ref.at[rows], stores.at[k])
-
-    @pl.when(step == 0)
-    def _():
-        barrier = pltpu.get_barrier_semaphore()
-        near = [*others, {"ctx": flipped(part, 1)}, {"ctx": flipped(part, 2)}, {"ctx": outer}]
-        for peer in near:
-            pl.semaphore_signal(barrier, inc=1, device_id=peer, device_id_type=pl.DeviceIdType.MESH)
-        for k in range(chunks):
-            gather.load(k, main_ref.at[k * WIDE : (k + 1) * WIDE, :] if k + 1 < chunks else rest_ref).start()
-        own_small[...] = small_ref[...]
-        own_seg[...] = seg_ref[...]
-        smalls[shard] = small_ref[...]
-        pl.semaphore_wait(barrier, len(near))
-        for hop in range(3):
-            small_copy(hop).start()
-        seg_copy().start()
-        for k in range(AHEAD):
-            gather.begin(k)
-        for hop in range(3):
-            small_copy(hop).wait()
-        seg_copy().wait()
-        smalls_ref[...] = smalls[...]
-        seg_before_ref[...] = jnp.where(part == 0, -1, seg_before[...])
-        gain = jnp.concatenate([smalls[s, 6:7, :SHARD] for s in range(4)], axis=1)
-        for k in range(length // Q):
-            rows = slice(k * Q, (k + 1) * Q)
-            units = units_ref[rows, :].astype(F32)
-            norm = lax.rsqrt(jnp.sum(units * units, axis=1, keepdims=True) * (1.0 / D) + epsilon)
-            value = units * norm * gain
-            normed[rows, :] = value.astype(BF16)
-            for s in range(4):
-                normed_t_ref[s, :, rows] = value[:, s * SHARD : (s + 1) * SHARD].T.astype(BF16)
-
-    def stage(lag):
-        def decorate(body):
-            k = step - lag
-
-            @pl.when((k >= 0) & (k < chunks))
-            def _():
-                body(k)
-
-        return decorate
-
-    stage(-AHEAD)(lambda k: pl.when(k >= AHEAD)(lambda: gather.begin(k)))
-    stage(0)(gather.first)
-    stage(1)(gather.second)
-    stage(2)(gather.third)
-
-    @stage(3)
-    def _(k):
-        gather.complete(k)
-        store(k).start()
-        low = dot_nt(normed[...], gathered[k]).astype(BF16)
-        projected_ref[...] = low
-        edges[k] = low[length - 16 :, :].astype(F32)[8:, :]
-        edge_copy(k).start()
-
-    @stage(4)
-    def _(k):
-        edge_copy(k).wait()
-        gather.drain(k)
-        store(k).wait()
-        halo_ref[...] = jnp.where(part == 0, 0.0, halos[k])
-
-
-def project(in_matrix, units, small, seg_ids):
-    length = units.shape[0]
-    chunks = WIDTH // WIDE
-    turned = in_matrix.T
-    rest = jnp.pad(turned[(chunks - 1) * WIDE :], ((0, WIDTH - PROJ), (0, 0)))
-    whole = lambda *shape: pl.BlockSpec(shape, lambda t: (0,) * len(shape))
-    column = lambda lag: lambda t: (0, jnp.clip(t - lag, 0, chunks - 1))
-    anywhere = pl.BlockSpec(memory_space=pl.ANY)
-    return pl.pallas_call(
-        project_kernel,
-        grid=(chunks + 4,),
-        in_specs=[
-            anywhere,
-            anywhere,
-            whole(length, D),
-            whole(8, SMALL_WIDTH),
-            whole(length // 128, 128),
-        ],
-        out_specs=[
-            anywhere,
-            pl.BlockSpec((length, WIDE), column(3)),
-            whole(4, SHARD, length),
-            whole(4, 8, SMALL_WIDTH),
-            pl.BlockSpec((PAD, WIDE), column(4)),
-            whole(length // 128, 128),
-        ],
-        out_shape=[
-            jax.ShapeDtypeStruct((WIDTH, D), BF16),
-            jax.ShapeDtypeStruct((length, WIDTH), BF16),
-            jax.ShapeDtypeStruct((4, SHARD, length), BF16),
-            jax.ShapeDtypeStruct((4, 8, SMALL_WIDTH), F32),
-            jax.ShapeDtypeStruct((PAD, WIDTH), F32),
-            jax.ShapeDtypeStruct((length // 128, 128), jnp.int32),
-        ],
-        scratch_shapes=[
-            pltpu.VMEM((length, D), BF16),
-            pltpu.VMEM((chunks, WIDE, D), BF16),
-            pltpu.VMEM((8, SMALL_WIDTH), F32),
-            pltpu.VMEM((4, 8, SMALL_WIDTH), F32),
-            pltpu.VMEM((length // 128, 128), jnp.int32),
-            pltpu.VMEM((length // 128, 128), jnp.int32),
-            pltpu.VMEM((chunks, PAD, WIDE), F32),
-            pltpu.VMEM((chunks, PAD, WIDE), F32),
-            *gather_sems(chunks),
-            pltpu.SemaphoreType.DMA((chunks,)),
-            pltpu.SemaphoreType.DMA((4,)),
-            pltpu.SemaphoreType.DMA((4,)),
-            pltpu.SemaphoreType.DMA((chunks,)),
-            pltpu.SemaphoreType.DMA((chunks,)),
-        ],
-        compiler_params=communicating(3, True),
-        name="project",
-    )(turned, rest, units, small, seg_ids.reshape(length // 128, 128))
-
-
 PARTS = 8
 SLAB = STATE // PARTS
 JOIN, DONE = 2, 4
@@ -464,127 +312,62 @@
     return result.astype(BF16)
 
 
+def prepare(
+    bc_ref, dt_raw, halo_bc_ref, taps_bc_ref, heads_ref, seg_ref, row_ref, b_ref, c_ref, dt_ref, run_ref, in_ref,
+    ext, scores, run_t, b_t, enter, leave,
+):
+    chunks = bc_ref.shape[0] // Q
+    ext[0:PAD, :] = halo_bc_ref[...]
+    ext[PAD:, :] = bc_ref[...].astype(F32)
+    lane = iota((Q, 128), 1)
+    lower = (iota((Q, Q), 1) <= iota((Q, Q), 0)).astype(F32)
+    offset = jnp.zeros((1, 128), F32)
+    for k in range(chunks):
+        rows = slice(k * Q, (k + 1) * Q)
+        total = conv_rows(ext, seg_ref, taps_bc_ref, k * Q, Q)
+        active = total * sigmoid(total)
+        b_rows, c_rows = active[:, :STATE], active[:, STATE:].astype(BF16)
+        b_t[:, rows] = b_rows.T.astype(BF16)
+        b_rows = b_rows.astype(BF16)
+        b_ref[rows, :] = b_rows
+        c_ref[rows, :] = c_rows
+        scores[rows, :] = masked_scores(seg_ref, row_ref, b_rows, c_rows, k)
+        raw = jnp.where(lane < HEADS, dt_raw(rows).astype(F32), 0.0) + heads_ref[0:1, :]
+        dt = jnp.maximum(raw, 0.0) + jnp.log1p(jnp.exp(-jnp.abs(raw)))
+        log_decay = -dt * jnp.exp(heads_ref[1:2, :])
+        running = jnp.dot(lower, log_decay, precision=HIGHEST, preferred_element_type=F32)
+        dt_ref[rows, :] = dt
+        run_ref[rows, :] = running
+        run_t[k] = running.T
+        carry, tail = chunk_flags(seg_ref, k)
+        enter[rows, :] = jnp.exp(running) * carry
+        leave[rows, :] = jnp.exp(running[Q - 1 : Q, :] - running) * tail
+        same = (seg_ref[PAD + k * Q : PAD + (k + 1) * Q, :] == seg_ref[PAD - 1 : PAD, :]).astype(F32)
+        whole = jnp.exp(running + offset) * same
+        in_ref[rows, :] = whole
+        offset = offset + running[Q - 1 : Q, :]
+    return jnp.broadcast_to(whole[Q - 1 : Q, :], (8, 128))
+
+
 def front_kernel(
-    x_ref, bc_ref, dtraw_ref, halo_ref, halo_bc_ref, taps_ref, taps_bc_ref, heads_ref, seg_ref, row_ref, shard_ref,
-    xs_ref, y_ref, state_ref, b_ref, c_ref, dt_ref, run_ref, in_ref, keep_ref, whole_ref,
-    ext, scores, run_t, b_t, enter, leave, *parts,
+    x_ref, bc_ref, dtraw_ref, halo_ref, halo_bc_ref, taps_ref, taps_bc_ref, heads_ref, seg_ref, row_ref,
+    xs_ref, y_ref, state_ref, b_ref, c_ref, dt_ref, run_ref, in_ref, keep_ref,
+    ext, scores, run_t, b_t, enter, leave,
 ):
     step = pl.program_id(0)
-    length = x_ref.shape[0]
-    chunks = length // Q
-    if parts:
-        exchange = Exchange(*parts[:5])
-        own_keep, keeps, keep_sends, keep_arrivals, gathered, loads, sends, arrivals, stores = parts[5:]
-        gather = Gather(
-            lambda k, s, start, size: gathered.at[k, s, pl.ds(pl.multiple_of(start, size), size)],
-            gathered.shape[2],
-            loads,
-            sends,
-            arrivals,
+
+    @pl.when(step == 0)
+    def _():
+        keep_ref[...] = prepare(
+            bc_ref, lambda rows: dtraw_ref[rows, :128], halo_bc_ref, taps_bc_ref, heads_ref, seg_ref, row_ref,
+            b_ref, c_ref, dt_ref, run_ref, in_ref, ext, scores, run_t, b_t, enter, leave,
         )
 
-        def store(k):
-            columns = pl.ds(pl.multiple_of(k * WIDE, WIDE), WIDE)
-            return pltpu.make_async_copy(gathered.at[k], whole_ref.at[:, :, columns], stores.at[k])
-
-
-        def keep_copy(hop):
-            return pltpu.make_async_remote_copy(
-                src_ref=own_keep,
-                dst_ref=keeps.at[exchange.me],
-                send_sem=keep_sends.at[hop],
-                recv_sem=keep_arrivals.at[hop],
-                device_id={"ctx": lax.rem(exchange.me + hop + 1, PARTS)},
-                device_id_type=pl.DeviceIdType.MESH,
-            )
-
-    @pl.when(step == 0)
-    def _():
-        ext[0:PAD, :] = halo_bc_ref[...]
-        ext[PAD:, :] = bc_ref[...].astype(F32)
-        lane = iota((Q, 128), 1)
-        lower = (iota((Q, Q), 1) <= iota((Q, Q), 0)).astype(F32)
-        offset = jnp.zeros((1, 128), F32)
-        for k in range(chunks):
-            rows = slice(k * Q, (k + 1) * Q)
-            total = conv_rows(ext, seg_ref, taps_bc_ref, k * Q, Q)
-            active = total * sigmoid(total)
-            b_rows, c_rows = active[:, :STATE], active[:, STATE:].astype(BF16)
-            b_t[:, rows] = b_rows.T.astype(BF16)
-            b_rows = b_rows.astype(BF16)
-            b_ref[rows, :] = b_rows
-            c_ref[rows, :] = c_rows
-            scores[rows, :] = masked_scores(seg_ref, row_ref, b_rows, c_rows, k)
-            raw = jnp.where(lane < HEADS, dtraw_ref[rows, :128].astype(F32), 0.0) + heads_ref[0:1, :]
-            dt = jnp.maximum(raw, 0.0) + jnp.log1p(jnp.exp(-jnp.abs(raw)))
-            log_decay = -dt * jnp.exp(heads_ref[1:2, :])
-            running = jnp.dot(lower, log_decay, precision=HIGHEST, preferred_element_type=F32)
-            dt_ref[rows, :] = dt
-            run_ref[rows, :] = running
-            run_t[k] = running.T
-            carry, tail = chunk_flags(seg_ref, k)
-            enter[rows, :] = jnp.exp(running) * carry
-            leave[rows, :] = jnp.exp(running[Q - 1 : Q, :] - running) * tail
-            same = (seg_ref[PAD + k * Q : PAD + (k + 1) * Q, :] == seg_ref[PAD - 1 : PAD, :]).astype(F32)
-            whole = jnp.exp(running + offset) * same
-            in_ref[rows, :] = whole
-            offset = offset + running[Q - 1 : Q, :]
-        keep = jnp.broadcast_to(whole[Q - 1 : Q, :], (8, 128))
-        if parts:
-            own_keep[...] = keep
-            keeps[exchange.me] = keep
-            exchange.greet(gather.peers["core"], gather.peers["y"])
-            for hop in range(PARTS - 1):
-                keep_copy(hop).start()
-            for k in range(D // WIDE):
-                gather.load(k, shard_ref.at[:, k * WIDE : (k + 1) * WIDE]).start()
-            for k in range(D // WIDE):
-                gather.begin(k)
-        else:
-            keep_ref[0] = keep
-
-    @pl.when(step < STEPS)
-    def _():
-        state = local_scan(
-            step, x_ref, halo_ref, taps_ref, seg_ref, xs_ref, y_ref, c_ref, dt_ref, run_ref,
-            ext, scores, run_t, b_t, enter, leave,
-        )
-        if parts:
-            exchange.spread(step, state)
-        else:
-            state_ref[...] = state.astype(BF16)
-
-    if parts:
-
-        @pl.when(step == JOIN)
-        def _():
-            for hop in range(PARTS - 1):
-                keep_copy(hop).wait()
-            keep_ref[...] = keeps[...]
-
-        @pl.when((step >= JOIN) & (step < STEPS + JOIN))
-        def _():
-            group = step - JOIN
-            exchange.join(group, widen(first_rows(keeps), chosen(group)), True)
-
-        @pl.when(step >= DONE)
-        def _():
-            state_ref[...] = exchange.finish(step - DONE)
-
-        def complete(k):
-            gather.complete(k)
-            store(k).start()
-
-        def drain(k):
-            gather.drain(k)
-            store(k).wait()
-
-        for lag, advance in enumerate((gather.first, gather.second, gather.third, complete, drain)):
-            k = step - 2 - 2 * lag
-
-            @pl.when((k >= 0) & (k < D // WIDE))
-            def _():
-                advance(k)
+    state = local_scan(
+        step, x_ref, halo_ref, taps_ref, seg_ref, xs_ref, y_ref, c_ref, dt_ref, run_ref,
+        ext, scores, run_t, b_t, enter, leave,
+    )
+    state_ref[...] = state.astype(BF16)
 
 
 def local_scan(
@@ -621,98 +404,361 @@
     return state
 
 
-def front(projected, halo, taps, heads, seg_lanes, seg_row, out_matrix, exchanging):
+def front_outputs(length, column, state_at):
+    whole = lambda *shape: (pl.BlockSpec(shape, lambda j: (0, 0)), shape)
+    columns = lambda rows, at: (pl.BlockSpec((rows, BLK), at), (rows, INNER))
+    specs = [
+        (columns(length, column), BF16),
+        (columns(length, column), BF16),
+        (columns(STATE, state_at), BF16),
+        (whole(length, 128), BF16),
+        (whole(length, 128), BF16),
+        (whole(length, 128), F32),
+        (whole(length, 128), F32),
+        (whole(length, 128), F32),
+    ]
+    return [spec for (spec, _), _ in specs], [jax.ShapeDtypeStruct(shape, kind) for (_, shape), kind in specs]
+
+
+def front_scratch(length):
+    return [
+        pltpu.VMEM((length + PAD, BLK), F32),
+        pltpu.VMEM((length, Q), F32),
+        pltpu.VMEM((length // Q, 128, Q), F32),
+        pltpu.VMEM((128, length), BF16),
+        pltpu.VMEM((length, 128), F32),
+        pltpu.VMEM((length, 128), F32),
+    ]
+
+
+def front(projected, halo, taps, heads, seg_lanes, seg_row):
     length = projected.shape[0]
-    last = STEPS - 1
-    keeps = PARTS if exchanging else 1
     whole = lambda *shape: pl.BlockSpec(shape, lambda j: (0,) * len(shape))
     columns = lambda rows, at: pl.BlockSpec((rows, BLK), at)
+    out_specs, out_shape = front_outputs(length, lambda j: (0, j), lambda j: (0, j))
     return pl.pallas_call(
         front_kernel,
-        grid=(STEPS + DONE * exchanging,),
+        grid=(STEPS,),
         in_specs=[
-            columns(length, lambda j: (0, STEPS + jnp.minimum(j, last))),
+            columns(length, lambda j: (0, STEPS + j)),
             columns(length, lambda j: (0, 2 * STEPS)),
             columns(length, lambda j: (0, 2 * STEPS + 1)),
-            columns(PAD, lambda j: (0, STEPS + jnp.minimum(j, last))),
+            columns(PAD, lambda j: (0, STEPS + j)),
             columns(PAD, lambda j: (0, 2 * STEPS)),
-            columns(8, lambda j: (0, jnp.minimum(j, last))),
+            columns(8, lambda j: (0, j)),
             columns(8, lambda j: (0, STEPS)),
             whole(8, 128),
             whole(length + 2 * PAD, 128),
             whole(8, length),
-            pl.BlockSpec(memory_space=pl.ANY),
+        ],
+        out_specs=[*out_specs, whole(8, 128)],
+        out_shape=[*out_shape, jax.ShapeDtypeStruct((8, 128), F32)],
+        scratch_shapes=front_scratch(length),
+        compiler_params=pltpu.CompilerParams(vmem_limit_bytes=VMEM_LIMIT),
+        name="front",
+    )(projected, projected, projected, halo, halo, taps, taps, heads, seg_lanes, seg_row)
+
+
+ORDER = (2 * INNER // WIDE, *range(INNER // WIDE, 2 * INNER // WIDE), *range(INNER // WIDE))
+MULTIPLY = 3
+SCAN = MULTIPLY + 2
+OUT_PIECES = D // WIDE
+SLOTS = SCAN + STEPS + DONE
+
+
+def chunk_at(position):
+    half = INNER // WIDE
+    return jnp.where(position == 0, 2 * half, jnp.where(position <= half, position - 1 + half, position - 1 - half))
+
+
+def forward_kernel(*refs):
+    main_ref, rest_ref, shard_ref, units_ref, small_ref, seg_own_ref, row_ref = refs[:7]
+    xs_ref, y_ref, state_ref, b_ref, c_ref, dt_ref, run_ref, in_ref = refs[7:15]
+    keep_ref, weight_ref, whole_ref, projected_ref, normed_t_ref = refs[15:20]
+    halo_ref, taps_ref, heads_ref, gain_ref, input_gain_ref, seg_ref = refs[20:26]
+    ext, scores, run_t, b_t, enter, leave = refs[26:32]
+    exchange = Exchange(*refs[32:37])
+    own_keep, keeps, keep_sends, keep_arrivals = refs[37:41]
+    gathered, loads, sends, arrivals, stores = refs[41:46]
+    out_gathered, out_loads, out_sends, out_arrivals, out_stores = refs[46:51]
+    normed, blocks, taps, own_small, smalls, seg_tail, seg_head = refs[51:58]
+    edges, halos, small_sends, small_arrivals, edge_sends, edge_arrivals = refs[58:]
+    step = pl.program_id(0)
+    length = units_ref.shape[0]
+    shard, part = lax.axis_index("fsdp"), lax.axis_index("ctx")
+    others = ({"fsdp": flipped(shard, 1)}, {"fsdp": flipped(shard, 2)}, {"fsdp": flipped(flipped(shard, 1), 2)})
+    following = {"ctx": lax.rem(part + 1, PARTS)}
+
+    def place_in(k, s, start, size):
+        rows, columns = pl.multiple_of(start, size), pl.multiple_of(s * SHARD, SHARD)
+        return gathered.at[k, pl.ds(rows, size), pl.ds(columns, SHARD)]
+
+    def place_out(k, s, start, size):
+        return out_gathered.at[k, s, pl.ds(pl.multiple_of(start, size), size)]
+
+    gather = Gather(place_in, WIDE, loads, sends, arrivals)
+    gather_out = Gather(place_out, 2 * SHARD, out_loads, out_sends, out_arrivals)
+
+    def small_copy(hop):
+        return remote(own_small, smalls.at[shard], small_sends.at[hop], small_arrivals.at[hop], others[hop])
+
+    def seg_copy():
+        return remote(seg_tail, seg_head, small_sends.at[3], small_arrivals.at[3], following)
+
+    def edge_copy(k):
+        return remote(edges.at[k], halos.at[k], edge_sends.at[k], edge_arrivals.at[k], following)
+
+    def keep_copy(hop):
+        peer = {"ctx": lax.rem(part + hop + 1, PARTS)}
+        return remote(own_keep, keeps.at[part], keep_sends.at[hop], keep_arrivals.at[hop], peer)
+
+    def store(k):
+        rows = pl.ds(pl.multiple_of(chunk_at(k) * WIDE, WIDE), WIDE)
+        return pltpu.make_async_copy(gathered.at[k], weight_ref.at[rows], stores.at[k])
+
+    def store_out(k):
+        columns = pl.ds(pl.multiple_of(k * WIDE, WIDE), WIDE)
+        return pltpu.make_async_copy(out_gathered.at[k], whole_ref.at[:, :, columns], out_stores.at[k])
+
+    @pl.when(step == 0)
+    def _():
+        for k, chunk in enumerate(ORDER):
+            source = rest_ref if (chunk + 1) * WIDE > PROJ else main_ref.at[chunk * WIDE : (chunk + 1) * WIDE, :]
+            gather.load(k, source).start()
+        for k in range(OUT_PIECES):
+            gather_out.load(k, shard_ref.at[:, k * WIDE : (k + 1) * WIDE]).start()
+        own_small[...] = small_ref[...]
+        smalls[shard] = small_ref[...]
+        seg_tail[...] = seg_own_ref[length - PAD :, :]
+        exchange.greet(*others)
+        for hop in range(3):
+            small_copy(hop).start()
+        seg_copy().start()
+        for k in range(AHEAD):
+            gather.begin(k)
+        for hop in range(3):
+            small_copy(hop).wait()
+        seg_copy().wait()
+        seg_ref[0:PAD, :] = jnp.where(part == 0, -1, seg_head[...])
+        seg_ref[PAD : PAD + length, :] = seg_own_ref[...]
+        seg_ref[PAD + length :, :] = jnp.full((PAD, 128), -2, jnp.int32)
+        gain = jnp.concatenate([smalls[s, 6:7, :SHARD] for s in range(4)], axis=1)
+        input_gain_ref[...] = gain
+        for k in range(length // Q):
+            rows = slice(k * Q, (k + 1) * Q)
+            units = units_ref[rows, :].astype(F32)
+            norm = lax.rsqrt(jnp.sum(units * units, axis=1, keepdims=True) * (1.0 / D) + epsilon)
+            normed[rows, :] = (units * norm * gain).astype(BF16)
+
+    @pl.when(step == 1)
+    def _():
+        mixer_gain = jnp.concatenate([smalls[s, 5:6, : INNER // 4] for s in range(4)], axis=1)
+        gain_ref[...] = jnp.broadcast_to(mixer_gain, (8, INNER))
+        whole = jnp.zeros((8, XBC), F32)
+        heads = jnp.zeros((8, 128), F32)
+        row, lane = iota((8, 128), 0), iota((8, 128), 1)
+        own = HEADS // 4
+        for s in range(4):
+            padded = jnp.concatenate([smalls[s], jnp.zeros((8, XBC - SMALL_WIDTH), F32)], axis=1)
+            padded = jnp.where(iota((8, XBC), 1) < XBC // 4, padded, 0.0)
+            whole = whole + (pltpu.roll(padded, s * (XBC // 4), 1) if s else padded)
+            line = jnp.broadcast_to(smalls[s, 7:8, :128], (8, 128))
+            inside = (lane >= s * own) & (lane < (s + 1) * own)
+            for kind in range(3):
+                shift = (s - kind) * own % 128
+                moved = pltpu.roll(line, shift, 1) if shift else line
+                heads = jnp.where(inside & (row == kind), moved, heads)
+        taps_ref[...] = whole
+        heads_ref[...] = heads
+        for block in range(STEPS + 1):
+            taps[block] = whole[:, block * BLK : (block + 1) * BLK]
+
+    def stage(lag, count=len(ORDER)):
+        def decorate(body):
+            k = step - lag
+
+            @pl.when((k >= 0) & (k < count))
+            def _():
+                body(k)
+
+        return decorate
+
+    stage(-AHEAD)(lambda k: pl.when(k >= AHEAD)(lambda: gather.begin(k)))
+    stage(6, OUT_PIECES)(gather_out.begin)
+    stage(0)(gather.first)
+    stage(1)(gather.second)
+    stage(2)(gather.third)
+    stage(12, OUT_PIECES)(gather_out.first)
+    stage(13, OUT_PIECES)(gather_out.second)
+    stage(14, OUT_PIECES)(gather_out.third)
+
+    @stage(MULTIPLY)
+    def _(k):
+        gather.complete(k)
+        store(k).start()
+        low = dot_nt(normed[...], gathered[k]).astype(BF16)
+        projected_ref[...] = low
+        edge = low[length - 16 :, :].astype(F32)[8:, :]
+        for half in range(2):
+            columns = slice(half * BLK, (half + 1) * BLK)
+            blocks[2 * chunk_at(k) + half] = low[:, columns]
+            edges[k, half] = edge[:, columns]
+        edge_copy(k).start()
+
+    @stage(MULTIPLY + 1)
+    def _(k):
+        edge_copy(k).wait()
+        gather.drain(k)
+        store(k).wait()
+        for half in range(2):
+            columns = slice(half * BLK, (half + 1) * BLK)
+            halos[k, half] = jnp.where(part == 0, 0.0, halos[k, half])
+            halo_ref[:, columns] = halos[k, half]
+
+    @pl.when(step == SCAN - 1)
+    def _():
+        keep = prepare(
+            blocks.at[2 * STEPS], lambda rows: blocks[2 * STEPS + 1, rows, :128], halos.at[0, 0], taps.at[STEPS], heads_ref,
+            seg_ref, row_ref, b_ref, c_ref, dt_ref, run_ref, in_ref, ext, scores, run_t, b_t, enter, leave,
+        )
+        own_keep[...] = keep
+        keeps[part] = keep
+        for hop in range(PARTS - 1):
+            keep_copy(hop).start()
+
+    @stage(SCAN, STEPS)
+    def _(j):
+        state = local_scan(
+            j, blocks.at[STEPS + j], halos.at[1 + j // 2, lax.rem(j, 2)], taps.at[j], seg_ref,
+            xs_ref, y_ref, c_ref, dt_ref, run_ref, ext, scores, run_t, b_t, enter, leave,
+        )
+        exchange.spread(j, state)
+
+    @pl.when(step == SCAN + JOIN)
+    def _():
+        for hop in range(PARTS - 1):
+            keep_copy(hop).wait()
+        keep_ref[...] = keeps[...]
+
+    @stage(SCAN + JOIN, STEPS)
+    def _(j):
+        exchange.join(j, widen(first_rows(keeps), chosen(j)), True)
+
+    @stage(SCAN + DONE, STEPS)
+    def _(j):
+        state_ref[...] = exchange.finish(j)
+
+    @stage(16, OUT_PIECES)
+    def _(k):
+        gather_out.complete(k)
+        store_out(k).start()
+
+    @stage(18, OUT_PIECES)
+    def _(k):
+        gather_out.drain(k)
+        store_out(k).wait()
+
+    @pl.when(step == SLOTS - 1)
+    def _():
+        for s in range(4):
+            columns = slice(s * SHARD, (s + 1) * SHARD)
+            normed_t_ref[s] = normed[:, columns].astype(F32).T.astype(BF16)
+
+
+def forward(in_matrix, out_matrix, units, small, seg_own, seg_row):
+    length = units.shape[0]
+    chunks = len(ORDER)
+    turned = in_matrix.T
+    rest = jnp.pad(turned[(chunks - 1) * WIDE :], ((0, WIDTH - PROJ), (0, 0)))
+    whole = lambda *shape: pl.BlockSpec(shape, lambda t: (0,) * len(shape))
+    once = lambda *shape: pl.BlockSpec(shape, lambda t: (0,) * len(shape), pipeline_mode=pl.Buffered(1))
+    anywhere = pl.BlockSpec(memory_space=pl.ANY)
+    chunk = lambda rows, lag: pl.BlockSpec((rows, WIDE), lambda t: (0, chunk_at(jnp.clip(t - lag, 0, chunks - 1))))
+    group = lambda lag: lambda t: (0, jnp.clip(t - lag, 0, STEPS - 1))
+    out_specs, out_shape = front_outputs(length, group(SCAN), group(SCAN + DONE))
+    shape = jax.ShapeDtypeStruct
+    return pl.pallas_call(
+        forward_kernel,
+        grid=(SLOTS,),
+        in_specs=[
+            anywhere,
+            anywhere,
+            anywhere,
+            once(length, D),
+            once(8, SMALL_WIDTH),
+            once(length, 128),
+            once(8, length),
         ],
         out_specs=[
-            columns(length, lambda j: (0, jnp.minimum(j, last))),
-            columns(length, lambda j: (0, jnp.minimum(j, last))),
-            columns(STATE, lambda j: (0, jnp.maximum(j - DONE * exchanging, 0))),
-            whole(length, 128),
-            whole(length, 128),
-            whole(length, 128),
-            whole(length, 128),
-            whole(length, 128),
-            whole(keeps, 8, 128),
-            pl.BlockSpec(memory_space=pl.ANY),
+            *out_specs,
+            whole(PARTS, 8, 128),
+            anywhere,
+            anywhere,
+            chunk(length, MULTIPLY),
+            once(4, SHARD, length),
+            chunk(PAD, MULTIPLY + 1),
+            whole(8, XBC),
+            whole(8, 128),
+            whole(8, INNER),
+            whole(1, D),
+            whole(length + 2 * PAD, 128),
         ],
         out_shape=[
-            jax.ShapeDtypeStruct((length, INNER), BF16),
-            jax.ShapeDtypeStruct((length, INNER), BF16),
-            jax.ShapeDtypeStruct((STATE, INNER), BF16),
-            jax.ShapeDtypeStruct((length, 128), BF16),
-            jax.ShapeDtypeStruct((length, 128), BF16),
-            jax.ShapeDtypeStruct((length, 128), F32),
-            jax.ShapeDtypeStruct((length, 128), F32),
-            jax.ShapeDtypeStruct((length, 128), F32),
-            jax.ShapeDtypeStruct((keeps, 8, 128), F32),
-            jax.ShapeDtypeStruct((4, *out_matrix.shape), BF16),
+            *out_shape,
+            shape((PARTS, 8, 128), F32),
+            shape((WIDTH, D), BF16),
+            shape((4, 2 * SHARD, D), BF16),
+            shape((length, WIDTH), BF16),
+            shape((4, SHARD, length), BF16),
+            shape((PAD, WIDTH), F32),
+            shape((8, XBC), F32),
+            shape((8, 128), F32),
+            shape((8, INNER), F32),
+            shape((1, D), F32),
+            shape((length + 2 * PAD, 128), jnp.int32),
         ],
         scratch_shapes=[
-            pltpu.VMEM((length + PAD, BLK), F32),
-            pltpu.VMEM((length, Q), F32),
-            pltpu.VMEM((length // Q, 128, Q), F32),
-            pltpu.VMEM((128, length), BF16),
-            pltpu.VMEM((length, 128), F32),
-            pltpu.VMEM((length, 128), F32),
-        ]
-        + (
-            exchange_scratch()
-            + [
-                pltpu.VMEM((8, 128), F32),
-                pltpu.VMEM((PARTS, 8, 128), F32),
-                pltpu.SemaphoreType.DMA((PARTS - 1,)),
-                pltpu.SemaphoreType.DMA((PARTS - 1,)),
-                pltpu.VMEM((D // WIDE, 4, 2 * SHARD, WIDE), BF16),
-                *gather_sems(D // WIDE),
-                pltpu.SemaphoreType.DMA((D // WIDE,)),
-            ]
-        )
-        * exchanging,
-        compiler_params=communicating(1, exchanging),
-        cost_estimate=pl.CostEstimate(
-            flops=6 * 10**9, bytes_accessed=16 * 10**6, transcendentals=10**7
-        ),
-        name="front",
-    )(projected, projected, projected, halo, halo, taps, taps, heads, seg_lanes, seg_row, out_matrix)
+            *front_scratch(length),
+            *exchange_scratch(),
+            pltpu.VMEM((8, 128), F32),
+            pltpu.VMEM((PARTS, 8, 128), F32),
+            pltpu.SemaphoreType.DMA((PARTS - 1,)),
+            pltpu.SemaphoreType.DMA((PARTS - 1,)),
+            pltpu.VMEM((chunks, WIDE, D), BF16),
+            *gather_sems(chunks),
+            pltpu.SemaphoreType.DMA((chunks,)),
+            pltpu.VMEM((OUT_PIECES, 4, 2 * SHARD, WIDE), BF16),
+            *gather_sems(OUT_PIECES),
+            pltpu.SemaphoreType.DMA((OUT_PIECES,)),
+            pltpu.VMEM((length, D), BF16),
+            pltpu.VMEM((2 * chunks, length, BLK), BF16),
+            pltpu.VMEM((STEPS + 1, 8, BLK), F32),
+            pltpu.VMEM((8, SMALL_WIDTH), F32),
+            pltpu.VMEM((4, 8, SMALL_WIDTH), F32),
+            pltpu.VMEM((PAD, 128), jnp.int32),
+            pltpu.VMEM((PAD, 128), jnp.int32),
+            pltpu.VMEM((chunks, 2, PAD, BLK), F32),
+            pltpu.VMEM((chunks, 2, PAD, BLK), F32),
+            pltpu.SemaphoreType.DMA((4,)),
+            pltpu.SemaphoreType.DMA((4,)),
+            pltpu.SemaphoreType.DMA((chunks,)),
+            pltpu.SemaphoreType.DMA((chunks,)),
+        ],
+        compiler_params=communicating(1),
+        name="forward",
+    )(turned, rest, out_matrix, units, small, seg_own, seg_row)
 
 
 def tail_kernel(
-    y_ref, xs_ref, gate_ref, incoming_ref, kept_ref, out_ref, c_ref, in_ref, heads_ref, gain_ref, g_ref, units_ref,
+    y_ref, xs_ref, gate_ref, incoming_ref, out_ref, c_ref, in_ref, heads_ref, gain_ref, g_ref, units_ref,
     mixer_ref, dproj_ref, dy_ref, dsin_ref, sums_ref, block_ref, stats_ref,
-    full, dmix, squares, products, mixed, c_t, *parts,
+    full, dmix, squares, products, mixed, c_t,
 ):
     step = pl.program_id(0)
     length = y_ref.shape[0]
     group = jnp.where(step < STEPS, step, jnp.minimum(step - STEPS, STEPS - 1))
     select = chosen(group)
     half = length // 2
-    if parts:
-        exchange = Exchange(*parts)
-
-        @pl.when(step == 0)
-        def _():
-            exchange.greet()
-
     @pl.when(step == 0)
     def _():
         squares[...] = jnp.zeros_like(squares)
@@ -782,10 +828,7 @@
             dy = dy.astype(F32)
             d_skip = d_skip + jnp.sum(dy * xs_ref[rows, :].astype(F32), axis=0, keepdims=True)
             d_state = d_state + dot(c_t[:, rows], (dy * widen(in_ref[rows, :], select)).astype(BF16))
-        if parts:
-            exchange.spread(group, d_state)
-        else:
-            dsin_ref[...] = d_state.astype(BF16)
+        dsin_ref[...] = d_state.astype(BF16)
         sums_ref[...] = jnp.concatenate([d_gain, d_skip, jnp.zeros((6, BLK), F32)], axis=0)
 
     @pl.when(step == 2 * STEPS - 1)
@@ -796,20 +839,8 @@
         second = jnp.sum(mixed[...] * mixed[...], axis=0, keepdims=True)
         stats_ref[...] = jnp.concatenate([first, second, jnp.zeros((6, D), F32)], axis=0)
 
-    if parts:
-        at = step - STEPS
-
-        @pl.when((at >= JOIN) & (at < STEPS + JOIN))
-        def _():
-            done = at - JOIN
-            exchange.join(done, widen(first_rows(kept_ref), chosen(done)), False)
-
-        @pl.when(at >= DONE)
-        def _():
-            dsin_ref[...] = exchange.finish(at - DONE)
-
-
-def tail(y, xs, projected, incoming, kept, out_whole, c_rows, entering, heads, gain, cot, units, exchanging):
+
+def tail(y, xs, projected, incoming, out_whole, c_rows, entering, heads, gain, cot, units):
     length = y.shape[0]
     group = lambda i: jnp.where(i < STEPS, i, jnp.minimum(i - STEPS, STEPS - 1))
     second = lambda i: jnp.clip(i - STEPS, 0, STEPS - 1)
@@ -819,13 +850,12 @@
     whole = lambda *shape: pl.BlockSpec(shape, lambda i: (0,) * len(shape))
     return pl.pallas_call(
         tail_kernel,
-        grid=(2 * STEPS + DONE * exchanging,),
+        grid=(2 * STEPS,),
         in_specs=[
             early(length),
             each(length),
             each(length),
             early(STATE),
-            whole(*kept.shape),
             pl.BlockSpec((BLK, D), lambda i: (group(i), 0)),
             whole(length, 128),
             whole(length, 128),
@@ -838,7 +868,7 @@
             pl.BlockSpec((BLK, length), lambda i: (second(i), 0)),
             late(length),
             late(length),
-            pl.BlockSpec((STATE, BLK), lambda i: (0, second(i - DONE * exchanging))),
+            pl.BlockSpec((STATE, BLK), lambda i: (0, second(i))),
             late(8),
             whole(length, D),
             whole(8, D),
@@ -859,14 +889,13 @@
             pltpu.VMEM((length, 128), F32),
             pltpu.VMEM((length, D), F32),
             pltpu.VMEM((128, length), BF16),
-        ]
-        + exchange_scratch() * exchanging,
-        compiler_params=communicating(2, exchanging),
+        ],
+        compiler_params=pltpu.CompilerParams(vmem_limit_bytes=VMEM_LIMIT),
         cost_estimate=pl.CostEstimate(
             flops=12 * 10**9, bytes_accessed=50 * 10**6, transcendentals=4 * 10**6
         ),
         name="tail",
-    )(y, xs, projected, incoming, kept, out_whole, c_rows, entering, heads, gain, cot, units)
+    )(y, xs, projected, incoming, out_whole, c_rows, entering, heads, gain, cot, units)
 
 
 def back_steps(step, given, scratch, write, write_halo, write_taps, write_heads):
@@ -1071,9 +1100,9 @@
     ]
 
 
-def back_inputs(length):
+def back_inputs(length, late=0):
     whole = lambda *shape: pl.BlockSpec(shape, lambda j: (0,) * len(shape))
-    upto = lambda last, first=0: lambda j: (0, first + jnp.minimum(j, last))
+    upto = lambda last, first=0: lambda j: (0, first + jnp.clip(j - late, 0, last))
     return [
         pl.BlockSpec((length, BLK), upto(STEPS, STEPS)),
         pl.BlockSpec((length, BLK), lambda j: (0, 2 * STEPS + 1)),
@@ -1088,7 +1117,7 @@
         whole(length, 128),
         pl.BlockSpec((length, BLK), upto(STEPS - 1)),
         pl.BlockSpec((STATE, BLK), upto(STEPS - 1)),
-        pl.BlockSpec((STATE, BLK), upto(STEPS - 1)),
+        whole(STATE, INNER) if late else pl.BlockSpec((STATE, BLK), upto(STEPS - 1)),
     ]
 
 
@@ -1124,6 +1153,7 @@
 CHUNKS = OUT_CHUNKS + IN_CHUNKS
 LAGS = 8
 RING = 8
+LATE = 3
 
 
 def small_sums(taps, columns, input_gain, heads, stats):
@@ -1142,9 +1172,10 @@
 
 def finish_kernel(*refs):
     given, refs = refs[:14], refs[14:]
-    lhs_in, lhs_out, gate_ref, weight_ref, cot_ref, units_ref, gain_ref, columns_ref, stats_ref = refs[:9]
-    din_ref, dout_ref, input_grad_ref, total_ref = refs[9:13]
-    scratch, refs = refs[13:31], refs[31:]
+    lhs_in, lhs_out, gate_ref, weight_ref, cot_ref, units_ref, gain_ref, columns_ref, stats_ref, kept_ref = refs[:10]
+    din_ref, dout_ref, input_grad_ref, total_ref = refs[10:14]
+    scratch, refs = refs[14:32], refs[32:]
+    exchange, outgoing, refs = Exchange(*refs[:5]), refs[5], refs[6:]
     grads, edges, halos, taps, heads, d_normed = refs[:6]
     own, core_send, core_recv, y_recv, x_recv, z_recv, w_recv, final, small_send, small_recv = refs[6:16]
     send_sems, recv_sems, small_send_sems, small_recv_sems, edge_sends, edge_arrivals = refs[16:]
@@ -1161,17 +1192,7 @@
         {"ctx": flipped(part, 2)},
         {"ctx": flipped(part, 4)},
     )
-    preceding, outer = lax.rem(part + PARTS - 1, PARTS), lax.rem(part + PARTS - 1 + 2 * lax.rem(part, 2), PARTS)
-
-    def remote(source, target, send, arrival, peer):
-        return pltpu.make_async_remote_copy(
-            src_ref=source,
-            dst_ref=target,
-            send_sem=send,
-            recv_sem=arrival,
-            device_id=peer,
-            device_id_type=pl.DeviceIdType.MESH,
-        )
+    preceding = lax.rem(part + PARTS - 1, PARTS)
 
     def ring(k):
         return lax.rem(k, RING)
@@ -1207,11 +1228,9 @@
 
     @pl.when(step == 0)
     def _():
-        barrier = pltpu.get_barrier_semaphore()
-        greeted = [*peers, {"ctx": outer}]
-        for peer in greeted:
-            pl.semaphore_signal(barrier, inc=1, device_id=peer, device_id_type=pl.DeviceIdType.MESH)
-        pl.semaphore_wait(barrier, len(greeted))
+        exchange.greet(peers[0], peers[1])
+        for group in range(STEPS):
+            exchange.spread(group, given[13][:, group * BLK : (group + 1) * BLK])
         d_normed[...] = jnp.zeros_like(d_normed)
 
     def partial(lhs_of, rhs):
@@ -1239,32 +1258,47 @@
     @pl.when((step >= OUT_CHUNKS + GATE_CHUNKS) & (step < CHUNKS))
     def _():
         first = 2 * (step - OUT_CHUNKS - GATE_CHUNKS)
-        for block in (first, first + 1):
-
-            @pl.when(block <= STEPS)
+        for done in (first, first + 1):
+
+            @pl.when(done <= STEPS)
             def _():
-                edge_copy(block).wait()
+                edge_copy(done).wait()
                 tail = slice(length - 16, length)
-                more = jnp.where(part == PARTS - 1, 0.0, halos[block])
+                more = jnp.where(part == PARTS - 1, 0.0, halos[done])
                 more = jnp.concatenate([jnp.zeros_like(more), more], axis=0)
-                grads[block, tail, :] = (grads[block, tail, :].astype(F32) + more).astype(BF16)
+                grads[done, tail, :] = (grads[done, tail, :].astype(F32) + more).astype(BF16)
 
         in_chunk(jnp.concatenate([grads[first], grads[first + 1]], axis=1))
 
+    for half in range(2):
+
+        @pl.when(step == 1 + half)
+        def _():
+            for group in range(half * STEPS // 2, (half + 1) * STEPS // 2):
+                exchange.join(group, widen(first_rows(kept_ref), chosen(group)), False)
+
+    block = step - LATE
+
     def write(rows, value):
-        grads[step, rows, :] = value
+        grads[block, rows, :] = value
 
     def write_halo(value):
-        edges[step] = value
-        edge_copy(step).start()
+        edges[block] = value
+        edge_copy(block).start()
 
     def write_taps(value):
-        taps[step] = value
+        taps[block] = value
 
     def write_heads(value):
         heads[...] = value
 
-    back_steps(step, given, scratch, write, write_halo, write_taps, write_heads)
+    @pl.when((block >= 0) & (block < STEPS))
+    def _():
+        outgoing[...] = exchange.finish(block)
+
+    @pl.when(block >= 0)
+    def _():
+        back_steps(block, (*given[:13], outgoing), scratch, write, write_halo, write_taps, write_heads)
 
     @pl.when(step < CHUNKS)
     def _():
@@ -1353,7 +1387,7 @@
             scaled = grad * gain_ref[0:1, :]
             mean = jnp.sum(scaled * base, axis=1, keepdims=True) * (1.0 / D)
             input_grad_ref[rows, :] = (cot_ref[rows, :].astype(F32) + norm * (scaled - base * mean)).astype(BF16)
-        whole = jnp.concatenate([taps[block] for block in range(STEPS + 1)], axis=1)
+        whole = jnp.concatenate([taps[one] for one in range(STEPS + 1)], axis=1)
         small_send[0] = small_sums(whole, columns_ref[...], input_gain, heads[...], stats_ref[...])
         small_copy(0).start()
 
@@ -1370,7 +1404,7 @@
                 total_ref[...] = total
 
 
-def finish(given, normed_t, mixer_t, dproj, w_turned, cot, units, input_gain, column_sums, stats):
+def finish(given, normed_t, mixer_t, dproj, w_turned, cot, units, input_gain, column_sums, stats, kept):
     length = cot.shape[0]
     per_half = D // WIDE
     once = pl.Buffered(1)
@@ -1386,7 +1420,7 @@
         finish_kernel,
         grid=(CHUNKS + LAGS - 1,),
         in_specs=[
-            *back_inputs(length),
+            *back_inputs(length, LATE),
             whole(4, SHARD, length),
             whole(4, 2, SHARD, length),
             pl.BlockSpec((length, WIDE), lambda t: (0, jnp.minimum(in_chunk(t), GATE_CHUNKS - 1))),
@@ -1396,6 +1430,7 @@
             whole(1, D),
             whole(8, INNER),
             whole(8, D),
+            whole(PARTS, 8, 128),
         ],
         out_specs=[
             pl.BlockSpec((WIDE, SHARD), lambda t: (in_chunk(t - LAGS + 1), 0)),
@@ -1411,6 +1446,8 @@
         ],
         scratch_shapes=[
             *back_scratch(length),
+            *exchange_scratch(),
+            pltpu.VMEM((STATE, BLK), BF16),
             pltpu.VMEM((STEPS + 2, length, BLK), BF16),
             pltpu.VMEM((STEPS + 1, PAD, BLK), F32),
             pltpu.VMEM((STEPS + 1, PAD, BLK), F32),
@@ -1434,9 +1471,9 @@
             pltpu.SemaphoreType.DMA((STEPS + 1,)),
             pltpu.SemaphoreType.DMA((STEPS + 1,)),
         ],
-        compiler_params=communicating(0, True),
+        compiler_params=communicating(0),
         name="finish",
-    )(*given, normed_t, mixer_t, dproj, w_turned, cot, units, input_gain, column_sums, stats)
+    )(*given, normed_t, mixer_t, dproj, w_turned, cot, units, input_gain, column_sums, stats, kept)
 
 
 def passed_along(block, axis, distance):
@@ -1498,16 +1535,21 @@
     length = units_low.shape[0]
     here = (shards, parts) == (4, PARTS)
     small = pack_small(conv_taps, conv_bias, dt_bias, decay_log, skip_scale, mixer_gain, input_gain)
+    seg_row = jnp.broadcast_to(seg_ids[None], (8, length))
     if here:
-        w_turned, projected, normed_t, smalls, halo, seg_before = project(in_matrix, units_low, small, seg_ids)
-        rim_seg = seg_before.reshape(length)[length - CONV + 1 :]
-        taps, gain, g_float, heads = unpack_small(smalls, conv_bias.shape[0])
+        seg_own = jnp.broadcast_to(seg_ids[:, None], (length, 128))
+        (
+            xs, y_local, incoming, b_rows, c_rows, dt, running, entering,
+            kept, w_turned, out_whole, projected, normed_t, halo, taps, heads, gain, g_float, seg_lanes,
+        ) = forward(in_matrix, out_matrix, units_low, small, seg_own, seg_row)
+        out_whole = out_whole.reshape(-1, D)
     else:
         units = units_low.astype(F32)
         inv_rms = lax.rsqrt(jnp.mean(units * units, axis=-1, keepdims=True) + epsilon)
         base_rows = units * inv_rms
         w_whole = jnp.pad(in_matrix, ((0, 0), (0, WIDTH - PROJ)))
         w_whole = lax.all_gather(w_whole, "fsdp", axis=0, tiled=True)
+        out_whole = lax.all_gather(out_matrix, "fsdp", axis=0, tiled=True)
         rim_seg = passed_along(seg_ids[length - CONV + 1 :], "ctx", 1)
         taps, gain, g_float, heads = unpack_small(lax.all_gather(small, "fsdp"), conv_bias.shape[0])
         normed = (base_rows * g_float).astype(BF16)
@@ -1515,27 +1557,22 @@
         projected = dot(normed, w_whole).astype(BF16)
         rim_rows = passed_along(projected[length - CONV + 1 :], "ctx", 1)
         halo = jnp.pad(rim_rows, ((PAD - CONV + 1, 0), (0, 0))).astype(F32)
-    seg_ext = jnp.concatenate(
-        [
-            jnp.full((PAD - CONV + 1,), -1, jnp.int32),
-            rim_seg,
-            seg_ids,
-            jnp.full((PAD,), -2, jnp.int32),
-        ]
-    )
-    seg_lanes = jnp.broadcast_to(seg_ext[:, None], (length + 2 * PAD, 128))
-    seg_row = jnp.broadcast_to(seg_ids[None], (8, length))
-
-    xs, y_local, incoming, b_rows, c_rows, dt, running, entering, kept, out_whole = front(
-        projected, halo, taps, heads, seg_lanes, seg_row, out_matrix, here
-    )
-    out_whole = out_whole.reshape(-1, D)
-    if not here:
-        out_whole = lax.all_gather(out_matrix, "fsdp", axis=0, tiled=True)
-        kept = lax.all_gather(kept[0], "ctx")
-        incoming = joined_plainly(lax.all_gather(incoming, "ctx"), kept, place, True)
+        seg_ext = jnp.concatenate(
+            [
+                jnp.full((PAD - CONV + 1,), -1, jnp.int32),
+                rim_seg,
+                seg_ids,
+                jnp.full((PAD,), -2, jnp.int32),
+            ]
+        )
+        seg_lanes = jnp.broadcast_to(seg_ext[:, None], (length + 2 * PAD, 128))
+        xs, y_local, state, b_rows, c_rows, dt, running, entering, keep = front(
+            projected, halo, taps, heads, seg_lanes, seg_row
+        )
+        kept = lax.all_gather(keep, "ctx")
+        incoming = joined_plainly(lax.all_gather(state, "ctx"), kept, place, True)
     mixer_t, dproj, dy, outgoing, column_sums, block_out, stats = tail(
-        y_local, xs, projected, incoming, kept, out_whole, c_rows, entering, heads, gain, cot, units_low, here
+        y_local, xs, projected, incoming, out_whole, c_rows, entering, heads, gain, cot, units_low
     )
     if not here:
         outgoing = joined_plainly(lax.all_gather(outgoing, "ctx"), kept, place, False)
@@ -1544,7 +1581,7 @@
     )
     if here:
         d_in, d_out, input_grad, total = finish(
-            given, normed_t, mixer_t.reshape(4, 2, SHARD, length), dproj, w_turned, cot, units_low, g_float, column_sums, stats
+            given, normed_t, mixer_t.reshape(4, 2, SHARD, length), dproj, w_turned, cot, units_low, g_float, column_sums, stats, kept
         )
         d_in, d_out = d_in.T.astype(F32), d_out.astype(F32)
     else:

time: 452 us -> 404 us (0.89)
  Pallas kernels: 411 us -> 375 us
  local copies, waits for them, and re-layouts: 26.1 us -> 14.3 us
    pallas_call x3 -> x2, Pallas kernels: 197 us -> 161 us  [the longest x1 120 us: forward(): pl.pallas_call(forward_kernel, grid=(SLOTS,), in_specs=[anywhere, anywher...]
    slice x6 -> x1, local copies, waits for them, and re-layouts: 5.67 us -> 0.96 us  [forward(): rest = jnp.pad(turned[(chunks - 1) * WIDE:], ((0, WIDTH - PROJ), (0, 0)))]
where the time goes in v6:
time: 404 us
  Pallas kernels  375 us (93%)
  local copies, waits for them, and re-layouts  14.3 us (4%)
  other arithmetic  13.3 us (3%)
    pallas_call x1, Pallas kernels, finish(): pl.pallas_call(finish_kernel, grid=(CHUNKS + LAGS - 1,), in_specs=[*back_...  215 us
    pallas_call x1, Pallas kernels, forward(): pl.pallas_call(forward_kernel, grid=(SLOTS,), in_specs=[anywhere, anywher...  120 us
    pallas_call x1, Pallas kernels, tail(): pl.pallas_call(tail_kernel, grid=(2 * STEPS,), in_specs=[early(length), e...  41 us
    convert_element_type x2, other arithmetic, on_device(): d_in, d_out = (d_in.T.astype(F32), d_out.astype(F32))  9.92 us

profile of v6, /device:TPU:0, one launch (start us, length us, event | category | flops | bytes accessed | tf_op | source)
XLA Modules:
  0.0 403.5 jit_solution(12128937611870404165)
XLA Ops:
  0.6 1.3 broadcast_in_dim.36.refs_6_
  1.9 1.0 slice.40
  2.9 0.8 pad.22.refs_1_
  3.7 1.5 broadcast_in_dim.35.refs_5_
  5.2 0.7 pad.23
  5.9 0.7 pad.24
  6.6 0.8 fusion.4
  7.4 0.7 broadcast_in_dim.30
  8.0 0.7 concatenate.7
  8.8 0.6 pad_convert_fusion.refs_4_
  9.4 119.6 %forward.1 = (bf16[512,3072]{1,0:T(8,128)(2,1)}, bf16[512,3072]{1,0:T(8,128)(2,1)}, bf16[128,3072]{1,0:T(8,128)(2,1)}, bf16[512,128]{1,0:T(8,128)(2,1)}, bf16[51...) custom-call(bf16[6448,384]{1,0:T(8,128)(2,1)} %bitcast.23, ...), custom_call_target="tpu_custom_call" | custom-call | tf_op jit(solution)/shard_map/forward/pallas_call | solution.py:680
  129.0 41.0 %tail.1 = (bf16[3072,512]{1,0:T(8,128)(2,1)}, bf16[512,6656]{1,0:T(8,128)(2,1)}, bf16[512,3072]{1,0:T(8,128)(2,1)}, bf16[128,3072]{1,0:T(8,128)(2,1)}, f32[8,307...) custom-call(bf16[512,3072]{1,0:T(8,128)(2,1)} %get-tuple-element.42.y_ref, ...), custom_call_target="tpu_custom_call" | custom-call | flops 12000000000 | bytes 50000000 | tf_op jit(solution)/shard_map/tail/pallas_call | solution.py:851
  170.0 214.7 %finish.1 = (bf16[6448,384]{1,0:T(8,128)(2,1)}, bf16[768,1536]{1,0:T(8,128)(2,1)}, bf16[512,1536]{1,0:T(8,128)(2,1)}, f32[8,3328]{1,0:T(8,128)}) custom-call(bf16[512,6656]{1,0:T(8,128)(2,1)} %get-tuple-element.44.gate_ref.refs_0_.refs_1_, bf16[512,6656]{1,0:T(8,128)(2,1)} %get-tuple-element.44.gate_ref.refs_0_.refs_1_, ...), custom_call_target="tpu_custom_call" | custom-call | tf_op jit(solution)/shard_map/finish/pallas_call | solution.py:1419
  384.7 1.2 fusion.8
  385.9 1.9 fusion.7
  387.7 0.7 fusion.10
  388.4 0.6 fusion.5
  389.0 0.0 copy-start
  389.0 7.1 %convert_bitcast_fusion = f32[384,6448]{0,1:T(8,128)} fusion(bf16[6448,384]{1,0:T(8,128)(2,1)} %get-tuple-element.69), kind=kLoop, calls=%fused_computation | loop fusion | flops 2476032 | bytes 14856192 | tf_op jit(solution)/shard_map/convert_element_type | solution.py:1586
  396.1 0.0 copy-done
  396.1 0.0 copy-start.2
  396.1 2.8 convert_element_type.22
  398.9 0.0 copy-done.2
  399.0 0.7 dynamic-slice_bitcast_fusion
  399.7 0.1 reshape_squeeze.3
  399.8 0.1 reduce_sum.9
  399.9 0.6 dynamic_slice.38
  400.5 0.6 dynamic-slice_reduce_fusion.1
  401.1 0.7 dynamic-slice_reduce_fusion
  401.8 0.6 dynamic-slice_reduce_fusion.2
  402.4 0.0 copy-done.1
  402.4 1.1 copy.25
  (8 shorter events, 0.1 us)
Async XLA Ops:
  389.0 7.1 %copy-start = (bf16[768,1536]{1,0:T(8,128)(2,1)S(1)}, bf16[768,1536]{1,0:T(8,128)(2,1)}, u32[]{:S(2)}) copy-start(bf16[768,1536]{1,0:T(8,128)(2,1)} %get-tuple-element.70) | copy-start | bytes 7077892
  396.1 2.8 copy-start.2
  396.1 6.3 %copy-start.1 = (bf16[512,1536]{1,0:T(8,128)(2,1)S(1)}, bf16[512,1536]{1,0:T(8,128)(2,1)}, u32[]{:S(2)}) copy-start(bf16[512,1536]{1,0:T(8,128)(2,1)} %get-tuple-element.68) | copy-start | bytes 4718596

commit v7 on v6

--- a/solution.py
+++ b/solution.py
@@ -128,21 +128,16 @@
 
 
 class Gather:
-    def __init__(self, locate, rows, loads, sends, arrivals):
-        self.locate, self.rows = locate, rows
+    def __init__(self, locate, several, rows, loads, sends, arrivals):
+        self.locate, self.several, self.rows = locate, several, rows
         self.loads, self.sends, self.arrivals = loads, sends, arrivals
         shard, part = lax.axis_index("fsdp"), lax.axis_index("ctx")
         self.own, self.other = shard, flipped(shard, 2)
-        self.sibling, self.opposite = flipped(shard, 1), flipped(flipped(shard, 2), 1)
         x, near = lax.rem(part, 2), lax.rem(part // 2, 2)
         self.mine, self.over_x, self.over_z = 2 * x + near, 2 * (1 - x) + near, 2 * x + 1 - near
         self.across = 2 * (1 - x) + 1 - near
-        self.peers = {
-            "core": {"fsdp": flipped(shard, 1)},
-            "y": {"fsdp": flipped(shard, 2)},
-            "x": {"ctx": flipped(part, 1)},
-            "z": {"ctx": flipped(part, 2)},
-        }
+        self.core, self.y = {"fsdp": flipped(shard, 1)}, {"fsdp": flipped(shard, 2)}
+        self.to_x, self.to_z = {"ctx": flipped(part, 1)}, {"ctx": flipped(part, 2)}
 
     def whole(self, shard, k):
         return self.locate(k, shard, 0, self.rows)
@@ -154,90 +149,78 @@
         return self.locate(k, shard, (2 * which + second) * (self.rows // 8), self.rows // 8)
 
     def copy(self, place, kind, k, peer):
-        return pltpu.make_async_remote_copy(
-            src_ref=place,
-            dst_ref=place,
-            send_sem=self.sends.at[kind, k],
-            recv_sem=self.arrivals.at[kind, k],
-            device_id=self.peers[peer],
-            device_id_type=pl.DeviceIdType.MESH,
-        )
-
-    def outgoing(self, kind, k):
-        own, other = self.own, self.other
-        if kind == 0:
-            return self.copy(self.whole(own, k), kind, k, "core")
-        if kind == 1:
-            return self.copy(self.quarter(own, k, self.mine), kind, k, "y")
-        if kind == 2:
-            return self.copy(self.quarter(other, k, self.mine), kind, k, "x")
-        if kind == 3:
-            return self.copy(self.quarter(other, k, self.mine), kind, k, "z")
-        if kind == 4:
-            return self.copy(self.half(other, k, self.over_x, 0), kind, k, "z")
-        if kind == 5:
-            return self.copy(self.half(other, k, self.over_z, 1), kind, k, "x")
-        which = (self.mine, self.over_x, self.over_z, self.across)[kind - 6]
-        return self.copy(self.quarter(other, k, which), kind, k, "core")
-
-    def arrived(self, kind, k):
-        other, opposite = self.other, self.opposite
-        if kind == 0:
-            place = self.whole(self.sibling, k)
-        elif kind < 4:
-            place = self.quarter(other, k, (self.mine, self.over_x, self.over_z)[kind - 1])
-        elif kind < 6:
-            place = self.half(other, k, self.across, kind - 4)
-        else:
-            place = self.quarter(opposite, k, (self.mine, self.over_x, self.over_z, self.across)[kind - 6])
-        self.copy(place, kind, k, "core").wait_recv()
+        return remote(place, place, self.sends.at[k], self.arrivals.at[kind, k], peer)
 
     def load(self, k, source):
         return pltpu.make_async_copy(source, self.whole(self.own, k), self.loads.at[k])
 
     def begin(self, k):
         self.load(k, self.whole(self.own, k)).wait()
-        self.outgoing(1, k).start()
-        self.outgoing(0, k).start()
+        self.send_own(k)
+
+    def send_own(self, k):
+        self.copy(self.quarter(self.own, k, self.mine), 1, k, self.y).start()
+        self.copy(self.whole(self.own, k), 0, k, self.core).start()
 
     def first(self, k):
-        self.arrived(1, k)
-        for kind in (2, 3, 6):
-            self.outgoing(kind, k).start()
+        quarter = self.quarter(self.other, k, self.mine)
+        self.copy(quarter, 1, k, self.y).wait_recv()
+        self.copy(quarter, 2, k, self.to_x).start()
+        self.copy(quarter, 3, k, self.to_z).start()
 
     def second(self, k):
-        self.arrived(2, k)
-        self.outgoing(4, k).start()
-        self.outgoing(7, k).start()
-        self.arrived(3, k)
-        self.outgoing(5, k).start()
-        self.outgoing(8, k).start()
+        self.copy(self.quarter(self.other, k, self.over_x), 2, k, self.to_x).wait_recv()
+        self.copy(self.half(self.other, k, self.over_x, 0), 4, k, self.to_z).start()
+        self.copy(self.quarter(self.other, k, self.over_z), 3, k, self.to_z).wait_recv()
+        self.copy(self.half(self.other, k, self.over_z, 1), 4, k, self.to_x).start()
 
     def third(self, k):
-        self.arrived(4, k)
-        self.arrived(5, k)
-        self.outgoing(9, k).start()
+        self.copy(self.quarter(self.other, k, self.across), 4, k, self.to_x).wait_recv()
+        self.copy(self.whole(self.other, k), 0, k, self.core).start()
 
     def complete(self, k):
-        for kind in (0, 6, 7, 8, 9):
-            self.arrived(kind, k)
+        self.copy(self.several(k, 2), 0, k, self.core).wait_recv()
 
     def drain(self, k):
-        for kind in range(10):
-            self.outgoing(kind, k).wait_send()
+        self.copy(self.several(k, 3), 0, k, self.core).wait_send()
+
+
+class PlainGather(Gather):
+    def direct(self, shard, k):
+        return self.locate(k, shard, 0, DIRECT * self.rows // 6)
+
+    def part_of(self, shard, k, which):
+        size = (6 - DIRECT) * self.rows // 12
+        return self.locate(k, shard, DIRECT * self.rows // 6 + which * size, size)
+
+    def send_own(self, k):
+        self.copy(self.direct(self.own, k), 3, k, self.y).start()
+        self.copy(self.part_of(self.own, k, self.mine // 2), 1, k, self.y).start()
+        self.copy(self.whole(self.own, k), 0, k, self.core).start()
+
+    def first(self, k):
+        part = self.part_of(self.other, k, self.mine // 2)
+        self.copy(part, 1, k, self.y).wait_recv()
+        self.copy(part, 2, k, self.to_x).start()
+
+    def second(self, k):
+        self.copy(self.direct(self.other, k), 3, k, self.y).wait_recv()
+        self.copy(self.part_of(self.other, k, self.over_x // 2), 2, k, self.to_x).wait_recv()
+        self.copy(self.whole(self.other, k), 0, k, self.core).start()
 
 
 def gather_sems(chunks):
     return [
         pltpu.SemaphoreType.DMA((chunks,)),
-        pltpu.SemaphoreType.DMA((10, chunks)),
-        pltpu.SemaphoreType.DMA((10, chunks)),
+        pltpu.SemaphoreType.DMA((chunks,)),
+        pltpu.SemaphoreType.DMA((5, chunks)),
     ]
 
 
 PARTS = 8
 SLAB = STATE // PARTS
-JOIN, DONE = 2, 4
+UNIT = 2 * BLK
+UNITS = INNER // UNIT
 
 
 class Exchange:
@@ -270,15 +253,17 @@
         some = pl.ds(0, PARTS - 1)
         return self.copy(source.at[group, some], target.at[group, some], kind, group, self.others()[0])
 
-    def spread(self, group, state):
-        self.held[group] = state.astype(BF16).reshape(PARTS, SLAB, BLK)
+    def hold(self, group, half, state):
+        self.held[group, :, :, half * BLK : (half + 1) * BLK] = state.astype(BF16).reshape(PARTS, SLAB, BLK)
+
+    def spread(self, group):
         self.gathered[group, self.me] = self.held[group, self.me]
         for other in self.others():
             self.copy(self.held.at[group, other], self.gathered.at[group, self.me], 0, group, other).start()
 
     def join(self, group, kept, forward):
         self.all_of(0, group).wait_recv()
-        total = jnp.zeros((SLAB, BLK), F32)
+        total = jnp.zeros((SLAB, UNIT), F32)
         for part in range(PARTS) if forward else range(PARTS - 1, -1, -1):
             self.joined[group, part] = total.astype(BF16)
             total = kept[part : part + 1, :] * total + self.gathered[group, part].astype(F32)
@@ -290,15 +275,16 @@
         self.all_of(1, group).wait_recv()
         self.all_of(0, group).wait_send()
         self.all_of(1, group).wait_send()
-        return self.incoming[group].reshape(STATE, BLK)
+        return self.incoming[group].reshape(STATE, UNIT)
 
 
 def exchange_scratch():
-    return [pltpu.VMEM((STEPS, PARTS, SLAB, BLK), BF16) for _ in range(4)] + [pltpu.SemaphoreType.DMA((4, STEPS))]
-
-
-def first_rows(kept_ref):
-    return jnp.concatenate([kept_ref[part, 0:1, :] for part in range(PARTS)], axis=0)
+    return [pltpu.VMEM((UNITS, PARTS, SLAB, UNIT), BF16) for _ in range(4)] + [pltpu.SemaphoreType.DMA((4, UNITS))]
+
+
+def kept_of(kept_ref, unit):
+    rows = jnp.concatenate([kept_ref[part, 0:1, :] for part in range(PARTS)], axis=0)
+    return jnp.concatenate([widen(rows, chosen(2 * unit)), widen(rows, chosen(2 * unit + 1))], axis=1)
 
 
 def joined_plainly(states, kept, place, forward):
@@ -404,9 +390,9 @@
     return state
 
 
-def front_outputs(length, column, state_at):
+def front_outputs(length, column, state_at, width=BLK):
     whole = lambda *shape: (pl.BlockSpec(shape, lambda j: (0, 0)), shape)
-    columns = lambda rows, at: (pl.BlockSpec((rows, BLK), at), (rows, INNER))
+    columns = lambda rows, at: (pl.BlockSpec((rows, width), at), (rows, INNER))
     specs = [
         (columns(length, column), BF16),
         (columns(length, column), BF16),
@@ -449,7 +435,7 @@
             columns(8, lambda j: (0, STEPS)),
             whole(8, 128),
             whole(length + 2 * PAD, 128),
-            whole(8, length),
+            whole(1, length),
         ],
         out_specs=[*out_specs, whole(8, 128)],
         out_shape=[*out_shape, jax.ShapeDtypeStruct((8, 128), F32)],
@@ -462,8 +448,12 @@
 ORDER = (2 * INNER // WIDE, *range(INNER // WIDE, 2 * INNER // WIDE), *range(INNER // WIDE))
 MULTIPLY = 3
 SCAN = MULTIPLY + 2
-OUT_PIECES = D // WIDE
-SLOTS = SCAN + STEPS + DONE
+OUT_WIDE = 128
+OUT_PIECES = D // OUT_WIDE
+OUT_BEGIN, DIRECT = 4, 4
+JOIN, DONE = 2, 4
+SLOTS = MULTIPLY + len(ORDER)
+EDGES = 1 + INNER // WIDE
 
 
 def chunk_at(position):
@@ -472,17 +462,17 @@
 
 
 def forward_kernel(*refs):
-    main_ref, rest_ref, shard_ref, units_ref, small_ref, seg_own_ref, row_ref = refs[:7]
-    xs_ref, y_ref, state_ref, b_ref, c_ref, dt_ref, run_ref, in_ref = refs[7:15]
-    keep_ref, weight_ref, whole_ref, projected_ref, normed_t_ref = refs[15:20]
-    halo_ref, taps_ref, heads_ref, gain_ref, input_gain_ref, seg_ref = refs[20:26]
-    ext, scores, run_t, b_t, enter, leave = refs[26:32]
-    exchange = Exchange(*refs[32:37])
-    own_keep, keeps, keep_sends, keep_arrivals = refs[37:41]
-    gathered, loads, sends, arrivals, stores = refs[41:46]
-    out_gathered, out_loads, out_sends, out_arrivals, out_stores = refs[46:51]
-    normed, blocks, taps, own_small, smalls, seg_tail, seg_head = refs[51:58]
-    edges, halos, small_sends, small_arrivals, edge_sends, edge_arrivals = refs[58:]
+    main_ref, shard_ref, units_ref, small_ref, row_ref = refs[:5]
+    xs_ref, y_ref, state_ref, b_ref, c_ref, dt_ref, run_ref, in_ref = refs[5:13]
+    keep_ref, weight_ref, whole_ref, projected_ref, normed_t_ref = refs[13:18]
+    halo_ref, taps_ref, heads_ref, gain_ref, input_gain_ref, seg_ref = refs[18:24]
+    ext, scores, run_t, b_t, enter, leave = refs[24:30]
+    exchange = Exchange(*refs[30:35])
+    own_keep, keeps, keep_sends, keep_arrivals = refs[35:39]
+    gathered, loads, sends, arrivals, stores = refs[39:44]
+    out_gathered, out_loads, out_sends, out_arrivals, out_stores = refs[44:49]
+    normed, blocks, taps, own_small, smalls, seg_tail, seg_head = refs[49:56]
+    edges, halos, small_sends, small_arrivals, edge_sends, edge_arrivals = refs[56:]
     step = pl.program_id(0)
     length = units_ref.shape[0]
     shard, part = lax.axis_index("fsdp"), lax.axis_index("ctx")
@@ -496,8 +486,17 @@
     def place_out(k, s, start, size):
         return out_gathered.at[k, s, pl.ds(pl.multiple_of(start, size), size)]
 
-    gather = Gather(place_in, WIDE, loads, sends, arrivals)
-    gather_out = Gather(place_out, 2 * SHARD, out_loads, out_sends, out_arrivals)
+    several_in = lambda k, count: gathered.at[k, :, pl.ds(0, count * SHARD)]
+    several_out = lambda k, count: out_gathered.at[k, pl.ds(0, count)]
+    gather = Gather(place_in, several_in, WIDE, loads, sends, arrivals)
+    gather_out = PlainGather(place_out, several_out, 2 * SHARD, out_loads, out_sends, out_arrivals)
+    rest = PROJ % WIDE
+
+    def load_rest():
+        columns = pl.ds(pl.multiple_of(shard * SHARD, SHARD), SHARD)
+        return pltpu.make_async_copy(
+            main_ref.at[PROJ - rest : PROJ, :], gathered.at[0, pl.ds(0, rest), columns], loads.at[0]
+        )
 
     def small_copy(hop):
         return remote(own_small, smalls.at[shard], small_sends.at[hop], small_arrivals.at[hop], others[hop])
@@ -517,31 +516,42 @@
         return pltpu.make_async_copy(gathered.at[k], weight_ref.at[rows], stores.at[k])
 
     def store_out(k):
-        columns = pl.ds(pl.multiple_of(k * WIDE, WIDE), WIDE)
+        columns = pl.ds(pl.multiple_of(k * OUT_WIDE, OUT_WIDE), OUT_WIDE)
         return pltpu.make_async_copy(out_gathered.at[k], whole_ref.at[:, :, columns], out_stores.at[k])
 
     @pl.when(step == 0)
     def _():
+        load_rest().start()
         for k, chunk in enumerate(ORDER):
-            source = rest_ref if (chunk + 1) * WIDE > PROJ else main_ref.at[chunk * WIDE : (chunk + 1) * WIDE, :]
-            gather.load(k, source).start()
+            if k:
+                gather.load(k, main_ref.at[chunk * WIDE : (chunk + 1) * WIDE, :]).start()
         for k in range(OUT_PIECES):
-            gather_out.load(k, shard_ref.at[:, k * WIDE : (k + 1) * WIDE]).start()
+            gather_out.load(k, shard_ref.at[:, k * OUT_WIDE : (k + 1) * OUT_WIDE]).start()
         own_small[...] = small_ref[...]
         smalls[shard] = small_ref[...]
-        seg_tail[...] = seg_own_ref[length - PAD :, :]
+        columns = pl.ds(pl.multiple_of(shard * SHARD, SHARD), SHARD)
+        gathered[0, rest:, columns] = jnp.zeros((WIDE - rest, SHARD), BF16)
+        for k in range(length // 128):
+            ids = jnp.broadcast_to(row_ref[0:1, k * 128 : (k + 1) * 128].astype(F32), (128, 128))
+            seg_ref[PAD + k * 128 : PAD + (k + 1) * 128, :] = ids.T.astype(jnp.int32)
+        seg_tail[...] = seg_ref[length : length + PAD, :]
         exchange.greet(*others)
         for hop in range(3):
             small_copy(hop).start()
         seg_copy().start()
-        for k in range(AHEAD):
+        load_rest().wait()
+        gather.send_own(0)
+        for k in range(1, AHEAD):
             gather.begin(k)
+
+    def take_small():
         for hop in range(3):
             small_copy(hop).wait()
         seg_copy().wait()
         seg_ref[0:PAD, :] = jnp.where(part == 0, -1, seg_head[...])
-        seg_ref[PAD : PAD + length, :] = seg_own_ref[...]
         seg_ref[PAD + length :, :] = jnp.full((PAD, 128), -2, jnp.int32)
+
+    def normalise():
         gain = jnp.concatenate([smalls[s, 6:7, :SHARD] for s in range(4)], axis=1)
         input_gain_ref[...] = gain
         for k in range(length // Q):
@@ -550,8 +560,7 @@
             norm = lax.rsqrt(jnp.sum(units * units, axis=1, keepdims=True) * (1.0 / D) + epsilon)
             normed[rows, :] = (units * norm * gain).astype(BF16)
 
-    @pl.when(step == 1)
-    def _():
+    def take_taps():
         mixer_gain = jnp.concatenate([smalls[s, 5:6, : INNER // 4] for s in range(4)], axis=1)
         gain_ref[...] = jnp.broadcast_to(mixer_gain, (8, INNER))
         whole = jnp.zeros((8, XBC), F32)
@@ -573,6 +582,10 @@
         for block in range(STEPS + 1):
             taps[block] = whole[:, block * BLK : (block + 1) * BLK]
 
+    def complete_out(k):
+        gather_out.complete(k)
+        store_out(k).start()
+
     def stage(lag, count=len(ORDER)):
         def decorate(body):
             k = step - lag
@@ -583,33 +596,51 @@
 
         return decorate
 
-    stage(-AHEAD)(lambda k: pl.when(k >= AHEAD)(lambda: gather.begin(k)))
-    stage(6, OUT_PIECES)(gather_out.begin)
-    stage(0)(gather.first)
-    stage(1)(gather.second)
-    stage(2)(gather.third)
-    stage(12, OUT_PIECES)(gather_out.first)
-    stage(13, OUT_PIECES)(gather_out.second)
-    stage(14, OUT_PIECES)(gather_out.third)
+    def advance(tick):
+        def at(lag, body, first=0, count=len(ORDER)):
+            k = tick - lag
+
+            @pl.when((k >= first) & (k < count))
+            def _():
+                body(k)
+
+        def complete(k):
+            gather.complete(k)
+            store(k).start()
+
+        at(-AHEAD, gather.begin, AHEAD)
+        at(0, gather.first)
+        at(1, gather.second)
+        at(2, gather.third)
+        at(3, complete)
+        at(OUT_BEGIN, gather_out.begin, 0, OUT_PIECES)
+        at(OUT_BEGIN + 2, gather_out.first, 0, OUT_PIECES)
+        at(OUT_BEGIN + 4, gather_out.second, 0, OUT_PIECES)
+        at(OUT_BEGIN + 6, complete_out, 0, OUT_PIECES)
+
+    tick = jnp.where(step < SCAN, step, 2 * step - SCAN)
+    advance(tick)
+    pl.when(step == 0)(take_small)
+    pl.when(step == 1)(normalise)
+    pl.when(step == 2)(take_taps)
 
     @stage(MULTIPLY)
     def _(k):
-        gather.complete(k)
-        store(k).start()
         low = dot_nt(normed[...], gathered[k]).astype(BF16)
         projected_ref[...] = low
-        edge = low[length - 16 :, :].astype(F32)[8:, :]
-        for half in range(2):
-            columns = slice(half * BLK, (half + 1) * BLK)
-            blocks[2 * chunk_at(k) + half] = low[:, columns]
-            edges[k, half] = edge[:, columns]
-        edge_copy(k).start()
-
-    @stage(MULTIPLY + 1)
+
+        @pl.when(k < EDGES)
+        def _():
+            edge = low[length - 16 :, :].astype(F32)[8:, :]
+            for half in range(2):
+                columns = slice(half * BLK, (half + 1) * BLK)
+                blocks[2 * k + half] = low[:, columns]
+                edges[k, half] = edge[:, columns]
+            edge_copy(k).start()
+
+    @stage(SCAN - 1, EDGES)
     def _(k):
         edge_copy(k).wait()
-        gather.drain(k)
-        store(k).wait()
         for half in range(2):
             columns = slice(half * BLK, (half + 1) * BLK)
             halos[k, half] = jnp.where(part == 0, 0.0, halos[k, half])
@@ -618,7 +649,7 @@
     @pl.when(step == SCAN - 1)
     def _():
         keep = prepare(
-            blocks.at[2 * STEPS], lambda rows: blocks[2 * STEPS + 1, rows, :128], halos.at[0, 0], taps.at[STEPS], heads_ref,
+            blocks.at[0], lambda rows: blocks[1, rows, :128], halos.at[0, 0], taps.at[STEPS], heads_ref,
             seg_ref, row_ref, b_ref, c_ref, dt_ref, run_ref, in_ref, ext, scores, run_t, b_t, enter, leave,
         )
         own_keep[...] = keep
@@ -626,13 +657,25 @@
         for hop in range(PARTS - 1):
             keep_copy(hop).start()
 
-    @stage(SCAN, STEPS)
-    def _(j):
-        state = local_scan(
-            j, blocks.at[STEPS + j], halos.at[1 + j // 2, lax.rem(j, 2)], taps.at[j], seg_ref,
-            xs_ref, y_ref, c_ref, dt_ref, run_ref, ext, scores, run_t, b_t, enter, leave,
-        )
-        exchange.spread(j, state)
+    for half in range(2):
+
+        @stage(SCAN, UNITS)
+        def _(unit):
+            columns = pl.ds(half * BLK, BLK)
+            group = 2 * unit + half
+            state = local_scan(
+                group, blocks.at[2 + group], halos.at[1 + unit, half], taps.at[group], seg_ref,
+                xs_ref.at[:, columns], y_ref.at[:, columns], c_ref, dt_ref, run_ref, ext, scores, run_t, b_t, enter, leave,
+            )
+            exchange.hold(unit, half, state)
+
+        if half == 0:
+
+            @pl.when(step >= SCAN)
+            def _():
+                advance(tick + 1)
+
+    stage(SCAN, UNITS)(exchange.spread)
 
     @pl.when(step == SCAN + JOIN)
     def _():
@@ -640,42 +683,36 @@
             keep_copy(hop).wait()
         keep_ref[...] = keeps[...]
 
-    @stage(SCAN + JOIN, STEPS)
-    def _(j):
-        exchange.join(j, widen(first_rows(keeps), chosen(j)), True)
-
-    @stage(SCAN + DONE, STEPS)
-    def _(j):
-        state_ref[...] = exchange.finish(j)
-
-    @stage(16, OUT_PIECES)
-    def _(k):
-        gather_out.complete(k)
-        store_out(k).start()
-
-    @stage(18, OUT_PIECES)
-    def _(k):
-        gather_out.drain(k)
-        store_out(k).wait()
+    @stage(SCAN + JOIN, UNITS)
+    def _(unit):
+        exchange.join(unit, kept_of(keeps, unit), True)
+
+    @stage(SCAN + DONE, UNITS)
+    def _(unit):
+        state_ref[...] = exchange.finish(unit)
 
     @pl.when(step == SLOTS - 1)
     def _():
+        for k in range(len(ORDER)):
+            gather.drain(k)
+            store(k).wait()
+        for k in range(OUT_PIECES):
+            gather_out.drain(k)
+            store_out(k).wait()
         for s in range(4):
             columns = slice(s * SHARD, (s + 1) * SHARD)
             normed_t_ref[s] = normed[:, columns].astype(F32).T.astype(BF16)
 
 
-def forward(in_matrix, out_matrix, units, small, seg_own, seg_row):
+def forward(in_matrix, out_matrix, units, small, seg_row):
     length = units.shape[0]
     chunks = len(ORDER)
-    turned = in_matrix.T
-    rest = jnp.pad(turned[(chunks - 1) * WIDE :], ((0, WIDTH - PROJ), (0, 0)))
     whole = lambda *shape: pl.BlockSpec(shape, lambda t: (0,) * len(shape))
     once = lambda *shape: pl.BlockSpec(shape, lambda t: (0,) * len(shape), pipeline_mode=pl.Buffered(1))
     anywhere = pl.BlockSpec(memory_space=pl.ANY)
     chunk = lambda rows, lag: pl.BlockSpec((rows, WIDE), lambda t: (0, chunk_at(jnp.clip(t - lag, 0, chunks - 1))))
-    group = lambda lag: lambda t: (0, jnp.clip(t - lag, 0, STEPS - 1))
-    out_specs, out_shape = front_outputs(length, group(SCAN), group(SCAN + DONE))
+    unit = lambda lag: lambda t: (0, jnp.clip(t - lag, 0, UNITS - 1))
+    out_specs, out_shape = front_outputs(length, unit(SCAN), unit(SCAN + DONE), UNIT)
     shape = jax.ShapeDtypeStruct
     return pl.pallas_call(
         forward_kernel,
@@ -683,11 +720,9 @@
         in_specs=[
             anywhere,
             anywhere,
-            anywhere,
             once(length, D),
             once(8, SMALL_WIDTH),
-            once(length, 128),
-            once(8, length),
+            once(1, length),
         ],
         out_specs=[
             *out_specs,
@@ -696,7 +731,7 @@
             anywhere,
             chunk(length, MULTIPLY),
             once(4, SHARD, length),
-            chunk(PAD, MULTIPLY + 1),
+            pl.BlockSpec((PAD, WIDE), lambda t: (0, chunk_at(jnp.clip(t - SCAN + 1, 0, EDGES - 1)))),
             whole(8, XBC),
             whole(8, 128),
             whole(8, INNER),
@@ -727,26 +762,26 @@
             pltpu.VMEM((chunks, WIDE, D), BF16),
             *gather_sems(chunks),
             pltpu.SemaphoreType.DMA((chunks,)),
-            pltpu.VMEM((OUT_PIECES, 4, 2 * SHARD, WIDE), BF16),
+            pltpu.VMEM((OUT_PIECES, 4, 2 * SHARD, OUT_WIDE), BF16),
             *gather_sems(OUT_PIECES),
             pltpu.SemaphoreType.DMA((OUT_PIECES,)),
             pltpu.VMEM((length, D), BF16),
-            pltpu.VMEM((2 * chunks, length, BLK), BF16),
+            pltpu.VMEM((2 * EDGES, length, BLK), BF16),
             pltpu.VMEM((STEPS + 1, 8, BLK), F32),
             pltpu.VMEM((8, SMALL_WIDTH), F32),
             pltpu.VMEM((4, 8, SMALL_WIDTH), F32),
             pltpu.VMEM((PAD, 128), jnp.int32),
             pltpu.VMEM((PAD, 128), jnp.int32),
-            pltpu.VMEM((chunks, 2, PAD, BLK), F32),
-            pltpu.VMEM((chunks, 2, PAD, BLK), F32),
+            pltpu.VMEM((EDGES, 2, PAD, BLK), F32),
+            pltpu.VMEM((EDGES, 2, PAD, BLK), F32),
             pltpu.SemaphoreType.DMA((4,)),
             pltpu.SemaphoreType.DMA((4,)),
-            pltpu.SemaphoreType.DMA((chunks,)),
-            pltpu.SemaphoreType.DMA((chunks,)),
+            pltpu.SemaphoreType.DMA((EDGES,)),
+            pltpu.SemaphoreType.DMA((EDGES,)),
         ],
         compiler_params=communicating(1),
         name="forward",
-    )(turned, rest, out_matrix, units, small, seg_own, seg_row)
+    )(in_matrix.T, out_matrix, units, small, seg_row)
 
 
 def tail_kernel(
@@ -1110,7 +1145,7 @@
         pl.BlockSpec((8, BLK), upto(STEPS)),
         whole(8, 128),
         whole(length + 2 * PAD, 128),
-        whole(8, length),
+        whole(1, length),
         whole(length, 128),
         whole(length, 128),
         whole(length, 128),
@@ -1230,7 +1265,9 @@
     def _():
         exchange.greet(peers[0], peers[1])
         for group in range(STEPS):
-            exchange.spread(group, given[13][:, group * BLK : (group + 1) * BLK])
+            exchange.hold(group // 2, group % 2, given[13][:, group * BLK : (group + 1) * BLK])
+            if group % 2:
+                exchange.spread(group // 2)
         d_normed[...] = jnp.zeros_like(d_normed)
 
     def partial(lhs_of, rhs):
@@ -1274,8 +1311,8 @@
 
         @pl.when(step == 1 + half)
         def _():
-            for group in range(half * STEPS // 2, (half + 1) * STEPS // 2):
-                exchange.join(group, widen(first_rows(kept_ref), chosen(group)), False)
+            for unit in range(half * UNITS // 2, (half + 1) * UNITS // 2):
+                exchange.join(unit, kept_of(kept_ref, unit), False)
 
     block = step - LATE
 
@@ -1292,13 +1329,15 @@
     def write_heads(value):
         heads[...] = value
 
-    @pl.when((block >= 0) & (block < STEPS))
-    def _():
-        outgoing[...] = exchange.finish(block)
+    @pl.when((block >= 0) & (block < STEPS) & (lax.rem(block, 2) == 0))
+    def _():
+        both_groups = exchange.finish(block // 2)
+        outgoing[0] = both_groups[:, :BLK]
+        outgoing[1] = both_groups[:, BLK:]
 
     @pl.when(block >= 0)
     def _():
-        back_steps(block, (*given[:13], outgoing), scratch, write, write_halo, write_taps, write_heads)
+        back_steps(block, (*given[:13], outgoing.at[lax.rem(block, 2)]), scratch, write, write_halo, write_taps, write_heads)
 
     @pl.when(step < CHUNKS)
     def _():
@@ -1447,7 +1486,7 @@
         scratch_shapes=[
             *back_scratch(length),
             *exchange_scratch(),
-            pltpu.VMEM((STATE, BLK), BF16),
+            pltpu.VMEM((2, STATE, BLK), BF16),
             pltpu.VMEM((STEPS + 2, length, BLK), BF16),
             pltpu.VMEM((STEPS + 1, PAD, BLK), F32),
             pltpu.VMEM((STEPS + 1, PAD, BLK), F32),
@@ -1535,13 +1574,12 @@
     length = units_low.shape[0]
     here = (shards, parts) == (4, PARTS)
     small = pack_small(conv_taps, conv_bias, dt_bias, decay_log, skip_scale, mixer_gain, input_gain)
-    seg_row = jnp.broadcast_to(seg_ids[None], (8, length))
+    seg_row = segment_ids
     if here:
-        seg_own = jnp.broadcast_to(seg_ids[:, None], (length, 128))
         (
             xs, y_local, incoming, b_rows, c_rows, dt, running, entering,
             kept, w_turned, out_whole, projected, normed_t, halo, taps, heads, gain, g_float, seg_lanes,
-        ) = forward(in_matrix, out_matrix, units_low, small, seg_own, seg_row)
+        ) = forward(in_matrix, out_matrix, units_low, small, seg_row)
         out_whole = out_whole.reshape(-1, D)
     else:
         units = units_low.astype(F32)

time: 404 us -> 385 us (0.953)
  Pallas kernels: 375 us -> 360 us
  local copies, waits for them, and re-layouts: 14.3 us -> 9.76 us
    pallas_call x1, Pallas kernels: 120 us -> 102 us  [forward(): pl.pallas_call(forward_kernel, grid=(SLOTS,), in_specs=[anywhere, anywher...]
where the time goes in v7:
time: 385 us; the launch traced here: 384 us
  Pallas kernels  360 us (94%)
  other arithmetic  13.3 us (3%)
  local copies, waits for them, and re-layouts  9.76 us (3%)
    pallas_call x1, Pallas kernels, finish(): pl.pallas_call(finish_kernel, grid=(CHUNKS + LAGS - 1,), in_specs=[*back_...  217 us
    pallas_call x1, Pallas kernels, forward(): pl.pallas_call(forward_kernel, grid=(SLOTS,), in_specs=[anywhere, anywher...  102 us
    pallas_call x1, Pallas kernels, tail(): pl.pallas_call(tail_kernel, grid=(2 * STEPS,), in_specs=[early(length), e...  41 us
    convert_element_type x2, other arithmetic, on_device(): d_in, d_out = (d_in.T.astype(F32), d_out.astype(F32))  9.92 us

profile of v7, /device:TPU:0, one launch (start us, length us, event | category | flops | bytes accessed | tf_op | source)
XLA Modules:
  0.0 384.1 jit_solution(8834346430767173545)
XLA Ops:
  0.6 0.7 pad.18
  1.3 0.7 pad.19
  2.0 0.8 fusion.4
  2.8 0.7 broadcast_in_dim.18
  3.5 0.7 concatenate.7
  4.2 0.6 pad_convert_fusion.refs_3_
  4.8 102.0 %forward.1 = (bf16[512,3072]{1,0:T(8,128)(2,1)}, bf16[512,3072]{1,0:T(8,128)(2,1)}, bf16[128,3072]{1,0:T(8,128)(2,1)}, bf16[512,128]{1,0:T(8,128)(2,1)}, bf16[51...) custom-call(bf16[6448,384]{1,0:T(8,128)(2,1)} %bitcast.21, ...), custom_call_target="tpu_custom_call" | custom-call | tf_op jit(solution)/shard_map/forward/pallas_call | solution.py:717
  106.8 41.0 %tail.1 = (bf16[3072,512]{1,0:T(8,128)(2,1)}, bf16[512,6656]{1,0:T(8,128)(2,1)}, bf16[512,3072]{1,0:T(8,128)(2,1)}, bf16[128,3072]{1,0:T(8,128)(2,1)}, f32[8,307...) custom-call(bf16[512,3072]{1,0:T(8,128)(2,1)} %get-tuple-element.42.y_ref, ...), custom_call_target="tpu_custom_call" | custom-call | flops 12000000000 | bytes 50000000 | tf_op jit(solution)/shard_map/tail/pallas_call | solution.py:886
  147.8 217.4 %finish.1 = (bf16[6448,384]{1,0:T(8,128)(2,1)}, bf16[768,1536]{1,0:T(8,128)(2,1)}, bf16[512,1536]{1,0:T(8,128)(2,1)}, f32[8,3328]{1,0:T(8,128)}) custom-call(bf16[512,6656]{1,0:T(8,128)(2,1)} %get-tuple-element.44.gate_ref.refs_0_.refs_1_, bf16[512,6656]{1,0:T(8,128)(2,1)} %get-tuple-element.44.gate_ref.refs_0_.refs_1_, ...), custom_call_target="tpu_custom_call" | custom-call | tf_op jit(solution)/shard_map/finish/pallas_call | solution.py:1458
  365.2 1.2 fusion.8
  366.4 1.9 fusion.7
  368.3 0.7 fusion.10
  369.0 0.6 fusion.5
  369.6 0.0 copy-start
  369.6 7.1 %convert_bitcast_fusion = f32[384,6448]{0,1:T(8,128)} fusion(bf16[6448,384]{1,0:T(8,128)(2,1)} %get-tuple-element.69), kind=kLoop, calls=%fused_computation | loop fusion | flops 2476032 | bytes 14856192 | tf_op jit(solution)/shard_map/convert_element_type | solution.py:1624
  376.7 0.0 copy-done
  376.7 0.0 copy-start.2
  376.7 0.0 copy-start.1
  376.7 2.8 convert_element_type.20
  379.5 0.0 copy-done.2
  379.5 0.7 dynamic-slice_bitcast_fusion
  380.3 0.1 reshape_squeeze.3
  380.3 0.1 reduce_sum.9
  380.4 0.6 dynamic_slice.38
  381.0 0.6 dynamic-slice_reduce_fusion.1
  381.7 0.7 dynamic-slice_reduce_fusion
  382.4 0.6 dynamic-slice_reduce_fusion.2
  383.0 0.0 copy-done.1
  383.0 1.1 copy.25
  (7 shorter events, 0.1 us)
Async XLA Ops:
  369.6 7.1 %copy-start = (bf16[768,1536]{1,0:T(8,128)(2,1)S(1)}, bf16[768,1536]{1,0:T(8,128)(2,1)}, u32[]{:S(2)}) copy-start(bf16[768,1536]{1,0:T(8,128)(2,1)} %get-tuple-element.70) | copy-start | bytes 7077892
  376.7 2.8 copy-start.2
  376.7 6.3 %copy-start.1 = (bf16[512,1536]{1,0:T(8,128)(2,1)S(1)}, bf16[512,1536]{1,0:T(8,128)(2,1)}, u32[]{:S(2)}) copy-start(bf16[512,1536]{1,0:T(8,128)(2,1)} %get-tuple-element.68) | copy-start | bytes 4718596

commit v8 on v7

--- a/solution.py
+++ b/solution.py
@@ -53,7 +53,7 @@
 
 
 def sigmoid(v):
-    return 1.0 / (1.0 + jnp.exp(-v))
+    return 0.5 + 0.5 * jnp.tanh(0.5 * v)
 
 
 def in_two(a):
@@ -462,7 +462,9 @@
 
 
 def forward_kernel(*refs):
-    main_ref, shard_ref, units_ref, small_ref, row_ref = refs[:5]
+    main_ref, shard_ref, units_ref, row_ref = refs[:4]
+    conv_ref, bias_ref, mixer_ref, input_ref, *head_refs = refs[4:11]
+    refs = refs[6:]
     xs_ref, y_ref, state_ref, b_ref, c_ref, dt_ref, run_ref, in_ref = refs[5:13]
     keep_ref, weight_ref, whole_ref, projected_ref, normed_t_ref = refs[13:18]
     halo_ref, taps_ref, heads_ref, gain_ref, input_gain_ref, seg_ref = refs[18:24]
@@ -527,8 +529,13 @@
                 gather.load(k, main_ref.at[chunk * WIDE : (chunk + 1) * WIDE, :]).start()
         for k in range(OUT_PIECES):
             gather_out.load(k, shard_ref.at[:, k * OUT_WIDE : (k + 1) * OUT_WIDE]).start()
-        own_small[...] = small_ref[...]
-        smalls[shard] = small_ref[...]
+        own_small[...] = jnp.zeros((8, SMALL_WIDTH), F32)
+        own_small[0:4, : XBC // 4] = conv_ref[...].astype(F32)
+        for row, ref in ((4, bias_ref), (5, mixer_ref), (6, input_ref)):
+            own_small[row : row + 1, : ref.shape[0]] = ref[...].astype(F32).reshape(1, ref.shape[0])
+        for kind, ref in enumerate(head_refs):
+            own_small[7:8, kind * 128 : kind * 128 + HEADS // 4] = ref[...].astype(F32).reshape(1, HEADS // 4)
+        smalls[shard] = own_small[...]
         columns = pl.ds(pl.multiple_of(shard * SHARD, SHARD), SHARD)
         gathered[0, rest:, columns] = jnp.zeros((WIDE - rest, SHARD), BF16)
         for k in range(length // 128):
@@ -571,11 +578,10 @@
             padded = jnp.concatenate([smalls[s], jnp.zeros((8, XBC - SMALL_WIDTH), F32)], axis=1)
             padded = jnp.where(iota((8, XBC), 1) < XBC // 4, padded, 0.0)
             whole = whole + (pltpu.roll(padded, s * (XBC // 4), 1) if s else padded)
-            line = jnp.broadcast_to(smalls[s, 7:8, :128], (8, 128))
             inside = (lane >= s * own) & (lane < (s + 1) * own)
             for kind in range(3):
-                shift = (s - kind) * own % 128
-                moved = pltpu.roll(line, shift, 1) if shift else line
+                moved = jnp.broadcast_to(smalls[s, 7:8, kind * 128 : (kind + 1) * 128], (8, 128))
+                moved = pltpu.roll(moved, s * own, 1) if s else moved
                 heads = jnp.where(inside & (row == kind), moved, heads)
         taps_ref[...] = whole
         heads_ref[...] = heads
@@ -704,7 +710,7 @@
             normed_t_ref[s] = normed[:, columns].astype(F32).T.astype(BF16)
 
 
-def forward(in_matrix, out_matrix, units, small, seg_row):
+def forward(in_matrix, out_matrix, units, seg_row, *small):
     length = units.shape[0]
     chunks = len(ORDER)
     whole = lambda *shape: pl.BlockSpec(shape, lambda t: (0,) * len(shape))
@@ -721,8 +727,8 @@
             anywhere,
             anywhere,
             once(length, D),
-            once(8, SMALL_WIDTH),
             once(1, length),
+            *[once(*each.shape) for each in small],
         ],
         out_specs=[
             *out_specs,
@@ -781,7 +787,7 @@
         ],
         compiler_params=communicating(1),
         name="forward",
-    )(in_matrix.T, out_matrix, units, small, seg_row)
+    )(in_matrix.T, out_matrix, units, seg_row, *small)
 
 
 def tail_kernel(
@@ -791,46 +797,44 @@
 ):
     step = pl.program_id(0)
     length = y_ref.shape[0]
-    group = jnp.where(step < STEPS, step, jnp.minimum(step - STEPS, STEPS - 1))
-    select = chosen(group)
+    unit = lax.rem(step, UNITS)
     half = length // 2
+
     @pl.when(step == 0)
     def _():
         squares[...] = jnp.zeros_like(squares)
         products[...] = jnp.zeros_like(products)
+        mixed[...] = jnp.zeros_like(mixed)
         for k in range(length // Q):
             rows = slice(k * Q, (k + 1) * Q)
             c_t[:, rows] = c_ref[rows, :].astype(F32).T.astype(BF16)
 
-    @pl.when(step < STEPS)
-    def _():
-        incoming = incoming_ref[...]
+    def earlier(one):
+        columns = slice(one * BLK, (one + 1) * BLK)
+        group = 2 * unit + one
+        select = chosen(group)
+        incoming = incoming_ref[:, columns]
         skip = widen(heads_ref[...], select)[2:3, :]
         for k in range(2):
             rows = slice(k * half, (k + 1) * half)
-            y = y_ref[rows, :].astype(F32)
+            y = y_ref[rows, columns].astype(F32)
             y = y + widen(in_ref[rows, :], select) * dot(c_ref[rows, :], incoming)
-            y = y + skip * xs_ref[rows, :].astype(F32)
-            full[step, rows, :] = y
-            gate = gate_ref[rows, :].astype(F32)
+            y = y + skip * xs_ref[rows, columns].astype(F32)
+            full[group, rows, :] = y
+            gate = gate_ref[rows, columns].astype(F32)
             gated = y * gate * sigmoid(gate)
-            d_mixer = dot_nt(g_ref[rows, :], out_ref[...])
-            dmix[step, rows, :] = d_mixer
+            d_mixer = dot_nt(g_ref[rows, :], out_ref[columns, :])
+            dmix[group, rows, :] = d_mixer
             square = gated * gated
-            product = gated * d_mixer * gain_ref[0:1, :]
+            product = gated * d_mixer * gain_ref[0:1, columns]
             squares[rows, :] += square[:, :128] + square[:, 128:]
             products[rows, :] += product[:, :128] + product[:, 128:]
 
-    @pl.when(step == STEPS)
-    def _():
-        norm = lax.rsqrt(jnp.sum(squares[...], axis=1, keepdims=True) * (1.0 / INNER) + epsilon)
-        mean = norm * jnp.sum(products[...], axis=1, keepdims=True) * (1.0 / INNER)
-        squares[...] = jnp.broadcast_to(norm, squares.shape)
-        products[...] = jnp.broadcast_to(mean, products.shape)
-
-    @pl.when((step >= STEPS) & (step < 2 * STEPS))
-    def _():
-        gain = gain_ref[0:1, :]
+    def later(one):
+        columns = slice(one * BLK, (one + 1) * BLK)
+        group = 2 * unit + one
+        select = chosen(group)
+        gain = gain_ref[0:1, columns]
         d_gain = jnp.zeros((1, BLK), F32)
         d_skip = jnp.zeros((1, BLK), F32)
         d_state = jnp.zeros((STATE, BLK), F32)
@@ -839,34 +843,42 @@
             norm, mean = both(squares[rows, :]), both(products[rows, :])
             y = full[group, rows, :]
             d_mixer = dmix[group, rows, :]
-            gate = gate_ref[rows, :].astype(F32)
+            gate = gate_ref[rows, columns].astype(F32)
             sig = sigmoid(gate)
             silu = gate * sig
-            unit = y * silu * norm
-            low = (unit * gain).astype(BF16)
-            mixer_ref[:, rows] = (unit * gain).T.astype(BF16)
-            part = dot(low, out_ref[...])
-
-            @pl.when(step == STEPS)
-            def _():
-                mixed[rows, :] = part
-
-            @pl.when(step > STEPS)
-            def _():
-                mixed[rows, :] += part
-
-            d_gain = d_gain + jnp.sum(d_mixer * unit, axis=0, keepdims=True)
-            d_gated = norm * (d_mixer * gain - unit * mean)
-            dproj_ref[rows, :] = (d_gated * y * (sig * (1.0 + gate * (1.0 - sig)))).astype(BF16)
+            unscaled = y * silu * norm
+            value = unscaled * gain
+            mixer_ref[columns, rows] = value.T.astype(BF16)
+            mixed[rows, :] += dot(value.astype(BF16), out_ref[columns, :])
+            d_gain = d_gain + jnp.sum(d_mixer * unscaled, axis=0, keepdims=True)
+            d_gated = norm * (d_mixer * gain - unscaled * mean)
+            dproj_ref[rows, columns] = (d_gated * y * (sig * (1.0 + gate * (1.0 - sig)))).astype(BF16)
             dy = (d_gated * silu).astype(BF16)
-            dy_ref[rows, :] = dy
+            dy_ref[rows, columns] = dy
             dy = dy.astype(F32)
-            d_skip = d_skip + jnp.sum(dy * xs_ref[rows, :].astype(F32), axis=0, keepdims=True)
+            d_skip = d_skip + jnp.sum(dy * xs_ref[rows, columns].astype(F32), axis=0, keepdims=True)
             d_state = d_state + dot(c_t[:, rows], (dy * widen(in_ref[rows, :], select)).astype(BF16))
-        dsin_ref[...] = d_state.astype(BF16)
-        sums_ref[...] = jnp.concatenate([d_gain, d_skip, jnp.zeros((6, BLK), F32)], axis=0)
-
-    @pl.when(step == 2 * STEPS - 1)
+        dsin_ref[:, columns] = d_state.astype(BF16)
+        sums_ref[:, columns] = jnp.concatenate([d_gain, d_skip, jnp.zeros((6, BLK), F32)], axis=0)
+
+    @pl.when(step < UNITS)
+    def _():
+        earlier(0)
+        earlier(1)
+
+    @pl.when(step == UNITS)
+    def _():
+        norm = lax.rsqrt(jnp.sum(squares[...], axis=1, keepdims=True) * (1.0 / INNER) + epsilon)
+        mean = norm * jnp.sum(products[...], axis=1, keepdims=True) * (1.0 / INNER)
+        squares[...] = jnp.broadcast_to(norm, squares.shape)
+        products[...] = jnp.broadcast_to(mean, products.shape)
+
+    @pl.when(step >= UNITS)
+    def _():
+        later(0)
+        later(1)
+
+    @pl.when(step == 2 * UNITS - 1)
     def _():
         total = units_ref[...].astype(F32) + mixed[...]
         block_ref[...] = total.astype(BF16)
@@ -877,21 +889,21 @@
 
 def tail(y, xs, projected, incoming, out_whole, c_rows, entering, heads, gain, cot, units):
     length = y.shape[0]
-    group = lambda i: jnp.where(i < STEPS, i, jnp.minimum(i - STEPS, STEPS - 1))
-    second = lambda i: jnp.clip(i - STEPS, 0, STEPS - 1)
-    early = lambda rows: pl.BlockSpec((rows, BLK), lambda i: (0, jnp.minimum(i, STEPS - 1)))
-    late = lambda rows: pl.BlockSpec((rows, BLK), lambda i: (0, second(i)))
-    each = lambda rows: pl.BlockSpec((rows, BLK), lambda i: (0, group(i)))
+    unit = lambda i: lax.rem(i, UNITS)
+    second = lambda i: jnp.maximum(i - UNITS, 0)
+    early = lambda rows: pl.BlockSpec((rows, UNIT), lambda i: (0, jnp.minimum(i, UNITS - 1)))
+    late = lambda rows: pl.BlockSpec((rows, UNIT), lambda i: (0, second(i)))
+    each = lambda rows: pl.BlockSpec((rows, UNIT), lambda i: (0, unit(i)))
     whole = lambda *shape: pl.BlockSpec(shape, lambda i: (0,) * len(shape))
     return pl.pallas_call(
         tail_kernel,
-        grid=(2 * STEPS,),
+        grid=(2 * UNITS,),
         in_specs=[
             early(length),
             each(length),
             each(length),
             early(STATE),
-            pl.BlockSpec((BLK, D), lambda i: (group(i), 0)),
+            pl.BlockSpec((UNIT, D), lambda i: (unit(i), 0)),
             whole(length, 128),
             whole(length, 128),
             whole(8, 128),
@@ -900,10 +912,10 @@
             whole(length, D),
         ],
         out_specs=[
-            pl.BlockSpec((BLK, length), lambda i: (second(i), 0)),
+            pl.BlockSpec((UNIT, length), lambda i: (second(i), 0)),
             late(length),
             late(length),
-            pl.BlockSpec((STATE, BLK), lambda i: (0, second(i))),
+            pl.BlockSpec((STATE, UNIT), lambda i: (0, second(i))),
             late(8),
             whole(length, D),
             whole(8, D),
@@ -1515,6 +1527,85 @@
     )(*given, normed_t, mixer_t, dproj, w_turned, cot, units, input_gain, column_sums, stats, kept)
 
 
+def settle_kernel(din_ref, dout_ref, total_ref, *outs, entries):
+    (
+        din_out, dout_out, taps_out, bias_out, step_bias_out, decay_out, skip_out, gain_out, input_gain_out, rms_out,
+    ) = outs
+    din_out[...] = din_ref[...].astype(F32)
+    dout_out[...] = dout_ref[...].astype(F32)
+
+    @pl.when(pl.program_id(0) == 0)
+    def _():
+        shard = lax.axis_index("fsdp")
+        own = HEADS // 4
+        width = XBC // 4
+
+        def mine(pieces):
+            result = pieces[0]
+            for s in range(1, 4):
+                result = jnp.where(shard == s, pieces[s], result)
+            return result
+
+        def flat(ref, row):
+            ref[...] = row.reshape(ref.shape)
+
+        total = total_ref[...]
+        columns = mine([pltpu.roll(total, (XBC - s * width) % XBC, 1) if s else total for s in range(4)])
+        taps_out[...] = columns[:4, :width]
+        flat(bias_out, columns[4:5, :width])
+
+        def heads(row):
+            rows = jnp.broadcast_to(row, (8, 128))
+            rows = mine([pltpu.roll(rows, (128 - s * own) % 128, 1) if s else rows for s in range(4)])
+            return rows[:1, :own]
+
+        flat(step_bias_out, heads(total[7:8, D : D + 128]))
+        flat(decay_out, heads(total[7:8, D + 128 : D + 256]))
+        skip = jnp.zeros((8, 128), F32)
+        for group in range(STEPS):
+            high, low = in_two(jnp.broadcast_to(total[6:7, group * BLK : (group + 1) * BLK], (8, BLK)))
+            skip = skip + dot(high, chosen_back(group)) + dot(low, chosen_back(group))
+        flat(skip_out, heads(skip[:1]))
+        flat(gain_out, mine([total[5:6, s * (INNER // 4) : (s + 1) * (INNER // 4)] for s in range(4)]))
+        flat(input_gain_out, mine([total[7:8, s * SHARD : (s + 1) * SHARD] for s in range(4)]))
+        squares = jnp.concatenate([total[7:8, D + 256 : D + 257], total[7:8, D + 384 : D + 385]], axis=1)
+        flat(rms_out, jnp.sqrt(squares * (1.0 / entries)))
+
+
+def settle(d_in, d_out, total, entries):
+    steps = 6
+    shapes = [
+        (4, XBC // 4),
+        (XBC // 4,),
+        (HEADS // 4,),
+        (HEADS // 4,),
+        (HEADS // 4,),
+        (INNER // 4,),
+        (SHARD,),
+        (2,),
+    ]
+    rows = -(-PROJ // steps // 16) * 16
+    whole = lambda shape: pl.BlockSpec(shape, lambda i: (0,) * len(shape))
+    blocks = [
+        pl.BlockSpec((rows, SHARD), lambda i: (i, 0)),
+        pl.BlockSpec((2 * SHARD // steps, D), lambda i: (i, 0)),
+    ]
+    d_in, d_out, taps, *rest = pl.pallas_call(
+        functools.partial(settle_kernel, entries=entries),
+        grid=(steps,),
+        in_specs=[*blocks, whole((8, XBC))],
+        out_specs=[*blocks, *[whole(shape) for shape in shapes]],
+        out_shape=[
+            jax.ShapeDtypeStruct((PROJ, SHARD), F32),
+            jax.ShapeDtypeStruct((2 * SHARD, D), F32),
+            *[jax.ShapeDtypeStruct(shape, F32) for shape in shapes],
+        ],
+        compiler_params=pltpu.CompilerParams(vmem_limit_bytes=VMEM_LIMIT),
+        name="settle",
+    )(d_in, d_out, total)
+    return (d_in.T, d_out, taps.T, *[each.reshape(-1) for each in rest])
+
+
 def passed_along(block, axis, distance):
     devices = range(lax.axis_size(axis))
     route = [(i - distance, i) for i in devices if i - distance in devices]
@@ -1573,13 +1664,15 @@
     seg_ids = segment_ids[0]
     length = units_low.shape[0]
     here = (shards, parts) == (4, PARTS)
-    small = pack_small(conv_taps, conv_bias, dt_bias, decay_log, skip_scale, mixer_gain, input_gain)
     seg_row = segment_ids
     if here:
         (
             xs, y_local, incoming, b_rows, c_rows, dt, running, entering,
             kept, w_turned, out_whole, projected, normed_t, halo, taps, heads, gain, g_float, seg_lanes,
-        ) = forward(in_matrix, out_matrix, units_low, small, seg_row)
+        ) = forward(
+            in_matrix, out_matrix, units_low, seg_row,
+            conv_taps.T, conv_bias, mixer_gain, input_gain, dt_bias, decay_log, skip_scale,
+        )
         out_whole = out_whole.reshape(-1, D)
     else:
         units = units_low.astype(F32)
@@ -1589,6 +1682,7 @@
         w_whole = lax.all_gather(w_whole, "fsdp", axis=0, tiled=True)
         out_whole = lax.all_gather(out_matrix, "fsdp", axis=0, tiled=True)
         rim_seg = passed_along(seg_ids[length - CONV + 1 :], "ctx", 1)
+        small = pack_small(conv_taps, conv_bias, dt_bias, decay_log, skip_scale, mixer_gain, input_gain)
         taps, gain, g_float, heads = unpack_small(lax.all_gather(small, "fsdp"), conv_bias.shape[0])
         normed = (base_rows * g_float).astype(BF16)
         normed_t = normed.T
@@ -1621,7 +1715,8 @@
         d_in, d_out, input_grad, total = finish(
             given, normed_t, mixer_t.reshape(4, 2, SHARD, length), dproj, w_turned, cot, units_low, g_float, column_sums, stats, kept
         )
-        d_in, d_out = d_in.T.astype(F32), d_out.astype(F32)
+        sums = settle(d_in, d_out, total, length * shards * parts * D)
+        return (block_out[None], input_grad[None], *sums)
     else:
         dproj, d_halo, d_taps, d_heads = back(given, dproj)
         returned = passed_along(d_halo.astype(BF16), "ctx", -1)

time: 385 us -> 361 us (0.938)
  other arithmetic: 13.3 us -> 0 us
  local copies, waits for them, and re-layouts: 9.76 us -> 1.15 us
    convert_element_type x2 -> x0, other arithmetic: 9.92 us -> none  [on_device(): d_in, d_out = (d_in.T.astype(F32), d_out.astype(F32))]
    pallas_call x1 -> x2, Pallas kernels: 41 us -> 39.6 us  [the longest x1 30 us: tail(): pl.pallas_call(tail_kernel, grid=(2 * UNITS,), in_specs=[early(length), e...]
where the time goes in v8:
time: 361 us
  Pallas kernels  359 us (99%)
    pallas_call x1, Pallas kernels, finish(): pl.pallas_call(finish_kernel, grid=(CHUNKS + LAGS - 1,), in_specs=[*back_...  217 us
    pallas_call x1, Pallas kernels, forward(): pl.pallas_call(forward_kernel, grid=(SLOTS,), in_specs=[anywhere, anywher...  102 us
    pallas_call x1, Pallas kernels, tail(): pl.pallas_call(tail_kernel, grid=(2 * UNITS,), in_specs=[early(length), e...  30 us
    pallas_call x1, Pallas kernels, settle(): pl.pallas_call(functools.partial(settle_kernel, entries=entries), grid=(s...  9.57 us

profile of v8, /device:TPU:0, one launch (start us, length us, event | category | flops | bytes accessed | tf_op | source)
XLA Modules:
  0.0 360.7 jit_solution(10960707044525801454)
XLA Ops:
  0.6 101.9 %forward.1 = (bf16[512,3072]{1,0:T(8,128)(2,1)}, bf16[512,3072]{1,0:T(8,128)(2,1)}, bf16[128,3072]{1,0:T(8,128)(2,1)}, bf16[512,128]{1,0:T(8,128)(2,1)}, bf16[51...) custom-call(bf16[6448,384]{1,0:T(8,128)(2,1)} %bitcast.13, ...), custom_call_target="tpu_custom_call" | custom-call | tf_op jit(solution)/shard_map/forward/pallas_call | solution.py:723
  102.6 30.0 %tail.1 = (bf16[3072,512]{1,0:T(8,128)(2,1)}, bf16[512,6656]{1,0:T(8,128)(2,1)}, bf16[512,3072]{1,0:T(8,128)(2,1)}, bf16[128,3072]{1,0:T(8,128)(2,1)}, f32[8,307...) custom-call(bf16[512,3072]{1,0:T(8,128)(2,1)} %get-tuple-element.52.y_ref, ...), custom_call_target="tpu_custom_call" | custom-call | flops 12000000000 | bytes 50000000 | tf_op jit(solution)/shard_map/tail/pallas_call | solution.py:898
  132.5 217.4 %finish.1 = (bf16[6448,384]{1,0:T(8,128)(2,1)}, bf16[768,1536]{1,0:T(8,128)(2,1)}, bf16[512,1536]{1,0:T(8,128)(2,1)}, f32[8,3328]{1,0:T(8,128)}) custom-call(bf16[512,6656]{1,0:T(8,128)(2,1)} %get-tuple-element.54.gate_ref.refs_0_.refs_1_, bf16[512,6656]{1,0:T(8,128)(2,1)} %get-tuple-element.54.gate_ref.refs_0_.refs_1_, ...), custom_call_target="tpu_custom_call" | custom-call | tf_op jit(solution)/shard_map/finish/pallas_call | solution.py:1470
  349.9 0.0 copy-start
  349.9 9.6 %settle.1 = (f32[6448,384]{1,0:T(8,128)}, f32[768,1536]{1,0:T(8,128)}, f32[4,832]{1,0:T(4,128)}, f32[832]{0:T(1024)}, f32[12]{0:T(128)}, /*index=5*/f32[12]{0:T(...) custom-call(bf16[6448,384]{1,0:T(8,128)(2,1)} %get-tuple-element.79.din_ref, ...), custom_call_target="tpu_custom_call" | custom-call | tf_op jit(solution)/shard_map/settle/pallas_call | solution.py:1593
  359.5 0.0 copy-done
  359.5 1.1 copy.25
Async XLA Ops:
  349.9 9.6 %copy-start = (bf16[512,1536]{1,0:T(8,128)(2,1)S(1)}, bf16[512,1536]{1,0:T(8,128)(2,1)}, u32[]{:S(2)}) copy-start(bf16[512,1536]{1,0:T(8,128)(2,1)} %get-tuple-element.78) | copy-start | bytes 4718596

commit v9 on v8

--- a/solution.py
+++ b/solution.py
@@ -523,6 +523,10 @@
 
     @pl.when(step == 0)
     def _():
+        barrier = pltpu.get_barrier_semaphore()
+        greeted = [*[{"ctx": other} for other in exchange.others()], *others]
+        for peer in greeted:
+            pl.semaphore_signal(barrier, inc=1, device_id=peer, device_id_type=pl.DeviceIdType.MESH)
         load_rest().start()
         for k, chunk in enumerate(ORDER):
             if k:
@@ -542,7 +546,7 @@
             ids = jnp.broadcast_to(row_ref[0:1, k * 128 : (k + 1) * 128].astype(F32), (128, 128))
             seg_ref[PAD + k * 128 : PAD + (k + 1) * 128, :] = ids.T.astype(jnp.int32)
         seg_tail[...] = seg_ref[length : length + PAD, :]
-        exchange.greet(*others)
+        pl.semaphore_wait(barrier, len(greeted))
         for hop in range(3):
             small_copy(hop).start()
         seg_copy().start()
@@ -630,6 +634,13 @@
     pl.when(step == 1)(normalise)
     pl.when(step == 2)(take_taps)
 
+    for s in range(4):
+
+        @pl.when(step == 2 + s // 2)
+        def _():
+            columns = slice(s * SHARD, (s + 1) * SHARD)
+            normed_t_ref[s] = normed[:, columns].astype(F32).T.astype(BF16)
+
     @stage(MULTIPLY)
     def _(k):
         low = dot_nt(normed[...], gathered[k]).astype(BF16)
@@ -705,9 +716,6 @@
         for k in range(OUT_PIECES):
             gather_out.drain(k)
             store_out(k).wait()
-        for s in range(4):
-            columns = slice(s * SHARD, (s + 1) * SHARD)
-            normed_t_ref[s] = normed[:, columns].astype(F32).T.astype(BF16)
 
 
 def forward(in_matrix, out_matrix, units, seg_row, *small):
@@ -790,6 +798,10 @@
     )(in_matrix.T, out_matrix, units, seg_row, *small)
 
 
+TAIL_GROUPS = 4
+TAIL_STEPS = STEPS // TAIL_GROUPS
+
+
 def tail_kernel(
     y_ref, xs_ref, gate_ref, incoming_ref, out_ref, c_ref, in_ref, heads_ref, gain_ref, g_ref, units_ref,
     mixer_ref, dproj_ref, dy_ref, dsin_ref, sums_ref, block_ref, stats_ref,
@@ -797,7 +809,7 @@
 ):
     step = pl.program_id(0)
     length = y_ref.shape[0]
-    unit = lax.rem(step, UNITS)
+    unit = lax.rem(step, TAIL_STEPS)
     half = length // 2
 
     @pl.when(step == 0)
@@ -811,7 +823,7 @@
 
     def earlier(one):
         columns = slice(one * BLK, (one + 1) * BLK)
-        group = 2 * unit + one
+        group = TAIL_GROUPS * unit + one
         select = chosen(group)
         incoming = incoming_ref[:, columns]
         skip = widen(heads_ref[...], select)[2:3, :]
@@ -832,7 +844,7 @@
 
     def later(one):
         columns = slice(one * BLK, (one + 1) * BLK)
-        group = 2 * unit + one
+        group = TAIL_GROUPS * unit + one
         select = chosen(group)
         gain = gain_ref[0:1, columns]
         d_gain = jnp.zeros((1, BLK), F32)
@@ -861,24 +873,24 @@
         dsin_ref[:, columns] = d_state.astype(BF16)
         sums_ref[:, columns] = jnp.concatenate([d_gain, d_skip, jnp.zeros((6, BLK), F32)], axis=0)
 
-    @pl.when(step < UNITS)
-    def _():
-        earlier(0)
-        earlier(1)
-
-    @pl.when(step == UNITS)
+    @pl.when(step < TAIL_STEPS)
+    def _():
+        for one in range(TAIL_GROUPS):
+            earlier(one)
+
+    @pl.when(step == TAIL_STEPS)
     def _():
         norm = lax.rsqrt(jnp.sum(squares[...], axis=1, keepdims=True) * (1.0 / INNER) + epsilon)
         mean = norm * jnp.sum(products[...], axis=1, keepdims=True) * (1.0 / INNER)
         squares[...] = jnp.broadcast_to(norm, squares.shape)
         products[...] = jnp.broadcast_to(mean, products.shape)
 
-    @pl.when(step >= UNITS)
-    def _():
-        later(0)
-        later(1)
-
-    @pl.when(step == 2 * UNITS - 1)
+    @pl.when(step >= TAIL_STEPS)
+    def _():
+        for one in range(TAIL_GROUPS):
+            later(one)
+
+    @pl.when(step == 2 * TAIL_STEPS - 1)
     def _():
         total = units_ref[...].astype(F32) + mixed[...]
         block_ref[...] = total.astype(BF16)
@@ -889,21 +901,21 @@
 
 def tail(y, xs, projected, incoming, out_whole, c_rows, entering, heads, gain, cot, units):
     length = y.shape[0]
-    unit = lambda i: lax.rem(i, UNITS)
-    second = lambda i: jnp.maximum(i - UNITS, 0)
-    early = lambda rows: pl.BlockSpec((rows, UNIT), lambda i: (0, jnp.minimum(i, UNITS - 1)))
-    late = lambda rows: pl.BlockSpec((rows, UNIT), lambda i: (0, second(i)))
-    each = lambda rows: pl.BlockSpec((rows, UNIT), lambda i: (0, unit(i)))
+    unit = lambda i: lax.rem(i, TAIL_STEPS)
+    second = lambda i: jnp.maximum(i - TAIL_STEPS, 0)
+    early = lambda rows: pl.BlockSpec((rows, TAIL_GROUPS * BLK), lambda i: (0, jnp.minimum(i, TAIL_STEPS - 1)))
+    late = lambda rows: pl.BlockSpec((rows, TAIL_GROUPS * BLK), lambda i: (0, second(i)))
+    each = lambda rows: pl.BlockSpec((rows, TAIL_GROUPS * BLK), lambda i: (0, unit(i)))
     whole = lambda *shape: pl.BlockSpec(shape, lambda i: (0,) * len(shape))
     return pl.pallas_call(
         tail_kernel,
-        grid=(2 * UNITS,),
+        grid=(2 * TAIL_STEPS,),
         in_specs=[
             early(length),
             each(length),
             each(length),
             early(STATE),
-            pl.BlockSpec((UNIT, D), lambda i: (unit(i), 0)),
+            pl.BlockSpec((TAIL_GROUPS * BLK, D), lambda i: (unit(i), 0)),
             whole(length, 128),
             whole(length, 128),
             whole(8, 128),
@@ -912,10 +924,10 @@
             whole(length, D),
         ],
         out_specs=[
-            pl.BlockSpec((UNIT, length), lambda i: (second(i), 0)),
+            pl.BlockSpec((TAIL_GROUPS * BLK, length), lambda i: (second(i), 0)),
             late(length),
             late(length),
-            pl.BlockSpec((STATE, UNIT), lambda i: (0, second(i))),
+            pl.BlockSpec((STATE, TAIL_GROUPS * BLK), lambda i: (0, second(i))),
             late(8),
             whole(length, D),
             whole(8, D),
@@ -1201,6 +1213,7 @@
 LAGS = 8
 RING = 8
 LATE = 3
+LAST_WIDE = 384
 
 
 def small_sums(taps, columns, input_gain, heads, stats):
@@ -1244,8 +1257,33 @@
     def ring(k):
         return lax.rem(k, RING)
 
-    def sent(stage, k, source, target, peer):
-        return remote(source, target, send_sems.at[stage, k], recv_sems.at[stage, k], peers[peer])
+    class Sent:
+        def __init__(self, stage, k, source, target, peer):
+            self.given = stage, k, source, target, peer
+
+        def act(self, name):
+            stage, k, source, target, peer = self.given
+            for last in range(2):
+
+                @pl.when((k == CHUNKS - 1) == bool(last))
+                def _():
+                    ends = source, target
+                    if last:
+                        columns = (*[slice(None)] * (len(source.shape) - 1), pl.ds(0, LAST_WIDE))
+                        ends = source.at[columns], target.at[columns]
+                    copy = remote(*ends, send_sems.at[stage, k], recv_sems.at[stage, k], peers[peer])
+                    getattr(copy, name)()
+
+        def start(self):
+            self.act("start")
+
+        def wait_send(self):
+            self.act("wait_send")
+
+        def wait_recv(self):
+            self.act("wait_recv")
+
+    sent = Sent
 
     copies = (
         lambda k: sent(0, k, core_send.at[lax.rem(k, 2)], core_recv.at[ring(k)], 0),
@@ -1573,7 +1611,7 @@
 
 
 def settle(d_in, d_out, total, entries):
-    steps = 6
+    steps = 3
     shapes = [
         (4, XBC // 4),
         (XBC // 4,),

time: 361 us -> 355 us (0.983)
  Pallas kernels: 359 us -> 353 us
where the time goes in v9:
time: 355 us
  Pallas kernels  353 us (99%)
    pallas_call x1, Pallas kernels, finish(): pl.pallas_call(finish_kernel, grid=(CHUNKS + LAGS - 1,), in_specs=[*back_...  215 us
    pallas_call x1, Pallas kernels, forward(): pl.pallas_call(forward_kernel, grid=(SLOTS,), in_specs=[anywhere, anywher...  101 us
    pallas_call x1, Pallas kernels, tail(): pl.pallas_call(tail_kernel, grid=(2 * TAIL_STEPS,), in_specs=[early(lengt...  28.2 us
    pallas_call x1, Pallas kernels, settle(): pl.pallas_call(functools.partial(settle_kernel, entries=entries), grid=(s...  8.36 us

profile of v9, /device:TPU:0, one launch (start us, length us, event | category | flops | bytes accessed | tf_op | source)
XLA Modules:
  0.0 354.6 jit_solution(6593034599552377125)
XLA Ops:
  0.6 101.5 %forward.1 = (bf16[512,3072]{1,0:T(8,128)(2,1)}, bf16[512,3072]{1,0:T(8,128)(2,1)}, bf16[128,3072]{1,0:T(8,128)(2,1)}, bf16[512,128]{1,0:T(8,128)(2,1)}, bf16[51...) custom-call(bf16[6448,384]{1,0:T(8,128)(2,1)} %bitcast.13, ...), custom_call_target="tpu_custom_call" | custom-call | tf_op jit(solution)/shard_map/forward/pallas_call | solution.py:731
  102.1 28.2 %tail.1 = (bf16[3072,512]{1,0:T(8,128)(2,1)}, bf16[512,6656]{1,0:T(8,128)(2,1)}, bf16[512,3072]{1,0:T(8,128)(2,1)}, bf16[128,3072]{1,0:T(8,128)(2,1)}, f32[8,307...) custom-call(bf16[512,3072]{1,0:T(8,128)(2,1)} %get-tuple-element.52.y_ref, ...), custom_call_target="tpu_custom_call" | custom-call | flops 12000000000 | bytes 50000000 | tf_op jit(solution)/shard_map/tail/pallas_call | solution.py:910
  130.3 214.7 %finish.1 = (bf16[6448,384]{1,0:T(8,128)(2,1)}, bf16[768,1536]{1,0:T(8,128)(2,1)}, bf16[512,1536]{1,0:T(8,128)(2,1)}, f32[8,3328]{1,0:T(8,128)}) custom-call(bf16[512,6656]{1,0:T(8,128)(2,1)} %get-tuple-element.54.gate_ref.refs_0_.refs_1_, bf16[512,6656]{1,0:T(8,128)(2,1)} %get-tuple-element.54.gate_ref.refs_0_.refs_1_, ...), custom_call_target="tpu_custom_call" | custom-call | tf_op jit(solution)/shard_map/finish/pallas_call | solution.py:1508
  345.1 0.0 copy-start
  345.1 8.4 %settle.1 = (f32[6448,384]{1,0:T(8,128)}, f32[768,1536]{1,0:T(8,128)}, f32[4,832]{1,0:T(4,128)}, f32[832]{0:T(1024)}, f32[12]{0:T(128)}, /*index=5*/f32[12]{0:T(...) custom-call(bf16[6448,384]{1,0:T(8,128)(2,1)} %get-tuple-element.79.din_ref, ...), custom_call_target="tpu_custom_call" | custom-call | tf_op jit(solution)/shard_map/settle/pallas_call | solution.py:1631
  353.4 0.0 copy-done
  353.4 1.1 copy.25
Async XLA Ops:
  345.1 8.4 %copy-start = (bf16[512,1536]{1,0:T(8,128)(2,1)S(1)}, bf16[512,1536]{1,0:T(8,128)(2,1)}, u32[]{:S(2)}) copy-start(bf16[512,1536]{1,0:T(8,128)(2,1)} %get-tuple-element.78) | copy-start | bytes 4718596

commit v10 on v9

--- a/solution.py
+++ b/solution.py
@@ -798,7 +798,7 @@
     )(in_matrix.T, out_matrix, units, seg_row, *small)
 
 
-TAIL_GROUPS = 4
+TAIL_GROUPS = 6
 TAIL_STEPS = STEPS // TAIL_GROUPS
 
 

time: 355 us -> 355 us (level)
  no operation moved by 1% of the time
where the time goes in v10:
time: 355 us
  Pallas kernels  353 us (99%)
    pallas_call x1, Pallas kernels, finish(): pl.pallas_call(finish_kernel, grid=(CHUNKS + LAGS - 1,), in_specs=[*back_...  215 us
    pallas_call x1, Pallas kernels, forward(): pl.pallas_call(forward_kernel, grid=(SLOTS,), in_specs=[anywhere, anywher...  101 us
    pallas_call x1, Pallas kernels, tail(): pl.pallas_call(tail_kernel, grid=(2 * TAIL_STEPS,), in_specs=[early(lengt...  28.9 us
    pallas_call x1, Pallas kernels, settle(): pl.pallas_call(functools.partial(settle_kernel, entries=entries), grid=(s...  8.36 us

profile of v10, /device:TPU:0, one launch (start us, length us, event | category | flops | bytes accessed | tf_op | source)
XLA Modules:
  0.0 355.3 jit_solution(7480293719929955835)
XLA Ops:
  0.6 101.5 %forward.1 = (bf16[512,3072]{1,0:T(8,128)(2,1)}, bf16[512,3072]{1,0:T(8,128)(2,1)}, bf16[128,3072]{1,0:T(8,128)(2,1)}, bf16[512,128]{1,0:T(8,128)(2,1)}, bf16[51...) custom-call(bf16[6448,384]{1,0:T(8,128)(2,1)} %bitcast.13, ...), custom_call_target="tpu_custom_call" | custom-call | tf_op jit(solution)/shard_map/forward/pallas_call | solution.py:731
  102.1 28.9 %tail.1 = (bf16[3072,512]{1,0:T(8,128)(2,1)}, bf16[512,6656]{1,0:T(8,128)(2,1)}, bf16[512,3072]{1,0:T(8,128)(2,1)}, bf16[128,3072]{1,0:T(8,128)(2,1)}, f32[8,307...) custom-call(bf16[512,3072]{1,0:T(8,128)(2,1)} %get-tuple-element.52.y_ref, ...), custom_call_target="tpu_custom_call" | custom-call | flops 12000000000 | bytes 50000000 | tf_op jit(solution)/shard_map/tail/pallas_call | solution.py:910
  131.0 214.7 %finish.1 = (bf16[6448,384]{1,0:T(8,128)(2,1)}, bf16[768,1536]{1,0:T(8,128)(2,1)}, bf16[512,1536]{1,0:T(8,128)(2,1)}, f32[8,3328]{1,0:T(8,128)}) custom-call(bf16[512,6656]{1,0:T(8,128)(2,1)} %get-tuple-element.54.gate_ref.refs_0_.refs_1_, bf16[512,6656]{1,0:T(8,128)(2,1)} %get-tuple-element.54.gate_ref.refs_0_.refs_1_, ...), custom_call_target="tpu_custom_call" | custom-call | tf_op jit(solution)/shard_map/finish/pallas_call | solution.py:1508
  345.8 0.0 copy-start
  345.8 8.4 %settle.1 = (f32[6448,384]{1,0:T(8,128)}, f32[768,1536]{1,0:T(8,128)}, f32[4,832]{1,0:T(4,128)}, f32[832]{0:T(1024)}, f32[12]{0:T(128)}, /*index=5*/f32[12]{0:T(...) custom-call(bf16[6448,384]{1,0:T(8,128)(2,1)} %get-tuple-element.79.din_ref, ...), custom_call_target="tpu_custom_call" | custom-call | tf_op jit(solution)/shard_map/settle/pallas_call | solution.py:1631
  354.1 0.0 copy-done
  354.1 1.1 copy.25
Async XLA Ops:
  345.8 8.4 %copy-start = (bf16[512,1536]{1,0:T(8,128)(2,1)S(1)}, bf16[512,1536]{1,0:T(8,128)(2,1)}, u32[]{:S(2)}) copy-start(bf16[512,1536]{1,0:T(8,128)(2,1)} %get-tuple-element.78) | copy-start | bytes 4718596
